TPU v7x, 512 devices: a whole 4x8x8 slice. The times are simulated.
512 devices in a mesh: line: 4 (over x), tile: 128 (over z, y, core).
Axes of the slice: x: 4, y: 8, z: 8, core: 2. Of those that a mesh axis runs over, the one named last changes fastest.
Arguments:
- forcing: float32 [10, 64, 128, 512], P(None, None, 'tile', 'line'), may hold values from -1100 to 1100
- block_inverse: float32 [10, 10, 128, 512], P(None, None, 'tile', 'line'), may hold values from -0.8 to 1
- wall_rates: float32 [2, 10, 128, 512], P(None, None, 'tile', 'line'), may hold values from 0 to 1, as said below
- span_couple: float32 [10], replicated, may hold values from 0.1 to 0.4
Outputs:
- basis: float32 [10, 64, 128, 512], P(None, None, 'tile', 'line')
Inputs may be any that keep to these rules, and one draw needn't show every extreme that they name: `wall_rates`: every entry lies strictly between 0 and 1.
All inputs are finite; a program needn't handle non-finite values.
Results may differ from a plain program's by a relative error of at most 0.00022.
Values sent between devices are 32-bit elements; how exact they have to be, the bound alone decides.
No kernel may reach another device: no remote copies, remote signals or barrier semaphores. Data moves between devices by JAX's collectives and lax.ppermute only.
A program may use at most 64 MiB of HBM per device.

v0:
```python
import math

import jax
import jax.numpy as jnp
from jax import lax
from jax.sharding import PartitionSpec as P


def prefix(value, axis, combine, identity, reverse):
    peers, mine = (lax.axis_size(axis), lax.axis_index(axis))
    everything = jax.tree.map(lambda part: lax.all_gather(part, axis), value)
    start = jax.tree.map(
        lambda part, zero: jnp.broadcast_to(jnp.asarray(zero, part.dtype), part.shape),
        value,
        identity,
    )

    def step(k, before):
        at = peers - 1 - k if reverse else k
        reached = at > mine if reverse else at < mine
        new = combine(before, jax.tree.map(lambda part: part[at], everything))
        return jax.tree.map(lambda a, b: jnp.where(reached, a, b), new, before)

    return lax.fori_loop(0, peers, step, start)


def with_halo(block, sides, width):
    for axis, dim in sides:
        count = lax.axis_size(axis)
        forward = [(i, i + 1) for i in range(count - 1)]
        forward.append((count - 1, 0))
        backward = [(target, source) for source, target in forward]
        low = lax.ppermute(
            lax.slice_in_dim(block, block.shape[dim] - width, None, axis=dim), axis, forward
        )
        high = lax.ppermute(lax.slice_in_dim(block, 0, width, axis=dim), axis, backward)
        block = jnp.concatenate([low, block, high], axis=dim)
    return block


def from_behind(value, axis, by):
    peers = lax.axis_size(axis)
    pairs = [(i, i + by) for i in range(peers) if 0 <= i + by < peers]
    return lax.ppermute(value, axis, pairs)


def apply_block(blocks, values_in):
    n_comp = blocks.shape[0]
    running = blocks[:, 0][:, None] * values_in[0][None]
    for member in range(1, n_comp):
        running = running + blocks[:, member][:, None] * values_in[member][None]
    return running


def compose(earlier, later):
    return (earlier[0] * later[0], later[0] * earlier[1] + later[1])


def local_scan(survival_fraction, source, backward):
    return lax.associative_scan(compose, (survival_fraction, source), reverse=backward, axis=3)


def chain_entry(end_rate, end_value, backward):
    identity_pair = (jnp.ones_like(end_rate), jnp.zeros_like(end_value))
    if backward:
        result = prefix((end_rate, end_value), "line", compose, identity_pair, True)
    else:
        result = prefix((end_rate, end_value), "line", compose, identity_pair, False)
    entry_value = result[1]
    return entry_value


def local(forcing, block_inverse, wall_rates, span_couple):
    n_comp, n_cols, n_station, n_point = forcing.shape
    row_count = n_comp * n_station * lax.axis_size("tile") * n_point * lax.axis_size("line")
    coupling = span_couple[:, None, None, None]
    rise_rate = wall_rates[0][:, None]
    fall_rate = wall_rates[1][:, None]
    start_field = apply_block(block_inverse, forcing)
    padded_start = with_halo(start_field, (("tile", 2),), 1)
    beside_zero = padded_start[:, :, :-2] + padded_start[:, :, 2:]
    next_row = from_behind(start_field[..., 0], "line", -1)
    above_row = jnp.concatenate([start_field[..., 1:], next_row[..., None]], axis=-1)
    source_one = (
        apply_block(block_inverse, forcing + coupling * beside_zero) + fall_rate * above_row
    )
    product_one, local_one = local_scan(rise_rate, source_one, False)
    entry_one = chain_entry(product_one[..., -1], local_one[..., -1], False)
    rising = product_one * entry_one[..., None] + local_one
    padded_one = with_halo(rising, (("tile", 2),), 1)
    beside_one = padded_one[:, :, :-2] + padded_one[:, :, 2:]
    below_row = jnp.concatenate([entry_one[..., None], rising[..., :-1]], axis=-1)
    source_two = apply_block(block_inverse, forcing + coupling * beside_one) + rise_rate * below_row
    product_two, local_two = local_scan(fall_rate, source_two, True)
    entry_two = chain_entry(product_two[..., 0], local_two[..., 0], True)
    falling = product_two * entry_two[..., None] + local_two
    local_gram = jnp.einsum("krzj,kszj->rs", falling, falling, precision=lax.Precision.HIGHEST)
    gram = lax.psum(local_gram, ("line", "tile"))
    lower_factor = jnp.linalg.cholesky(gram)
    identity_matrix = jnp.eye(n_cols, dtype=gram.dtype)
    inverse_factor = jax.scipy.linalg.solve_triangular(lower_factor, identity_matrix, lower=True).T
    scale_value = math.sqrt(row_count)
    return (
        jnp.einsum("krzj,rs->kszj", falling, inverse_factor, precision=lax.Precision.HIGHEST)
        * scale_value
    )


def solution(mesh):
    in_specs = (
        P(None, None, "tile", "line"),
        P(None, None, "tile", "line"),
        P(None, None, "tile", "line"),
        P(),
    )
    out_specs = P(None, None, "tile", "line")
    return jax.shard_map(local, mesh=mesh, in_specs=in_specs, out_specs=out_specs, check_vma=False)
```

profile of v0, /device:TPU:1, one launch (start us, length us, event | category | flops | bytes accessed | tf_op | source)
XLA Modules:
  0.0 211.6 jit_solution(14242950842360742571)
XLA Ops:
  0.0 0.8 fusion.26
  0.8 0.9 fusion.25
  2.8 1.8 multiply_add_fusion.2
  4.8 8.7 %collective-permute-start.1 = (f32[10,64,1,128]{3,1,2,0:T(8,128)S(1)}, f32[10,64,1,128]{3,1,2,0:T(8,128)S(1)}, u32[]{:S(2)}, u32[]{:S(2)}) collective-permute-start(f32[10,64,1,128]{3,1,2,0:T(8,128)S(1)} %copy.529), channel_id=1, source_target_pairs={{1,0},{2,1},{3,2},{4,3},{5,4},{6,5},{7,6},{8,7},{9,8},{10,9},{11,1... | collective-permute-start | bytes 983048 | tf_op jit(solution)/shard_map/ppermute | solution.py:36
  13.6 1.9 collective-permute-start
  15.5 1.3 collective-permute-start.2
  17.4 0.5 copy-done.3
  18.4 0.5 copy-done.4
  19.3 0.6 slice-done.2
  20.3 0.6 slice-done.3
  22.3 1.3 dynamic-slice
  24.5 8.3 %all-reduce.58 = (f32[40]{0:T(128)S(1)}, f32[40]{0:T(128)S(1)}) all-reduce(f32[40]{0:T(128)S(1)} %fusion.23, f32[40]{0:T(128)S(1)} %fusion.24), channel_id=3, replica_groups=mesh['line'=4,'tile'=128] {'line'}, use_global_device_ids=true, to_apply=%add.57 | all-reduce | flops 80 | bytes 640
  32.9 0.6 copy-done.6
  34.7 2.1 fusion
  36.8 0.3 slice.735
  37.1 0.3 slice.706
  37.4 0.3 slice.705
  37.8 0.2 slice.733
  40.0 0.2 slice.727
  40.3 0.2 slice.718
  41.1 0.2 slice.720
  42.0 0.6 slice-done
  44.3 9.1 %all-gather.2 = f32[40,64,1,1]{1,3,2,0:T(1,128)S(1)} all-gather(f32[10,64,1,1]{1,3,2,0:T(1,128)S(1)} %slice_add_fusion.3), channel_id=4, replica_groups=mesh['line'=4,'tile'=128] {'line'}, dimensions={0}, use_global_device_ids=true | all-gather | bytes 12800 | tf_op jit(solution)/shard_map/all_gather | solution.py:11
  53.5 0.5 while.30
  54.0 0.2 multiply_add_fusion.1
  54.4 14.4 %collective-permute-start.4 = (f32[10,64,1,128]{3,1,2,0:T(8,128)S(1)}, f32[10,64,1,128]{3,1,2,0:T(8,128)S(1)}, u32[]{:S(2)}, u32[]{:S(2)}) collective-permute-start(f32[10,64,1,128]{3,1,2,0:T(8,128)S(1)} %copy.556), channel_id=1, source_target_pairs={{1,0},{2,1},{3,2},{4,3},{5,4},{6,5},{7,6},{8,7},{9,8},{10,9},{11,1... | collective-permute-start | bytes 983048 | tf_op jit(solution)/shard_map/ppermute | solution.py:36
  68.8 2.1 collective-permute-start.3
  72.1 2.6 %collective-permute-done.3 = f32[10,64,1,128]{3,1,2,0:T(8,128)S(1)} collective-permute-done((f32[10,64,1,128]{3,1,2,0:T(8,128)S(1)}, f32[10,64,1,128]{3,1,2,0:T(8,128)S(1)}, u32[]{:S(2)}, u32[]{:S(2)}) %collective-permute-start.3) | collective-permute-done | bytes 327712 | tf_op jit(solution)/shard_map/ppermute | solution.py:33
  75.9 2.1 fusion.1
  78.0 0.3 slice.781
  78.3 0.3 slice.751
  78.6 0.3 slice.749
  79.1 0.2 slice.779
  81.3 0.2 slice.773
  81.6 0.2 slice.764
  82.4 0.2 slice.766
  83.4 0.6 slice-done.1
  85.8 0.3 rev.9
  86.1 9.1 %all-gather.3 = f32[40,64,1,1]{1,3,2,0:T(1,128)S(1)} all-gather(f32[10,64,1,1]{1,3,2,0:T(1,128)S(1)} %slice_add_fusion), channel_id=5, replica_groups=mesh['line'=4,'tile'=128] {'line'}, dimensions={0}, use_global_device_ids=true | all-gather | bytes 12800 | tf_op jit(solution)/shard_map/all_gather | solution.py:11
  95.2 0.5 while.31
  95.7 1.6 convolution_bitcast_fusion.1
  97.3 100.2 %psum.7 = f32[64,64]{0,1:T(8,128)S(1)} all-reduce(f32[64,64]{0,1:T(8,128)S(1)} %convolution_bitcast_fusion.1), channel_id=1, replica_groups=mesh['line'=4,'tile'=128] {'line','tile'}, use_global_device_ids=true, to_apply=%region_4.5 | all-reduce | flops 4096 | bytes 32768 | tf_op jit(solution)/shard_map/psum | solution.py:98
  197.7 5.8 %cholesky.17 = f32[64,64]{1,0:T(8,128)S(1)} custom-call(f32[64,64]{1,0:T(8,128)S(1)} %fusion.18), custom_call_target="Cholesky" | custom-call | tf_op jit(solution)/shard_map/jit(cholesky)/cholesky | solution.py:99
  203.6 0.6 compare_reduce_fusion
  204.2 0.7 fusion.16
  204.9 4.9 %custom-call.7 = f32[1,64,64]{1,2,0:T(8,128)S(1)} custom-call(f32[1,64,64]{2,1,0:T(8,128)S(1)} %fusion.16), custom_call_target="InvertDiagBlocksLowerTriangular" | custom-call | tf_op jit(solution)/shard_map/jit(_solve_triangular)/triangular_solve | solution.py:101
  209.8 0.2 convolution_bitcast_fusion
  210.0 1.6 convolution_multiply_fusion
  (350 shorter events, 18.3 us)
Async XLA Ops:
  4.8 12.0 %copy-start.5 = (f32[2,10,1,128]{3,2,1,0:T(1,128)S(1)}, f32[2,10,1,128]{3,2,1,0:T(1,128)}, u32[]{:S(2)}) copy-start(f32[2,10,1,128]{3,2,1,0:T(1,128)} %param.10) | copy-start | bytes 30724
  4.8 28.1 %collective-permute-start.1 = (f32[10,64,1,128]{3,1,2,0:T(8,128)S(1)}, f32[10,64,1,128]{3,1,2,0:T(8,128)S(1)}, u32[]{:S(2)}, u32[]{:S(2)}) collective-permute-start(f32[10,64,1,128]{3,1,2,0:T(8,128)S(1)} %copy.529), channel_id=1, source_target_pairs={{1,0},{2,1},{3,2},{4,3},{5,4},{6,5},{7,6},{8,7},{9,8},{10,9},{11,1... | collective-permute-start | bytes 983048 | tf_op jit(solution)/shard_map/ppermute | solution.py:36
  13.6 19.3 %collective-permute-start = (f32[10,64,1,128]{3,1,2,0:T(8,128)S(1)}, f32[10,64,1,128]{3,1,2,0:T(8,128)S(1)}, u32[]{:S(2)}, u32[]{:S(2)}) collective-permute-start(f32[10,64,1,128]{3,1,2,0:T(8,128)S(1)} %copy.529), channel_id=1, source_target_pairs={{0,1},{1,2},{2,3},{3,4},{4,5},{5,6},{6,7},{7,8},{8,9},{9,10},{10,1... | collective-permute-start | bytes 983048 | tf_op jit(solution)/shard_map/ppermute | solution.py:33
  15.5 19.2 %collective-permute-start.2 = (f32[10,64,1]{1,2,0:T(1,128)S(1)}, f32[10,64,1]{1,2,0:T(1,128)S(1)}, u32[]{:S(2)}, u32[]{:S(2)}) collective-permute-start(f32[10,64,1]{1,2,0:T(1,128)S(1)} %slice_bitcast_fusion.20), channel_id=1, source_target_pairs={{128,0},{256,128},{384,256},{129,1},{257,129},{385,257},{130,2},{2... | collective-permute-start | bytes 7688 | tf_op jit(solution)/shard_map/ppermute | solution.py:44
  17.3 0.6 copy-start.3
  18.4 0.6 copy-start.4
  19.3 0.6 slice-start.2
  20.3 0.7 slice-start.3
  22.2 10.8 %copy-start = (f32[10,64,1,128]{3,2,1,0:T(1,128)S(1)}, f32[10,64,1,128]{3,2,1,0:T(1,128)}, u32[]{:S(2)}) copy-start(f32[10,64,1,128]{3,2,1,0:T(1,128)} %param.8) | copy-start | bytes 983044
  32.9 0.7 copy-start.6
  40.0 0.6 copy-start.1
  41.9 0.7 slice-start
  54.4 17.7 %collective-permute-start.4 = (f32[10,64,1,128]{3,1,2,0:T(8,128)S(1)}, f32[10,64,1,128]{3,1,2,0:T(8,128)S(1)}, u32[]{:S(2)}, u32[]{:S(2)}) collective-permute-start(f32[10,64,1,128]{3,1,2,0:T(8,128)S(1)} %copy.556), channel_id=1, source_target_pairs={{1,0},{2,1},{3,2},{4,3},{5,4},{6,5},{7,6},{8,7},{9,8},{10,9},{11,1... | collective-permute-start | bytes 983048 | tf_op jit(solution)/shard_map/ppermute | solution.py:36
  68.8 5.9 %collective-permute-start.3 = (f32[10,64,1,128]{3,1,2,0:T(8,128)S(1)}, f32[10,64,1,128]{3,1,2,0:T(8,128)S(1)}, u32[]{:S(2)}, u32[]{:S(2)}) collective-permute-start(f32[10,64,1,128]{3,1,2,0:T(8,128)S(1)} %copy.556), channel_id=1, source_target_pairs={{0,1},{1,2},{2,3},{3,4},{4,5},{5,6},{6,7},{7,8},{8,9},{9,10},{10,1... | collective-permute-start | bytes 983048 | tf_op jit(solution)/shard_map/ppermute | solution.py:33
  81.3 0.6 copy-start.2
  83.3 0.7 slice-start.1
where the time goes:
time: 212 us
  blocking collectives  127 us (60%)
  starting transfers between devices  28.5 us (13%)
  local copies, waits for them, and re-layouts  24.6 us (12%)
  other arithmetic  22.9 us (11%)
  matrix products  3.48 us (2%)
  waiting for transfers between devices  2.65 us (1%)
  between operations  2.53 us (1%)
    psum x1, blocking collectives, local(): gram = lax.psum(local_gram, ('line', 'tile'))  100 us
    ppermute x2, starting transfers between devices, with_halo(): lax.ppermute(lax.slice_in_dim(block, 0, width, axis=dim), axis, backward)  23.1 us
    all_gather x2, blocking collectives, prefix(): everything = jax.tree.map(lambda part: lax.all_gather(part, axis), value)  18.3 us
    slice x98, local copies, waits for them, and re-layouts, local_scan(): lax.associative_scan(compose, (survival_fraction, source), reverse=backwa...  10.8 us
    unnamed x1, blocking collectives  8.34 us
    another operation x3, other arithmetic, local(): lower_factor = jnp.linalg.cholesky(gram)  6.52 us
    another operation x2, other arithmetic, local(): jax.scipy.linalg.solve_triangular(lower_factor, identity_matrix, lower=True)  5.55 us
  transfers between devices with their start and end apart: 5, of which 1 were waited for; matrix products, arithmetic and copies ran while one was open for 3% of the time, Pallas kernels for 0%

commit v1 on v0

v1 whole, which is shorter than its diff:
```python
import math

import jax
import jax.numpy as jnp
from jax import lax
from jax.experimental import pallas as pl
from jax.experimental.pallas import tpu as pltpu
from jax.sharding import Mesh, PartitionSpec as P

NZ, NY, NCORE = 8, 8, 2
TILE = ("z", "y", "core")
HIGH = lax.Precision.HIGHEST
F32 = jnp.float32
LANES = 128
STEPS = (1, 2, 4, 8, 16, 32, 64)
VMEM = pl.BlockSpec(memory_space=pltpu.VMEM)
SMEM = pl.BlockSpec(memory_space=pltpu.SMEM)


def lane_ids(rows):
    return lax.broadcasted_iota(jnp.int32, (rows, LANES), 1)


def row_ids(rows):
    return lax.broadcasted_iota(jnp.int32, (rows, LANES), 0)


def dot_nt(a, b):
    return lax.dot_general(
        a, b, (((1,), (1,)), ((), ())), precision=HIGH, preferred_element_type=F32
    )


def call(body, outs, flops=0, scratch=()):
    many = isinstance(outs[0], tuple)
    shapes = [jax.ShapeDtypeStruct(s, F32) for s in (outs if many else [outs])]

    def run(*args):
        size = sum(a.size for a in args) + sum(math.prod(s.shape) for s in shapes)
        return pl.pallas_call(
            body,
            out_shape=shapes if many else shapes[0],
            in_specs=[SMEM if a.ndim == 1 else VMEM for a in args],
            out_specs=[VMEM] * len(shapes) if many else VMEM,
            scratch_shapes=list(scratch),
            cost_estimate=pl.CostEstimate(
                flops=flops, bytes_accessed=4 * size, transcendentals=0
            ),
        )(*args)

    return run


def apply_rows(b_ref, k, n, take, rows):
    total = b_ref[k * n : k * n + 1, :] * take(0)
    for m in range(1, n):
        total = total + b_ref[k * n + m : k * n + m + 1, :] * take(m)
    return total


def start_body(f_ref, b_ref, s_ref):
    n, cols, _ = f_ref.shape
    for g in range(0, cols, 16):
        vals = [f_ref[m, g : g + 16, :] for m in range(n)]
        for k in range(n):
            s_ref[k, g : g + 16, :] = apply_rows(b_ref, k, n, lambda m: vals[m], 16)


def rates_body(w_ref, up_ref, down_ref, pre_ref, suf_ref, row_ref, ext_ref):
    n = w_ref.shape[0] // 2
    lane = lane_ids(n)
    up, down = w_ref[0:n, :], w_ref[n : 2 * n, :]
    pre, suf = up, down
    p = jnp.where(lane >= 1, up, 0.0)
    q = jnp.where(lane < LANES - 1, down, 0.0)
    for i, d in enumerate(STEPS):
        up_ref[i, 0:n, :] = p
        down_ref[i, 0:n, :] = q
        p = p * pltpu.roll(p, d, 1)
        q = q * pltpu.roll(q, LANES - d, 1)
        pre = jnp.where(lane >= d, pre * pltpu.roll(pre, d, 1), pre)
        suf = jnp.where(lane < LANES - d, suf * pltpu.roll(suf, LANES - d, 1), suf)
    pre_ref[0:n, :] = pre
    suf_ref[0:n, :] = suf
    norm = jnp.sum(suf * suf, axis=1, keepdims=True)
    table = jnp.zeros((8, LANES), F32)
    at, row = lane_ids(8), row_ids(8)
    for k in range(n):
        mine = jnp.where(row == 0, pre[k : k + 1, LANES - 1 : LANES], 0.0)
        mine = jnp.where(row == 1, down[k : k + 1, LANES - 1 : LANES], mine)
        mine = jnp.where(row == 2, suf[k : k + 1, 0:1], mine)
        mine = jnp.where(row == 3, norm[k : k + 1, 0:1], mine)
        table = jnp.where(lax.rem(at, 16) == k, mine, table)
    row_ref[...] = table
    place = row_ids(64)
    first = (lane_ids(64) == 0).astype(F32)
    for k in range(n):
        block = jnp.where(place == k, jnp.broadcast_to(suf[k : k + 1, :], (64, LANES)), 0.0)
        block = jnp.where(place == 16 + k, first, block)
        ext_ref[:, k * LANES : (k + 1) * LANES] = block


def neighbours_into(h_ref, c_ref, n_ref, g_ref):
    other = 1 - lax.axis_index("core")
    for m in range(n_ref.shape[0]):
        h_ref[m] = c_ref[m] * (n_ref[m] + g_ref[other, m])


def up_body(c_ref, b_ref, w_ref, s_ref, n_ref, g_ref, up_ref, row_ref, loc_ref, pay_ref, h_ref):
    n, cols, _ = s_ref.shape
    neighbours_into(h_ref, c_ref, n_ref, g_ref)
    lane = lane_ids(16)
    inner = lane < LANES - 1
    groups = cols // 16
    pay = jnp.zeros((16, LANES), F32)
    for k in range(n):
        fall = w_ref[n + k : n + k + 1, :]
        for g in range(groups):
            rows = slice(16 * g, 16 * g + 16)
            s = s_ref[k, rows, :]
            above = jnp.where(inner, pltpu.roll(s, LANES - 1, 1), 0.0)
            v = s + fall * above + apply_rows(b_ref, k, n, lambda m: h_ref[m, rows, :], 16)
            for i, d in enumerate(STEPS):
                v = v + up_ref[i, k : k + 1, :] * pltpu.roll(v, d, 1)
            loc_ref[k, rows, :] = v
            pay = jnp.where(lane == 32 * g + k, v[:, LANES - 1 : LANES], pay)
            pay = jnp.where(lane == 32 * g + 16 + k, s[:, 0:1], pay)
    for peer in range(pay_ref.shape[0]):
        pay_ref[peer, 0:16, :] = pay
        pay_ref[peer, 16:24, :] = row_ref[...]


def enter_body(r_ref, loc_ref, pre_ref, w_ref, out_ref, edge_ref):
    n, cols, _ = loc_ref.shape
    peers = r_ref.shape[0]
    mine = lax.axis_index("line")
    state = jnp.zeros((16, LANES), F32)
    entry = state
    top = state
    for at in range(peers - 1):
        lead = pltpu.roll(r_ref[at + 1, 0:16, :], LANES - 16, 1)
        tail = r_ref[at, 17:18, :] * lead
        top = jnp.where(mine == at, tail, top)
        state = r_ref[at, 16:17, :] * state + (r_ref[at, 0:16, :] + tail)
        entry = jnp.where(mine == at + 1, state, entry)
    lane = lane_ids(16)
    for k in range(n):
        pre = pre_ref[k : k + 1, :]
        for g in range(cols // 16):
            rows = slice(16 * g, 16 * g + 16)
            at = 32 * g + k
            v = loc_ref[k, rows, :] + pre * entry[:, at : at + 1]
            out_ref[k, rows, :] = jnp.where(lane == LANES - 1, v + top[:, at : at + 1], v)
    edge_ref[...] = entry


def below_body(s_ref, up_ref, edge_ref, w_ref, out_ref):
    n, cols, _ = s_ref.shape
    lane = lane_ids(16)
    entry = edge_ref[...]
    for k in range(n):
        rise = w_ref[k : k + 1, :]
        for g in range(cols // 16):
            rows = slice(16 * g, 16 * g + 16)
            at = 32 * g + k
            below = pltpu.roll(up_ref[k, rows, :], 1, 1)
            below = jnp.where(lane == 0, entry[:, at : at + 1], below)
            out_ref[k, rows, :] = s_ref[k, rows, :] + rise * below


def down_body(c_ref, b_ref, base_ref, n_ref, g_ref, down_ref, ext_ref, loc_ref, pay_ref, h_ref, a_ref):
    n, cols, _ = base_ref.shape
    neighbours_into(h_ref, c_ref, n_ref, g_ref)
    for k in range(n):
        for g in range(cols // 16):
            rows = slice(16 * g, 16 * g + 16)
            v = base_ref[k, rows, :] + apply_rows(b_ref, k, n, lambda m: h_ref[m, rows, :], 16)
            for i, d in enumerate(STEPS):
                v = v + down_ref[i, k : k + 1, :] * pltpu.roll(v, LANES - d, 1)
            loc_ref[k, rows, :] = v
            a_ref[rows, k * LANES : (k + 1) * LANES] = v
    a_ref[cols : 2 * cols, :] = ext_ref[...]
    total = dot_nt(a_ref[0:cols, :], a_ref[...])
    for peer in range(pay_ref.shape[0]):
        pay_ref[peer] = total


def line_body(r_ref, q_ref, gram_ref, entry_ref):
    peers, cols, _ = r_ref.shape
    mine = lax.axis_index("line")
    lane = lane_ids(cols)
    state = jnp.zeros((cols, LANES), F32)
    entry = state
    left = state
    total = r_ref[peers - 1]
    for at in range(peers - 2, -1, -1):
        state = q_ref[at + 1, 18:19, :] * state + r_ref[at + 1]
        entry = jnp.where(mine == at, state, entry)
        total = total + r_ref[at]
        cross = r_ref[at] + (0.5 * q_ref[at, 19:20, :]) * pltpu.roll(state, LANES - 16, 1)
        here = (lane >= 16 * at) & (lane < 16 * at + 10)
        left = jnp.where(here, pltpu.roll(cross, (LANES + 16 * at - 64) % LANES, 1), left)
        here = (lane >= 64 + 16 * at) & (lane < 64 + 16 * at + 10)
        left = jnp.where(here, pltpu.roll(state, (LANES + 16 * at - 16) % LANES, 1), left)
    fix = dot_nt(left, pltpu.roll(left, 64, 1))
    half = cols // 2
    gram = total[:, 0:64] + fix
    gram_ref[:, 0:64] = gram[0:half, :]
    gram_ref[:, 64:128] = gram[half:cols, :]
    entry_ref[...] = entry


def sum_body(r_ref, o_ref):
    total = r_ref[0]
    for i in range(1, r_ref.shape[0]):
        total = total + r_ref[i]
    for peer in range(o_ref.shape[0]):
        o_ref[peer] = total


def basis_body(scale, r_ref, loc_ref, suf_ref, entry_ref, out_ref, f_ref):
    n, cols, _ = loc_ref.shape
    for k in range(n):
        e = entry_ref[:, 80 + k : 81 + k]
        f_ref[:, k * LANES : (k + 1) * LANES] = loc_ref[k] + suf_ref[k : k + 1, :] * e
    packed = r_ref[0]
    for i in range(1, r_ref.shape[0]):
        packed = packed + r_ref[i]
    low = pltpu.roll(packed, 64, 1)
    lane, row = lane_ids(cols), row_ids(cols)
    m = jnp.concatenate([packed, low], axis=0)
    m = jnp.where(lane < 64, m, jnp.where(lane - 64 == row, 1.0, 0.0))
    diag = jnp.zeros((cols, LANES), F32)
    for j in range(cols):
        col = jnp.broadcast_to(m[:, j : j + 1], (cols, LANES))
        pivot = jnp.broadcast_to(col[j : j + 1, :], (cols, LANES))
        diag = jnp.where(row == j, pivot, diag)
        factor = jnp.where(row > j, col / pivot, 0.0)
        m = m - factor * m[j : j + 1, :]
    inv = pltpu.roll(m * (scale / jnp.sqrt(diag)), 64, 1)[:, 0:64]
    out = jnp.dot(inv, f_ref[...], precision=HIGH, preferred_element_type=F32)
    for k in range(n):
        out_ref[k] = out[:, k * LANES : (k + 1) * LANES]


def exchange(value, axis):
    return lax.all_to_all(value, axis, 0, 0, tiled=True)


def local(forcing, block_inverse, wall_rates, span_couple):
    n, cols, _, pts = forcing.shape
    peers = lax.axis_size("line")
    stations = lax.axis_size("z") * lax.axis_size("y") * lax.axis_size("core")
    rows = n * stations * pts * peers
    field = (n, cols, pts)
    f = forcing.reshape(field)
    b = block_inverse.reshape(n * n, pts)
    w = wall_rates.reshape(2 * n, pts)
    across = [(i, (i + 1) % stations if i % 2 else (i - 1) % stations) for i in range(stations)]
    work = 2 * n * n * cols * pts
    scratch = pltpu.VMEM(field, F32)

    start = call(start_body, field, work)(f, b)
    far = lax.ppermute(start, TILE, across)
    near = lax.all_gather(start, "core")
    steps = (len(STEPS), 16, pts)
    up, down, pre, suf, row, ext = call(
        rates_body, [steps, steps, (16, pts), (16, pts), (8, pts), (64, n * pts)], work // 8
    )(w)
    loc, pay = call(up_body, [field, (peers, 24, pts)], 2 * work, [scratch])(
        span_couple, b, w, start, far, near, up, row
    )
    got = exchange(pay, "line")
    rising, edge = call(enter_body, [field, (16, pts)], work // 4)(got, loc, pre, w)
    far = lax.ppermute(rising, TILE, across)
    near = lax.all_gather(rising, "core")
    base = call(below_body, field, work // 4)(start, rising, edge, w)
    wide = pltpu.VMEM((2 * cols, n * pts), F32)
    loc, pay = call(down_body, [field, (peers, cols, pts)], 4 * work, [scratch, wide])(
        span_couple, b, base, far, near, down, ext
    )
    sums = exchange(pay, "line")
    gram, entry = call(line_body, [(cols // 2, pts), (cols, pts)], work // 4)(sums, got)
    half = (cols // 2, pts)
    both = lax.all_gather(gram, "core")
    gram = call(sum_body, (NY,) + half)(both)
    gram = call(sum_body, (NZ,) + half)(exchange(gram, "y"))
    gram = exchange(gram, "z")

    def basis(*refs):
        basis_body(math.sqrt(rows), *refs)

    out = call(basis, field, 4 * work, [pltpu.VMEM((cols, n * pts), F32)])(gram, loc, suf, entry)
    return out.reshape(n, cols, 1, pts)


def solution(mesh):
    devices = mesh.devices.reshape(mesh.shape["line"], NZ, NY, NCORE)
    inner = Mesh(devices, ("line",) + TILE)
    spec = P(None, None, TILE, "line")
    return jax.shard_map(
        local, mesh=inner, in_specs=(spec, spec, spec, P()), out_specs=spec, check_vma=False
    )
```

time: 212 us -> 118 us (0.56)
  blocking collectives: 127 us -> 70.5 us
  Pallas kernels: 0 us -> 36.3 us
  starting transfers between devices: 28.5 us -> 6.48 us
  other arithmetic: 22.9 us -> 0.96 us
  local copies, waits for them, and re-layouts: 24.6 us -> 2.7 us
  matrix products: 3.48 us -> 0 us
  between operations: 2.53 us -> 0.06 us
  waiting for transfers between devices: 2.65 us -> 0.39 us
    psum x1 -> x0, blocking collectives: 100 us -> none  [local(): gram = lax.psum(local_gram, ('line', 'tile'))]
    all_to_all x0 -> x4, blocking collectives: none -> 41.9 us  [exchange(): return lax.all_to_all(value, axis, 0, 0, tiled=True)]
    pallas_call x0 -> x10, Pallas kernels: none -> 36.3 us  [run(): pl.pallas_call(body, out_shape=shapes if many else shapes[0], in_specs=[S...]
    ppermute x5 -> x2, starting transfers between devices: 28.5 us -> 6.48 us  [the longest x1 4.57 us: local(): far = lax.ppermute(start, TILE, across)]
    slice x102 -> x0, local copies, waits for them, and re-layouts: 12.6 us -> none  [the longest x98 10.8 us: local_scan(): lax.associative_scan(compose, (survival_fraction, source), reverse=backwa...]
    another operation x5 -> x0, other arithmetic: 12.1 us -> none  [the longest x3 6.52 us: local(): lower_factor = jnp.linalg.cholesky(gram)]
    all_gather x2 -> x3, blocking collectives: 18.3 us -> 28.6 us  [the longest x1 15.5 us: local(): near = lax.all_gather(start, 'core')]
    add x58 -> x0, other arithmetic: 9.13 us -> none  [the longest x24 2.34 us: compose(): return (earlier[0] * later[0], later[0] * earlier[1] + later[1])]
  transfers between devices with their start and end apart: 5 -> 2, of which waited for: 1 -> 1; matrix products, arithmetic and copies ran while one was open for 3% -> 1% of each run, Pallas kernels for 0% -> 4%
where the time goes in v1:
time: 118 us; the launch traced here: 117 us
  blocking collectives  70.5 us (60%)
  Pallas kernels  36.3 us (31%)
  starting transfers between devices  6.48 us (5%)
  local copies, waits for them, and re-layouts  2.7 us (2%)
    all_to_all x4, blocking collectives, exchange(): return lax.all_to_all(value, axis, 0, 0, tiled=True)  41.9 us
    pallas_call x10, Pallas kernels, run(): pl.pallas_call(body, out_shape=shapes if many else shapes[0], in_specs=[S...  36.3 us
    all_gather x1, blocking collectives, local(): near = lax.all_gather(start, 'core')  15.5 us
    all_gather x1, blocking collectives, local(): both = lax.all_gather(gram, 'core')  9 us
    ppermute x1, starting transfers between devices, local(): far = lax.ppermute(start, TILE, across)  4.57 us
    all_gather x1, blocking collectives, local(): near = lax.all_gather(rising, 'core')  4.06 us
  transfers between devices with their start and end apart: 2, of which 1 were waited for; matrix products, arithmetic and copies ran while one was open for 1% of the time, Pallas kernels for 4%

profile of v1, /device:TPU:1, one launch (start us, length us, event | category | flops | bytes accessed | tf_op | source)
XLA Modules:
  0.0 117.4 jit_solution(2122517362564282731)
XLA Ops:
  0.0 0.9 reduce
  0.9 0.6 reshape.12.b_ref
  1.6 0.0 copy-start.3
  1.6 1.9 %shard_map.46.s_ref = f32[10,64,128]{2,1,0:T(8,128)} custom-call(f32[10,64,128]{2,1,0:T(8,128)} %bitcast.9, f32[100,128]{1,0:T(8,128)} %reshape.12.b_ref), custom_call_target="tpu_custom_call" | custom-call | flops 1638400 | bytes 706560 | tf_op jit(solution)/shard_map/pallas_call | solution.py:40
  3.5 4.6 %collective-permute-start = (f32[10,64,128]{2,1,0:T(8,128)}, f32[10,64,128]{2,1,0:T(8,128)S(1)}, u32[]{:S(2)}, u32[]{:S(2)}) collective-permute-start(f32[10,64,128]{2,1,0:T(8,128)} %shard_map.46.s_ref), channel_id=1, source_target_pairs={{0,127},{1,2},{2,1},{3,4},{4,3},{5,6},{6,5},{7,8},{8,7},{9,10},{10... | collective-permute-start | bytes 983048 | tf_op jit(solution)/shard_map/ppermute | solution.py:264
  8.1 0.0 copy-done.3
  8.1 0.6 reshape.14.w_ref
  8.7 2.1 %shard_map.47 = (f32[7,16,128]{2,1,0:T(8,128)}, f32[7,16,128]{2,1,0:T(8,128)}, f32[16,128]{1,0:T(8,128)}, f32[16,128]{1,0:T(8,128)}, f32[8,128]{1,0:T(8,128)}, /*index=5*/f32[64,1280]{1,0:T(8,128)}) custom-call(f32[20,128]{1,0:T(8,128)} %reshape.14.w_ref), custom_call_target="tpu_custom_call" | custom-call | flops 204800 | bytes 473088 | tf_op jit(solution)/shard_map/pallas_call | solution.py:40
  10.8 15.5 %all-gather = f32[20,64,128]{2,1,0:T(8,128)} all-gather(f32[10,64,128]{2,1,0:T(8,128)} %shard_map.46.s_ref), channel_id=2, replica_groups=mesh['line'=4,'z'=8,'y'=8,'core'=2] {'core'}, dimensions={0}, use_global_device_ids=true | all-gather | bytes 983040 | tf_op jit(solution)/shard_map/all_gather | solution.py:265
  26.3 0.0 collective-permute-done.n_ref
  26.3 0.0 copy-start.2
  26.3 0.7 copy-done.2
  27.1 8.8 %shard_map.48 = (f32[10,64,128]{2,1,0:T(8,128)}, f32[4,24,128]{2,1,0:T(8,128)}) custom-call(f32[10]{0:T(128)} %c_ref.3, f32[100,128]{1,0:T(8,128)} %reshape.12.b_ref, f32[20,128]{1,0:T(8,128)} %reshape.14.w_ref, f32[10,64,128]{2,1,0:T(8,128)} %shard_map.46.s_ref, f32[10,64,128]{2,1,0:T(8,128)} %copy-done.2, f32[2,10,64,128]{3,2,1,0:T(8,128)} %bitcast.8, ...), custom_call_target="tpu_custom_call" | custom-call | flops 3276800 | bytes 1810472 | tf_op jit(solution)/shard_map/pallas_call | solution.py:40
  35.8 8.5 %all_to_all.20.r_ref.q_ref = f32[4,24,128]{2,1,0:T(8,128)} all-to-all(f32[4,24,128]{2,1,0:T(8,128)} %get-tuple-element.21), channel_id=1, replica_groups=mesh['line'=4,'z'=8,'y'=8,'core'=2] {'line'}, dimensions={0} | all-to-all | bytes 98304 | tf_op jit(solution)/shard_map/all_to_all | solution.py:247
  44.3 2.1 %shard_map.49 = (f32[10,64,128]{2,1,0:T(8,128)}, f32[16,128]{1,0:T(8,128)}) custom-call(f32[4,24,128]{2,1,0:T(8,128)} %all_to_all.20.r_ref.q_ref, f32[10,64,128]{2,1,0:T(8,128)} %get-tuple-element.22.loc_ref, f32[16,128]{1,0:T(8,128)} %get-tuple-element.23.pre_ref, f32[20,128]{1,0:T(8,128)} %reshape.14.w_ref), custom_call_target="tpu_custom_call" | custom-call | flops 409600 | bytes 731136 | tf_op jit(solution)/shard_map/pallas_call | solution.py:40
  46.4 1.9 %collective-permute-start.1 = (f32[10,64,128]{2,1,0:T(8,128)}, f32[10,64,128]{2,1,0:T(8,128)S(1)}, u32[]{:S(2)}, u32[]{:S(2)}) collective-permute-start(f32[10,64,128]{2,1,0:T(8,128)} %get-tuple-element.24.up_ref), channel_id=1, source_target_pairs={{0,127},{1,2},{2,1},{3,4},{4,3},{5,6},{6,5},{7,8},{8,7},{9,10},{10... | collective-permute-start | bytes 983048 | tf_op jit(solution)/shard_map/ppermute | solution.py:275
  48.4 0.0 copy-start
  48.4 2.2 %shard_map.50.base_ref = f32[10,64,128]{2,1,0:T(8,128)} custom-call(f32[10,64,128]{2,1,0:T(8,128)} %shard_map.46.s_ref, f32[10,64,128]{2,1,0:T(8,128)} %get-tuple-element.24.up_ref, f32[16,128]{1,0:T(8,128)} %get-tuple-element.25.edge_ref, f32[20,128]{1,0:T(8,128)} %reshape.14.w_ref), custom_call_target="tpu_custom_call" | custom-call | flops 409600 | bytes 1001472 | tf_op jit(solution)/shard_map/pallas_call | solution.py:40
  50.6 0.0 copy-done
  50.6 4.1 %all-gather.1 = f32[20,64,128]{2,1,0:T(8,128)} all-gather(f32[10,64,128]{2,1,0:T(8,128)S(1)} %copy-done), channel_id=3, replica_groups=mesh['line'=4,'z'=8,'y'=8,'core'=2] {'core'}, dimensions={0}, use_global_device_ids=true | all-gather | bytes 983040 | tf_op jit(solution)/shard_map/all_gather | solution.py:276
  54.6 0.4 collective-permute-done.1.n_ref
  55.0 0.0 copy-start.1
  55.0 0.7 copy-done.1
  55.8 3.7 %shard_map.51 = (f32[10,64,128]{2,1,0:T(8,128)}, f32[4,64,128]{2,1,0:T(8,128)}) custom-call(f32[10]{0:T(128)} %c_ref.3, f32[100,128]{1,0:T(8,128)} %reshape.12.b_ref, f32[10,64,128]{2,1,0:T(8,128)} %shard_map.50.base_ref, f32[10,64,128]{2,1,0:T(8,128)} %copy-done.1, f32[2,10,64,128]{3,2,1,0:T(8,128)} %bitcast.7, f32[7,16,128]{2,1,0:T(8,128)} %get-tuple-element.26.down_ref, ...), custom_call_target="tpu_custom_call" | custom-call | flops 6553600 | bytes 2205736 | tf_op jit(solution)/shard_map/pallas_call | solution.py:40
  59.4 8.8 %all_to_all.21.r_ref = f32[4,64,128]{2,1,0:T(8,128)} all-to-all(f32[4,64,128]{2,1,0:T(8,128)} %get-tuple-element.28), channel_id=1, replica_groups=mesh['line'=4,'z'=8,'y'=8,'core'=2] {'line'}, dimensions={0} | all-to-all | bytes 262144 | tf_op jit(solution)/shard_map/all_to_all | solution.py:247
  68.3 2.0 %shard_map.52 = (f32[32,128]{1,0:T(8,128)}, f32[64,128]{1,0:T(8,128)}) custom-call(f32[4,64,128]{2,1,0:T(8,128)} %all_to_all.21.r_ref, f32[4,24,128]{2,1,0:T(8,128)} %all_to_all.20.r_ref.q_ref), custom_call_target="tpu_custom_call" | custom-call | flops 409600 | bytes 229376 | tf_op jit(solution)/shard_map/pallas_call | solution.py:40
  70.3 9.0 %all-gather.2 = f32[64,128]{1,0:T(8,128)} all-gather(f32[32,128]{1,0:T(8,128)} %get-tuple-element.29), channel_id=4, replica_groups=mesh['line'=4,'z'=8,'y'=8,'core'=2] {'core'}, dimensions={0}, use_global_device_ids=true | all-gather | bytes 49152 | tf_op jit(solution)/shard_map/all_gather | solution.py:285
  79.3 1.4 %shard_map.53 = f32[8,32,128]{2,1,0:T(8,128)} custom-call(f32[2,32,128]{2,1,0:T(8,128)} %bitcast.10), custom_call_target="tpu_custom_call" | custom-call | bytes 163840 | tf_op jit(solution)/shard_map/pallas_call | solution.py:40
  80.7 12.6 %all_to_all.22.r_ref = f32[8,32,128]{2,1,0:T(8,128)} all-to-all(f32[8,32,128]{2,1,0:T(8,128)} %shard_map.53), channel_id=1, replica_groups=mesh['line'=4,'z'=8,'y'=8,'core'=2] {'y'}, dimensions={0} | all-to-all | bytes 262144 | tf_op jit(solution)/shard_map/all_to_all | solution.py:247
  93.3 1.6 %shard_map.54 = f32[8,32,128]{2,1,0:T(8,128)} custom-call(f32[8,32,128]{2,1,0:T(8,128)} %all_to_all.22.r_ref), custom_call_target="tpu_custom_call" | custom-call | bytes 262144 | tf_op jit(solution)/shard_map/pallas_call | solution.py:40
  94.9 12.0 %all_to_all.23.refs_0_ = f32[8,32,128]{2,1,0:T(8,128)} all-to-all(f32[8,32,128]{2,1,0:T(8,128)} %shard_map.54), channel_id=1, replica_groups=mesh['line'=4,'z'=8,'y'=8,'core'=2] {'z'}, dimensions={0} | all-to-all | bytes 262144 | tf_op jit(solution)/shard_map/all_to_all | solution.py:247
  106.9 10.5 %shard_map.55 = f32[10,64,128]{2,1,0:T(8,128)} custom-call(f32[8,32,128]{2,1,0:T(8,128)} %all_to_all.23.refs_0_, f32[10,64,128]{2,1,0:T(8,128)} %get-tuple-element.30.refs_1_, f32[16,128]{1,0:T(8,128)} %get-tuple-element.31.refs_2_, f32[64,128]{1,0:T(8,128)} %get-tuple-element.32.refs_3_), custom_call_target="tpu_custom_call" | custom-call | flops 6553600 | bytes 827392 | tf_op jit(solution)/shard_map/pallas_call | solution.py:40
  (1 shorter events, 0.0 us)
Async XLA Ops:
  1.6 6.5 %copy-start.3 = (f32[2,10,1,128]{3,2,1,0:T(1,128)S(1)}, f32[2,10,1,128]{3,2,1,0:T(1,128)}, u32[]{:S(2)}) copy-start(f32[2,10,1,128]{3,2,1,0:T(1,128)} %param.6) | copy-start | bytes 30724
  3.5 22.8 %collective-permute-start = (f32[10,64,128]{2,1,0:T(8,128)}, f32[10,64,128]{2,1,0:T(8,128)S(1)}, u32[]{:S(2)}, u32[]{:S(2)}) collective-permute-start(f32[10,64,128]{2,1,0:T(8,128)} %shard_map.46.s_ref), channel_id=1, source_target_pairs={{0,127},{1,2},{2,1},{3,4},{4,3},{5,6},{6,5},{7,8},{8,7},{9,10},{10... | collective-permute-start | bytes 983048 | tf_op jit(solution)/shard_map/ppermute | solution.py:264
  26.3 0.7 copy-start.2
  46.4 8.6 %collective-permute-start.1 = (f32[10,64,128]{2,1,0:T(8,128)}, f32[10,64,128]{2,1,0:T(8,128)S(1)}, u32[]{:S(2)}, u32[]{:S(2)}) collective-permute-start(f32[10,64,128]{2,1,0:T(8,128)} %get-tuple-element.24.up_ref), channel_id=1, source_target_pairs={{0,127},{1,2},{2,1},{3,4},{4,3},{5,6},{6,5},{7,8},{8,7},{9,10},{10... | collective-permute-start | bytes 983048 | tf_op jit(solution)/shard_map/ppermute | solution.py:275
  48.4 2.2 %copy-start = (f32[10,64,128]{2,1,0:T(8,128)S(1)}, f32[10,64,128]{2,1,0:T(8,128)}, u32[]{:S(2)}) copy-start(f32[10,64,128]{2,1,0:T(8,128)} %get-tuple-element.24.up_ref) | copy-start | bytes 983044
  55.0 0.7 copy-start.1

commit v2 on v1

--- a/solution.py
+++ b/solution.py
@@ -12,9 +12,11 @@
 HIGH = lax.Precision.HIGHEST
 F32 = jnp.float32
 LANES = 128
+LIMIT = 16 << 20
 STEPS = (1, 2, 4, 8, 16, 32, 64)
 VMEM = pl.BlockSpec(memory_space=pltpu.VMEM)
 SMEM = pl.BlockSpec(memory_space=pltpu.SMEM)
+HBM = pl.BlockSpec(memory_space=pltpu.HBM)
 
 
 def lane_ids(rows):
@@ -31,7 +33,7 @@
     )
 
 
-def call(body, outs, flops=0, scratch=()):
+def call(body, outs, flops=0, scratch=(), space=VMEM):
     many = isinstance(outs[0], tuple)
     shapes = [jax.ShapeDtypeStruct(s, F32) for s in (outs if many else [outs])]
 
@@ -40,9 +42,10 @@
         return pl.pallas_call(
             body,
             out_shape=shapes if many else shapes[0],
-            in_specs=[SMEM if a.ndim == 1 else VMEM for a in args],
+            in_specs=[SMEM if a.ndim == 1 else space for a in args],
             out_specs=[VMEM] * len(shapes) if many else VMEM,
             scratch_shapes=list(scratch),
+            compiler_params=pltpu.CompilerParams(vmem_limit_bytes=LIMIT),
             cost_estimate=pl.CostEstimate(
                 flops=flops, bytes_accessed=4 * size, transcendentals=0
             ),
@@ -51,25 +54,55 @@
     return run
 
 
-def apply_rows(b_ref, k, n, take, rows):
-    total = b_ref[k * n : k * n + 1, :] * take(0)
+def apply_rows(block, n, take):
+    total = block(0) * take(0)
     for m in range(1, n):
-        total = total + b_ref[k * n + m : k * n + m + 1, :] * take(m)
+        total = total + block(m) * take(m)
     return total
 
 
-def start_body(f_ref, b_ref, s_ref):
+def pick(values, mask):
+    total = None
+    for _ in range(3):
+        piece = values.astype(jnp.bfloat16)
+        values = values - piece.astype(F32)
+        part = lax.dot_general(
+            piece, mask, (((1,), (1,)), ((), ())), preferred_element_type=F32
+        )
+        total = part if total is None else total + part
+    return total
+
+
+def lane_mask(rows, n, shift, at):
+    wide = (rows, n * LANES)
+    col = lax.broadcasted_iota(jnp.int32, wide, 1)
+    row = lax.broadcasted_iota(jnp.int32, wide, 0)
+    return (col == (row - shift) * LANES + at).astype(jnp.bfloat16)
+
+
+def start_body(f_hbm, b_hbm, w_hbm, s_ref, b_ref, w_ref, f_ref, sems):
+    copies = [
+        pltpu.make_async_copy(src, dst, sems.at[i])
+        for i, (src, dst) in enumerate(((f_hbm, f_ref), (b_hbm, b_ref), (w_hbm, w_ref)))
+    ]
+    for copy in copies:
+        copy.start()
+    for copy in copies:
+        copy.wait()
     n, cols, _ = f_ref.shape
     for g in range(0, cols, 16):
         vals = [f_ref[m, g : g + 16, :] for m in range(n)]
         for k in range(n):
-            s_ref[k, g : g + 16, :] = apply_rows(b_ref, k, n, lambda m: vals[m], 16)
-
-
-def rates_body(w_ref, up_ref, down_ref, pre_ref, suf_ref, row_ref, ext_ref):
-    n = w_ref.shape[0] // 2
+            s_ref[k, g : g + 16, :] = apply_rows(lambda m: b_ref[k, m], n, lambda m: vals[m])
+
+
+def side_body(
+    c_ref, b_ref, w_ref, s_ref,
+    cb_ref, base_ref, edge_ref, up_ref, down_ref, pre_ref, suf_ref, row_ref, ext_ref, a_ref,
+):
+    n = w_ref.shape[1]
     lane = lane_ids(n)
-    up, down = w_ref[0:n, :], w_ref[n : 2 * n, :]
+    up, down = (jnp.concatenate([w_ref[i, k] for k in range(n)], axis=0) for i in range(2))
     pre, suf = up, down
     p = jnp.where(lane >= 1, up, 0.0)
     q = jnp.where(lane < LANES - 1, down, 0.0)
@@ -100,37 +133,51 @@
         ext_ref[:, k * LANES : (k + 1) * LANES] = block
 
 
-def neighbours_into(h_ref, c_ref, n_ref, g_ref):
+    inner = lane_ids(64) < LANES - 1
+    for k in range(n):
+        for m in range(n):
+            cb_ref[k * n + m : k * n + m + 1, :] = c_ref[m] * b_ref[k, m]
+        start = s_ref[k]
+        a_ref[:, k * LANES : (k + 1) * LANES] = start
+        above = jnp.where(inner, pltpu.roll(start, LANES - 1, 1), 0.0)
+        base_ref[k] = start + w_ref[1, k] * above
+    edge_ref[...] = pick(a_ref[...], lane_mask(32, n, 16, 0))
+
+
+def neighbours_into(h_ref, n_ref, g_ref):
     other = 1 - lax.axis_index("core")
     for m in range(n_ref.shape[0]):
-        h_ref[m] = c_ref[m] * (n_ref[m] + g_ref[other, m])
-
-
-def up_body(c_ref, b_ref, w_ref, s_ref, n_ref, g_ref, up_ref, row_ref, loc_ref, pay_ref, h_ref):
-    n, cols, _ = s_ref.shape
-    neighbours_into(h_ref, c_ref, n_ref, g_ref)
-    lane = lane_ids(16)
-    inner = lane < LANES - 1
-    groups = cols // 16
-    pay = jnp.zeros((16, LANES), F32)
-    for k in range(n):
-        fall = w_ref[n + k : n + k + 1, :]
-        for g in range(groups):
+        h_ref[m] = n_ref[m] + g_ref[other, m]
+
+
+def coupled(cb_ref, h_ref, k, n, rows):
+    return apply_rows(
+        lambda m: cb_ref[k * n + m : k * n + m + 1, :], n, lambda m: h_ref[m, rows, :]
+    )
+
+
+def up_body(cb_ref, base_ref, n_ref, g_ref, up_ref, edge_ref, row_ref, loc_ref, pay_ref, h_ref, a_ref):
+    n, cols, _ = base_ref.shape
+    neighbours_into(h_ref, n_ref, g_ref)
+    for k in range(n):
+        for g in range(cols // 16):
             rows = slice(16 * g, 16 * g + 16)
-            s = s_ref[k, rows, :]
-            above = jnp.where(inner, pltpu.roll(s, LANES - 1, 1), 0.0)
-            v = s + fall * above + apply_rows(b_ref, k, n, lambda m: h_ref[m, rows, :], 16)
+            v = base_ref[k, rows, :] + coupled(cb_ref, h_ref, k, n, rows)
             for i, d in enumerate(STEPS):
                 v = v + up_ref[i, k : k + 1, :] * pltpu.roll(v, d, 1)
             loc_ref[k, rows, :] = v
-            pay = jnp.where(lane == 32 * g + k, v[:, LANES - 1 : LANES], pay)
-            pay = jnp.where(lane == 32 * g + 16 + k, s[:, 0:1], pay)
+            a_ref[rows, k * LANES : (k + 1) * LANES] = v
+    ends = pick(a_ref[...], lane_mask(32, n, 0, LANES - 1)) + edge_ref[...]
+    ends = jnp.concatenate([ends, jnp.zeros((cols, LANES - 32), F32)], axis=1)
+    pay = ends[0:16, :]
+    for g in range(1, cols // 16):
+        pay = pay + pltpu.roll(ends[16 * g : 16 * g + 16, :], 32 * g, 1)
     for peer in range(pay_ref.shape[0]):
         pay_ref[peer, 0:16, :] = pay
         pay_ref[peer, 16:24, :] = row_ref[...]
 
 
-def enter_body(r_ref, loc_ref, pre_ref, w_ref, out_ref, edge_ref):
+def enter_body(r_ref, loc_ref, pre_ref, out_ref, edge_ref):
     n, cols, _ = loc_ref.shape
     peers = r_ref.shape[0]
     mine = lax.axis_index("line")
@@ -159,7 +206,7 @@
     lane = lane_ids(16)
     entry = edge_ref[...]
     for k in range(n):
-        rise = w_ref[k : k + 1, :]
+        rise = w_ref[0, k]
         for g in range(cols // 16):
             rows = slice(16 * g, 16 * g + 16)
             at = 32 * g + k
@@ -168,13 +215,13 @@
             out_ref[k, rows, :] = s_ref[k, rows, :] + rise * below
 
 
-def down_body(c_ref, b_ref, base_ref, n_ref, g_ref, down_ref, ext_ref, loc_ref, pay_ref, h_ref, a_ref):
+def down_body(cb_ref, base_ref, n_ref, g_ref, down_ref, ext_ref, loc_ref, pay_ref, h_ref, a_ref):
     n, cols, _ = base_ref.shape
-    neighbours_into(h_ref, c_ref, n_ref, g_ref)
+    neighbours_into(h_ref, n_ref, g_ref)
     for k in range(n):
         for g in range(cols // 16):
             rows = slice(16 * g, 16 * g + 16)
-            v = base_ref[k, rows, :] + apply_rows(b_ref, k, n, lambda m: h_ref[m, rows, :], 16)
+            v = base_ref[k, rows, :] + coupled(cb_ref, h_ref, k, n, rows)
             for i, d in enumerate(STEPS):
                 v = v + down_ref[i, k : k + 1, :] * pltpu.roll(v, LANES - d, 1)
             loc_ref[k, rows, :] = v
@@ -218,7 +265,44 @@
         o_ref[peer] = total
 
 
-def basis_body(scale, r_ref, loc_ref, suf_ref, entry_ref, out_ref, f_ref):
+def inverse_factor(scale, gram, v_ref):
+    cols = gram.shape[0]
+    count = cols // 8
+    lane, row = lane_ids(8), row_ids(8)
+    tiles = []
+    for t in range(count):
+        unit = jnp.where(lane - 64 == row + 8 * t, 1.0, 0.0)
+        tiles.append(jnp.where(lane < 64, gram[8 * t : 8 * t + 8, :], unit))
+    for p in range(count):
+        later = range(p + 1, count)
+        r = [tiles[p][i : i + 1, :] for i in range(8)]
+        s = {}
+        for i in range(8):
+            for j in range(i + 1):
+                at = 8 * p + j
+                s[i, j] = jnp.broadcast_to(r[i][:, at : at + 1], (1, LANES))
+        c = []
+        for i in range(8):
+            at = 8 * p + i
+            c.append([jnp.broadcast_to(tiles[t][:, at : at + 1], (8, LANES)) for t in later])
+        scaled = []
+        for i in range(8):
+            inv = 1.0 / s[i, i]
+            for t in range(i + 1, 8):
+                f = s[t, i] * inv
+                for u in range(i + 1, t + 1):
+                    s[t, u] = s[t, u] - f * s[u, i]
+                r[t] = r[t] - f * r[i]
+                c[t] = [x - f * y for x, y in zip(c[t], c[i])]
+            v_ref[8 * p + i : 8 * p + i + 1, :] = r[i] * (scale / jnp.sqrt(s[i, i]))
+            scaled.append(r[i] * inv)
+        for x, t in enumerate(later):
+            for i in range(8):
+                tiles[t] = tiles[t] - c[i][x] * scaled[i]
+    return pltpu.roll(v_ref[...], 64, 1)[:, 0:64]
+
+
+def basis_body(scale, r_ref, loc_ref, suf_ref, entry_ref, out_ref, f_ref, v_ref):
     n, cols, _ = loc_ref.shape
     for k in range(n):
         e = entry_ref[:, 80 + k : 81 + k]
@@ -226,21 +310,15 @@
     packed = r_ref[0]
     for i in range(1, r_ref.shape[0]):
         packed = packed + r_ref[i]
-    low = pltpu.roll(packed, 64, 1)
-    lane, row = lane_ids(cols), row_ids(cols)
-    m = jnp.concatenate([packed, low], axis=0)
-    m = jnp.where(lane < 64, m, jnp.where(lane - 64 == row, 1.0, 0.0))
-    diag = jnp.zeros((cols, LANES), F32)
-    for j in range(cols):
-        col = jnp.broadcast_to(m[:, j : j + 1], (cols, LANES))
-        pivot = jnp.broadcast_to(col[j : j + 1, :], (cols, LANES))
-        diag = jnp.where(row == j, pivot, diag)
-        factor = jnp.where(row > j, col / pivot, 0.0)
-        m = m - factor * m[j : j + 1, :]
-    inv = pltpu.roll(m * (scale / jnp.sqrt(diag)), 64, 1)[:, 0:64]
+    unpacked = jnp.concatenate([packed, pltpu.roll(packed, 64, 1)], axis=0)
+    inv = inverse_factor(scale, unpacked, v_ref)
     out = jnp.dot(inv, f_ref[...], precision=HIGH, preferred_element_type=F32)
     for k in range(n):
         out_ref[k] = out[:, k * LANES : (k + 1) * LANES]
+
+
+def in_hbm(value):
+    return pltpu.with_memory_space_constraint(value, pltpu.HBM)
 
 
 def exchange(value, axis):
@@ -253,31 +331,35 @@
     stations = lax.axis_size("z") * lax.axis_size("y") * lax.axis_size("core")
     rows = n * stations * pts * peers
     field = (n, cols, pts)
-    f = forcing.reshape(field)
-    b = block_inverse.reshape(n * n, pts)
-    w = wall_rates.reshape(2 * n, pts)
+    f, b, w, c = map(in_hbm, (forcing.reshape(field), block_inverse, wall_rates, span_couple))
     across = [(i, (i + 1) % stations if i % 2 else (i - 1) % stations) for i in range(stations)]
     work = 2 * n * n * cols * pts
     scratch = pltpu.VMEM(field, F32)
 
-    start = call(start_body, field, work)(f, b)
+    start, b, w = call(
+        start_body, [field, b.shape, w.shape], work, [scratch, pltpu.SemaphoreType.DMA((3,))], HBM
+    )(f, b, w)
     far = lax.ppermute(start, TILE, across)
     near = lax.all_gather(start, "core")
     steps = (len(STEPS), 16, pts)
-    up, down, pre, suf, row, ext = call(
-        rates_body, [steps, steps, (16, pts), (16, pts), (8, pts), (64, n * pts)], work // 8
-    )(w)
-    loc, pay = call(up_body, [field, (peers, 24, pts)], 2 * work, [scratch])(
-        span_couple, b, w, start, far, near, up, row
+    wide = pltpu.VMEM((cols, n * pts), F32)
+    cb, base, edge, up, down, pre, suf, row, ext = call(
+        side_body,
+        [(n * n, pts), field, (cols, 32), steps, steps, (16, pts), (16, pts), (8, pts), (64, n * pts)],
+        work // 4,
+        [wide],
+    )(c, b, w, start)
+    loc, pay = call(up_body, [field, (peers, 24, pts)], 2 * work, [scratch, wide])(
+        cb, base, far, near, up, edge, row
     )
     got = exchange(pay, "line")
-    rising, edge = call(enter_body, [field, (16, pts)], work // 4)(got, loc, pre, w)
+    rising, edge = call(enter_body, [field, (16, pts)], work // 4)(got, loc, pre)
     far = lax.ppermute(rising, TILE, across)
     near = lax.all_gather(rising, "core")
     base = call(below_body, field, work // 4)(start, rising, edge, w)
-    wide = pltpu.VMEM((2 * cols, n * pts), F32)
-    loc, pay = call(down_body, [field, (peers, cols, pts)], 4 * work, [scratch, wide])(
-        span_couple, b, base, far, near, down, ext
+    tall = pltpu.VMEM((2 * cols, n * pts), F32)
+    loc, pay = call(down_body, [field, (peers, cols, pts)], 4 * work, [scratch, tall])(
+        cb, base, far, near, down, ext
     )
     sums = exchange(pay, "line")
     gram, entry = call(line_body, [(cols // 2, pts), (cols, pts)], work // 4)(sums, got)
@@ -290,7 +372,9 @@
     def basis(*refs):
         basis_body(math.sqrt(rows), *refs)
 
-    out = call(basis, field, 4 * work, [pltpu.VMEM((cols, n * pts), F32)])(gram, loc, suf, entry)
+    out = call(basis, field, 4 * work, [wide, pltpu.VMEM((cols, pts), F32)])(
+        gram, loc, suf, entry
+    )
     return out.reshape(n, cols, 1, pts)
 
 

time: 118 us -> 81.6 us (0.69)
  Pallas kernels: 36.3 us -> 9.6 us
  blocking collectives: 70.5 us -> 64.1 us
  local copies, waits for them, and re-layouts: 2.7 us -> 0 us
    pallas_call x10, Pallas kernels: 36.3 us -> 9.6 us  [run(): pl.pallas_call(body, out_shape=shapes if many else shapes[0], in_specs=[S...]
    all_to_all x4, blocking collectives: 41.9 us -> 37.3 us  [exchange(): return lax.all_to_all(value, axis, 0, 0, tiled=True)]
    all_gather x1, blocking collectives: 4.06 us -> 8.18 us  [local(): near = lax.all_gather(rising, 'core')]
    all_gather x1, blocking collectives: 15.5 us -> 12.1 us  [local(): near = lax.all_gather(start, 'core')]
    all_gather x1, blocking collectives: 9 us -> 6.52 us  [local(): both = lax.all_gather(gram, 'core')]
    unnamed x8 -> x0, local copies, waits for them, and re-layouts: 1.47 us -> none
    reshape x2 -> x0, local copies, waits for them, and re-layouts: 1.23 us -> none  [the longest x1 0.63 us: local(): b = block_inverse.reshape(n * n, pts)]
  transfers between devices with their start and end apart: 2 -> 2, of which waited for: 1 -> 0; matrix products, arithmetic and copies ran while one was open for 1% -> 0% of each run, Pallas kernels for 4% -> 2%
where the time goes in v2:
time: 81.6 us; the launch traced here: 80.3 us
  blocking collectives  64.1 us (79%)
  Pallas kernels  9.6 us (12%)
  starting transfers between devices  6.5 us (8%)
    all_to_all x4, blocking collectives, exchange(): return lax.all_to_all(value, axis, 0, 0, tiled=True)  37.3 us
    all_gather x1, blocking collectives, local(): near = lax.all_gather(start, 'core')  12.1 us
    pallas_call x10, Pallas kernels, run(): pl.pallas_call(body, out_shape=shapes if many else shapes[0], in_specs=[S...  9.6 us
    all_gather x1, blocking collectives, local(): near = lax.all_gather(rising, 'core')  8.18 us
    all_gather x1, blocking collectives, local(): both = lax.all_gather(gram, 'core')  6.52 us
    ppermute x1, starting transfers between devices, local(): far = lax.ppermute(start, TILE, across)  4.58 us
    ppermute x1, starting transfers between devices, local(): far = lax.ppermute(rising, TILE, across)  1.92 us
  transfers between devices with their start and end apart: 2, of which 0 were waited for; matrix products, arithmetic and copies ran while one was open for 0% of the time, Pallas kernels for 2%

profile of v2, /device:TPU:1, one launch (start us, length us, event | category | flops | bytes accessed | tf_op | source)
XLA Modules:
  0.0 80.3 jit_solution(11533200625618539008)
XLA Ops:
  0.0 1.2 %shard_map.46 = (f32[10,64,128]{2,1,0:T(8,128)S(1)}, f32[10,10,1,128]{3,2,1,0:T(1,128)S(1)}, f32[2,10,1,128]{3,2,1,0:T(1,128)S(1)}) custom-call(f32[10,64,128]{2,1,0:T(8,128)} %bitcast.10, f32[10,10,1,128]{3,2,1,0:T(1,128)} %b_hbm.1, f32[2,10,1,128]{3,2,1,0:T(1,128)} %w_hbm.1), custom_call_target="tpu_custom_call" | custom-call | flops 1638400 | bytes 778240 | tf_op jit(solution)/shard_map/pallas_call | solution.py:42
  1.2 4.6 %collective-permute-start = (f32[10,64,128]{2,1,0:T(8,128)S(1)}, f32[10,64,128]{2,1,0:T(8,128)S(1)}, u32[]{:S(2)}, u32[]{:S(2)}) collective-permute-start(f32[10,64,128]{2,1,0:T(8,128)S(1)} %get-tuple-element.27.s_ref), channel_id=1, source_target_pairs={{0,127},{1,2},{2,1},{3,4},{4,3},{5,6},{6,5},{7,8},{8,7},{9,10},{10... | collective-permute-start | bytes 983048 | tf_op jit(solution)/shard_map/ppermute | solution.py:342
  5.8 1.6 %shard_map.47 = (f32[100,128]{1,0:T(8,128)S(1)}, f32[10,64,128]{2,1,0:T(8,128)S(1)}, f32[64,32]{1,0:T(8,128)S(1)}, f32[7,16,128]{2,1,0:T(8,128)S(1)}, f32[7,16,1...) custom-call(f32[10]{0:T(128)} %c_ref.1, ...), custom_call_target="tpu_custom_call" | custom-call | flops 409600 | bytes 1239080 | tf_op jit(solution)/shard_map/pallas_call | solution.py:42
  7.4 12.1 %all-gather = f32[20,64,128]{2,1,0:T(8,128)S(1)} all-gather(f32[10,64,128]{2,1,0:T(8,128)S(1)} %get-tuple-element.27.s_ref), channel_id=2, replica_groups=mesh['line'=4,'z'=8,'y'=8,'core'=2] {'core'}, dimensions={0}, use_global_device_ids=true | all-gather | bytes 983040 | tf_op jit(solution)/shard_map/all_gather | solution.py:343
  19.5 0.0 collective-permute-done.n_ref
  19.5 1.1 %shard_map.48 = (f32[10,64,128]{2,1,0:T(8,128)S(1)}, f32[4,24,128]{2,1,0:T(8,128)S(1)}) custom-call(f32[100,128]{1,0:T(8,128)S(1)} %get-tuple-element.28.cb_ref, f32[10,64,128]{2,1,0:T(8,128)S(1)} %get-tuple-element.29.base_ref, f32[10,64,128]{2,1,0:T(8,128)S(1)} %collective-permute-done.n_ref, f32[2,10,64,128]{3,2,1,0:T(8,128)S(1)} %bitcast.8, ...), custom_call_target="tpu_custom_call" | custom-call | flops 3276800 | bytes 1808384 | tf_op jit(solution)/shard_map/pallas_call | solution.py:42
  20.7 8.2 %all_to_all.20.r_ref.q_ref = f32[4,24,128]{2,1,0:T(8,128)S(1)} all-to-all(f32[4,24,128]{2,1,0:T(8,128)S(1)} %get-tuple-element.33), channel_id=1, replica_groups=mesh['line'=4,'z'=8,'y'=8,'core'=2] {'line'}, dimensions={0} | all-to-all | bytes 98304 | tf_op jit(solution)/shard_map/all_to_all | solution.py:325
  28.9 0.4 shard_map.49
  29.2 1.9 %collective-permute-start.1 = (f32[10,64,128]{2,1,0:T(8,128)S(1)}, f32[10,64,128]{2,1,0:T(8,128)S(1)}, u32[]{:S(2)}, u32[]{:S(2)}) collective-permute-start(f32[10,64,128]{2,1,0:T(8,128)S(1)} %get-tuple-element.36.up_ref), channel_id=1, source_target_pairs={{0,127},{1,2},{2,1},{3,4},{4,3},{5,6},{6,5},{7,8},{8,7},{9,10},{10... | collective-permute-start | bytes 983048 | tf_op jit(solution)/shard_map/ppermute | solution.py:357
  31.2 0.4 shard_map.50.base_ref
  31.5 8.2 %all-gather.1 = f32[20,64,128]{2,1,0:T(8,128)S(1)} all-gather(f32[10,64,128]{2,1,0:T(8,128)S(1)} %get-tuple-element.36.up_ref), channel_id=3, replica_groups=mesh['line'=4,'z'=8,'y'=8,'core'=2] {'core'}, dimensions={0}, use_global_device_ids=true | all-gather | bytes 983040 | tf_op jit(solution)/shard_map/all_gather | solution.py:358
  39.7 0.0 collective-permute-done.1.n_ref
  39.7 1.6 %shard_map.51 = (f32[10,64,128]{2,1,0:T(8,128)S(1)}, f32[4,64,128]{2,1,0:T(8,128)S(1)}) custom-call(f32[100,128]{1,0:T(8,128)S(1)} %get-tuple-element.28.cb_ref, f32[10,64,128]{2,1,0:T(8,128)S(1)} %shard_map.50.base_ref, f32[10,64,128]{2,1,0:T(8,128)S(1)} %collective-permute-done.1.n_ref, f32[2,10,64,128]{3,2,1,0:T(8,128)S(1)} %bitcast.7, ...), custom_call_target="tpu_custom_call" | custom-call | flops 6553600 | bytes 2205696 | tf_op jit(solution)/shard_map/pallas_call | solution.py:42
  41.4 7.2 %all_to_all.21.r_ref = f32[4,64,128]{2,1,0:T(8,128)S(1)} all-to-all(f32[4,64,128]{2,1,0:T(8,128)S(1)} %get-tuple-element.40), channel_id=1, replica_groups=mesh['line'=4,'z'=8,'y'=8,'core'=2] {'line'}, dimensions={0} | all-to-all | bytes 262144 | tf_op jit(solution)/shard_map/all_to_all | solution.py:325
  48.6 0.5 shard_map.52
  49.1 6.5 %all-gather.2 = f32[64,128]{1,0:T(8,128)S(1)} all-gather(f32[32,128]{1,0:T(8,128)S(1)} %get-tuple-element.41), channel_id=4, replica_groups=mesh['line'=4,'z'=8,'y'=8,'core'=2] {'core'}, dimensions={0}, use_global_device_ids=true | all-gather | bytes 49152 | tf_op jit(solution)/shard_map/all_gather | solution.py:367
  55.6 10.8 %all_to_all.22.r_ref = f32[8,32,128]{2,1,0:T(8,128)S(1)} all-to-all(f32[8,32,128]{2,1,0:T(8,128)S(1)} %shard_map.53), channel_id=1, replica_groups=mesh['line'=4,'z'=8,'y'=8,'core'=2] {'y'}, dimensions={0} | all-to-all | bytes 262144 | tf_op jit(solution)/shard_map/all_to_all | solution.py:325
  66.4 11.1 %all_to_all.23.refs_0_ = f32[8,32,128]{2,1,0:T(8,128)S(1)} all-to-all(f32[8,32,128]{2,1,0:T(8,128)S(1)} %shard_map.54), channel_id=1, replica_groups=mesh['line'=4,'z'=8,'y'=8,'core'=2] {'z'}, dimensions={0} | all-to-all | bytes 262144 | tf_op jit(solution)/shard_map/all_to_all | solution.py:325
  77.5 2.8 %shard_map.55 = f32[10,64,128]{2,1,0:T(8,128)} custom-call(f32[8,32,128]{2,1,0:T(8,128)S(1)} %all_to_all.23.refs_0_, f32[10,64,128]{2,1,0:T(8,128)S(1)} %get-tuple-element.42.refs_1_, f32[16,128]{1,0:T(8,128)S(1)} %get-tuple-element.43.refs_2_, f32[64,128]{1,0:T(8,128)S(1)} %get-tuple-element.44.refs_3_), custom_call_target="tpu_custom_call" | custom-call | flops 6553600 | bytes 827392 | tf_op jit(solution)/shard_map/pallas_call | solution.py:42
  (2 shorter events, 0.0 us)
Async XLA Ops:
  1.2 18.3 %collective-permute-start = (f32[10,64,128]{2,1,0:T(8,128)S(1)}, f32[10,64,128]{2,1,0:T(8,128)S(1)}, u32[]{:S(2)}, u32[]{:S(2)}) collective-permute-start(f32[10,64,128]{2,1,0:T(8,128)S(1)} %get-tuple-element.27.s_ref), channel_id=1, source_target_pairs={{0,127},{1,2},{2,1},{3,4},{4,3},{5,6},{6,5},{7,8},{8,7},{9,10},{10... | collective-permute-start | bytes 983048 | tf_op jit(solution)/shard_map/ppermute | solution.py:342
  29.2 10.5 %collective-permute-start.1 = (f32[10,64,128]{2,1,0:T(8,128)S(1)}, f32[10,64,128]{2,1,0:T(8,128)S(1)}, u32[]{:S(2)}, u32[]{:S(2)}) collective-permute-start(f32[10,64,128]{2,1,0:T(8,128)S(1)} %get-tuple-element.36.up_ref), channel_id=1, source_target_pairs={{0,127},{1,2},{2,1},{3,4},{4,3},{5,6},{6,5},{7,8},{8,7},{9,10},{10... | collective-permute-start | bytes 983048 | tf_op jit(solution)/shard_map/ppermute | solution.py:357

commit v3 on v2

--- a/solution.py
+++ b/solution.py
@@ -215,7 +215,9 @@
             out_ref[k, rows, :] = s_ref[k, rows, :] + rise * below
 
 
-def down_body(cb_ref, base_ref, n_ref, g_ref, down_ref, ext_ref, loc_ref, pay_ref, h_ref, a_ref):
+def down_body(
+    cb_ref, base_ref, n_ref, g_ref, down_ref, ext_ref, row_ref, loc_ref, pay_ref, h_ref, a_ref
+):
     n, cols, _ = base_ref.shape
     neighbours_into(h_ref, n_ref, g_ref)
     for k in range(n):
@@ -228,32 +230,56 @@
             a_ref[rows, k * LANES : (k + 1) * LANES] = v
     a_ref[cols : 2 * cols, :] = ext_ref[...]
     total = dot_nt(a_ref[0:cols, :], a_ref[...])
+    lane = lane_ids(16)
+    edges = jnp.zeros((16, LANES), F32)
+    for g in range(cols // 16):
+        moved = pltpu.roll(total[16 * g : 16 * g + 16, :], (32 * g + 64) % LANES, 1)
+        edges = jnp.where(lane // 32 == g, moved, edges)
+    half = cols // 2
     for peer in range(pay_ref.shape[0]):
-        pay_ref[peer] = total
-
-
-def line_body(r_ref, q_ref, gram_ref, entry_ref):
-    peers, cols, _ = r_ref.shape
-    mine = lax.axis_index("line")
-    lane = lane_ids(cols)
-    state = jnp.zeros((cols, LANES), F32)
-    entry = state
-    left = state
-    total = r_ref[peers - 1]
-    for at in range(peers - 2, -1, -1):
-        state = q_ref[at + 1, 18:19, :] * state + r_ref[at + 1]
-        entry = jnp.where(mine == at, state, entry)
-        total = total + r_ref[at]
-        cross = r_ref[at] + (0.5 * q_ref[at, 19:20, :]) * pltpu.roll(state, LANES - 16, 1)
-        here = (lane >= 16 * at) & (lane < 16 * at + 10)
-        left = jnp.where(here, pltpu.roll(cross, (LANES + 16 * at - 64) % LANES, 1), left)
-        here = (lane >= 64 + 16 * at) & (lane < 64 + 16 * at + 10)
-        left = jnp.where(here, pltpu.roll(state, (LANES + 16 * at - 16) % LANES, 1), left)
-    fix = dot_nt(left, pltpu.roll(left, 64, 1))
+        at = half * (peer % NCORE)
+        low = pltpu.roll(total[at + 16 : at + 32, :], 64, 1)
+        pay_ref[peer, 0:16, :] = jnp.where(lane < 64, total[at : at + 16, :], low)
+        pay_ref[peer, 16:32, :] = edges
+        pay_ref[peer, 32:40, :] = row_ref[...]
+
+
+def line_body(r_ref, gram_ref, entry_ref, left_ref, right_ref):
+    peers = r_ref.shape[0] // NCORE
+    cols = left_ref.shape[0]
+    mine, core = lax.axis_index("line"), lax.axis_index("core")
+    lane = lane_ids(16)
+    first = lane % 32 < 16
+    zero = jnp.zeros((16, LANES), F32)
+    entry = zero
+    for station in range(NCORE):
+        state = zero
+        left = [zero] * (cols // 16)
+        right = [zero] * (cols // 16)
+        for at in range(peers - 2, -1, -1):
+            above, here = NCORE * (at + 1) + station, NCORE * at + station
+            state = r_ref[above, 34:35, :] * state + r_ref[above, 16:32, :]
+            entry = jnp.where((mine == at) & (core == station), state, entry)
+            back = pltpu.roll(state, LANES - 16, 1)
+            cross = r_ref[here, 16:32, :] + (0.5 * r_ref[here, 35:36, :]) * back
+            a = jnp.where(first, cross, state)
+            b = jnp.where(first, back, pltpu.roll(cross, 16, 1))
+            for g in range(cols // 16):
+                shift = (32 * (at - g)) % LANES
+                left[g] = jnp.where(lane // 32 == at, pltpu.roll(a, shift, 1), left[g])
+                right[g] = jnp.where(lane // 32 == at, pltpu.roll(b, shift, 1), right[g])
+        for g in range(cols // 16):
+            rows = slice(16 * g, 16 * g + 16)
+            left_ref[rows, station * LANES : (station + 1) * LANES] = left[g]
+            right_ref[rows, station * LANES : (station + 1) * LANES] = right[g]
     half = cols // 2
-    gram = total[:, 0:64] + fix
-    gram_ref[:, 0:64] = gram[0:half, :]
-    gram_ref[:, 64:128] = gram[half:cols, :]
+    mine = left_ref[pl.ds(pl.multiple_of(half * core, half), half), :]
+    fix = dot_nt(mine, right_ref[...])
+    total = jnp.concatenate([fix[0:16, :], fix[16:32, :]], axis=1)
+    for i in range(r_ref.shape[0]):
+        total = total + r_ref[i, 0:16, :]
+    for peer in range(gram_ref.shape[0]):
+        gram_ref[peer] = total
     entry_ref[...] = entry
 
 
@@ -305,12 +331,18 @@
 def basis_body(scale, r_ref, loc_ref, suf_ref, entry_ref, out_ref, f_ref, v_ref):
     n, cols, _ = loc_ref.shape
     for k in range(n):
-        e = entry_ref[:, 80 + k : 81 + k]
-        f_ref[:, k * LANES : (k + 1) * LANES] = loc_ref[k] + suf_ref[k : k + 1, :] * e
-    packed = r_ref[0]
-    for i in range(1, r_ref.shape[0]):
-        packed = packed + r_ref[i]
-    unpacked = jnp.concatenate([packed, pltpu.roll(packed, 64, 1)], axis=0)
+        suf = suf_ref[k : k + 1, :]
+        for g in range(cols // 16):
+            rows, at = slice(16 * g, 16 * g + 16), 32 * g + 16 + k
+            v = loc_ref[k, rows, :] + suf * entry_ref[:, at : at + 1]
+            f_ref[rows, k * LANES : (k + 1) * LANES] = v
+    parts = []
+    for core in range(NCORE):
+        packed = r_ref[core]
+        for i in range(NCORE + core, r_ref.shape[0], NCORE):
+            packed = packed + r_ref[i]
+        parts += [packed, pltpu.roll(packed, 64, 1)]
+    unpacked = jnp.concatenate(parts, axis=0)
     inv = inverse_factor(scale, unpacked, v_ref)
     out = jnp.dot(inv, f_ref[...], precision=HIGH, preferred_element_type=F32)
     for k in range(n):
@@ -358,16 +390,16 @@
     near = lax.all_gather(rising, "core")
     base = call(below_body, field, work // 4)(start, rising, edge, w)
     tall = pltpu.VMEM((2 * cols, n * pts), F32)
-    loc, pay = call(down_body, [field, (peers, cols, pts)], 4 * work, [scratch, tall])(
-        cb, base, far, near, down, ext
-    )
-    sums = exchange(pay, "line")
-    gram, entry = call(line_body, [(cols // 2, pts), (cols, pts)], work // 4)(sums, got)
-    half = (cols // 2, pts)
-    both = lax.all_gather(gram, "core")
-    gram = call(sum_body, (NY,) + half)(both)
-    gram = call(sum_body, (NZ,) + half)(exchange(gram, "y"))
-    gram = exchange(gram, "z")
+    loc, pay = call(down_body, [field, (peers * NCORE, 40, pts)], 4 * work, [scratch, tall])(
+        cb, base, far, near, down, ext, row
+    )
+    side = pltpu.VMEM((cols, NCORE * pts), F32)
+    part = (cols // 4, pts)
+    gram, entry = call(line_body, [(NY,) + part, (16, pts)], work // 4, [side, side])(
+        exchange(pay, ("line", "core"))
+    )
+    gram = call(sum_body, (NZ * NCORE,) + part)(exchange(gram, "y"))
+    gram = exchange(gram, ("z", "core"))
 
     def basis(*refs):
         basis_body(math.sqrt(rows), *refs)

time: 81.6 us -> 81.5 us (level); the launches traced: 80.3 us -> 81.1 us
  blocking collectives: 64.1 us -> 65 us
    all_to_all x4, blocking collectives: 37.3 us -> 44.7 us  [exchange(): return lax.all_to_all(value, axis, 0, 0, tiled=True)]
    all_gather x1 -> x0, blocking collectives: 6.52 us -> none  [local(): both = lax.all_gather(gram, 'core')]
    pallas_call x10 -> x9, Pallas kernels: 9.6 us -> 9.58 us  [run(): pl.pallas_call(body, out_shape=shapes if many else shapes[0], in_specs=[S...]
where the time goes in v3:
time: 81.5 us; the launch traced here: 81.1 us
  blocking collectives  65 us (80%)
  Pallas kernels  9.58 us (12%)
  starting transfers between devices  6.5 us (8%)
    all_to_all x4, blocking collectives, exchange(): return lax.all_to_all(value, axis, 0, 0, tiled=True)  44.7 us
    all_gather x1, blocking collectives, local(): near = lax.all_gather(start, 'core')  12.1 us
    pallas_call x9, Pallas kernels, run(): pl.pallas_call(body, out_shape=shapes if many else shapes[0], in_specs=[S...  9.58 us
    all_gather x1, blocking collectives, local(): near = lax.all_gather(rising, 'core')  8.18 us
    ppermute x1, starting transfers between devices, local(): far = lax.ppermute(start, TILE, across)  4.58 us
    ppermute x1, starting transfers between devices, local(): far = lax.ppermute(rising, TILE, across)  1.92 us
  transfers between devices with their start and end apart: 2, of which 0 were waited for; matrix products, arithmetic and copies ran while one was open for 0% of the time, Pallas kernels for 2%

profile of v3, /device:TPU:1, one launch (start us, length us, event | category | flops | bytes accessed | tf_op | source)
XLA Modules:
  0.0 81.1 jit_solution(478478287872845132)
XLA Ops:
  0.0 1.2 %shard_map.46 = (f32[10,64,128]{2,1,0:T(8,128)S(1)}, f32[10,10,1,128]{3,2,1,0:T(1,128)S(1)}, f32[2,10,1,128]{3,2,1,0:T(1,128)S(1)}) custom-call(f32[10,64,128]{2,1,0:T(8,128)} %bitcast.8, f32[10,10,1,128]{3,2,1,0:T(1,128)} %b_hbm.1, f32[2,10,1,128]{3,2,1,0:T(1,128)} %w_hbm.1), custom_call_target="tpu_custom_call" | custom-call | flops 1638400 | bytes 778240 | tf_op jit(solution)/shard_map/pallas_call | solution.py:42
  1.2 4.6 %collective-permute-start = (f32[10,64,128]{2,1,0:T(8,128)S(1)}, f32[10,64,128]{2,1,0:T(8,128)S(1)}, u32[]{:S(2)}, u32[]{:S(2)}) collective-permute-start(f32[10,64,128]{2,1,0:T(8,128)S(1)} %get-tuple-element.27.s_ref), channel_id=1, source_target_pairs={{0,127},{1,2},{2,1},{3,4},{4,3},{5,6},{6,5},{7,8},{8,7},{9,10},{10... | collective-permute-start | bytes 983048 | tf_op jit(solution)/shard_map/ppermute | solution.py:374
  5.8 1.6 %shard_map.47 = (f32[100,128]{1,0:T(8,128)S(1)}, f32[10,64,128]{2,1,0:T(8,128)S(1)}, f32[64,32]{1,0:T(8,128)S(1)}, f32[7,16,128]{2,1,0:T(8,128)S(1)}, f32[7,16,1...) custom-call(f32[10]{0:T(128)} %c_ref.1, ...), custom_call_target="tpu_custom_call" | custom-call | flops 409600 | bytes 1239080 | tf_op jit(solution)/shard_map/pallas_call | solution.py:42
  7.4 12.1 %all-gather = f32[20,64,128]{2,1,0:T(8,128)S(1)} all-gather(f32[10,64,128]{2,1,0:T(8,128)S(1)} %get-tuple-element.27.s_ref), channel_id=2, replica_groups=mesh['line'=4,'z'=8,'y'=8,'core'=2] {'core'}, dimensions={0}, use_global_device_ids=true | all-gather | bytes 983040 | tf_op jit(solution)/shard_map/all_gather | solution.py:375
  19.5 0.0 collective-permute-done.n_ref
  19.5 1.1 %shard_map.48 = (f32[10,64,128]{2,1,0:T(8,128)S(1)}, f32[4,24,128]{2,1,0:T(8,128)S(1)}) custom-call(f32[100,128]{1,0:T(8,128)S(1)} %get-tuple-element.28.cb_ref, f32[10,64,128]{2,1,0:T(8,128)S(1)} %get-tuple-element.29.base_ref, f32[10,64,128]{2,1,0:T(8,128)S(1)} %collective-permute-done.n_ref, f32[2,10,64,128]{3,2,1,0:T(8,128)S(1)} %bitcast.7, ...), custom_call_target="tpu_custom_call" | custom-call | flops 3276800 | bytes 1808384 | tf_op jit(solution)/shard_map/pallas_call | solution.py:42
  20.6 8.2 %all_to_all.20.r_ref = f32[4,24,128]{2,1,0:T(8,128)S(1)} all-to-all(f32[4,24,128]{2,1,0:T(8,128)S(1)} %get-tuple-element.33), channel_id=1, replica_groups=mesh['line'=4,'z'=8,'y'=8,'core'=2] {'line'}, dimensions={0} | all-to-all | bytes 98304 | tf_op jit(solution)/shard_map/all_to_all | solution.py:357
  28.8 0.4 shard_map.49
  29.2 1.9 %collective-permute-start.1 = (f32[10,64,128]{2,1,0:T(8,128)S(1)}, f32[10,64,128]{2,1,0:T(8,128)S(1)}, u32[]{:S(2)}, u32[]{:S(2)}) collective-permute-start(f32[10,64,128]{2,1,0:T(8,128)S(1)} %get-tuple-element.36.up_ref), channel_id=1, source_target_pairs={{0,127},{1,2},{2,1},{3,4},{4,3},{5,6},{6,5},{7,8},{8,7},{9,10},{10... | collective-permute-start | bytes 983048 | tf_op jit(solution)/shard_map/ppermute | solution.py:389
  31.1 0.4 shard_map.50.base_ref
  31.5 8.2 %all-gather.1 = f32[20,64,128]{2,1,0:T(8,128)S(1)} all-gather(f32[10,64,128]{2,1,0:T(8,128)S(1)} %get-tuple-element.36.up_ref), channel_id=3, replica_groups=mesh['line'=4,'z'=8,'y'=8,'core'=2] {'core'}, dimensions={0}, use_global_device_ids=true | all-gather | bytes 983040 | tf_op jit(solution)/shard_map/all_gather | solution.py:390
  39.7 0.0 collective-permute-done.1.n_ref
  39.7 1.7 %shard_map.51 = (f32[10,64,128]{2,1,0:T(8,128)S(1)}, f32[8,40,128]{2,1,0:T(8,128)S(1)}) custom-call(f32[100,128]{1,0:T(8,128)S(1)} %get-tuple-element.28.cb_ref, f32[10,64,128]{2,1,0:T(8,128)S(1)} %shard_map.50.base_ref, f32[10,64,128]{2,1,0:T(8,128)S(1)} %collective-permute-done.1.n_ref, f32[2,10,64,128]{3,2,1,0:T(8,128)S(1)} %bitcast.6, ...), custom_call_target="tpu_custom_call" | custom-call | flops 6553600 | bytes 2242560 | tf_op jit(solution)/shard_map/pallas_call | solution.py:42
  41.4 11.8 %all_to_all.21.r_ref = f32[8,40,128]{2,1,0:T(8,128)S(1)} all-to-all(f32[8,40,128]{2,1,0:T(8,128)S(1)} %get-tuple-element.40), channel_id=1, replica_groups=mesh['line'=4,'z'=8,'y'=8,'core'=2] {'line','core'}, dimensions={0} | all-to-all | bytes 327680 | tf_op jit(solution)/shard_map/all_to_all | solution.py:357
  53.2 0.5 shard_map.52
  53.7 9.7 %all_to_all.22.r_ref = f32[8,16,128]{2,1,0:T(8,128)S(1)} all-to-all(f32[8,16,128]{2,1,0:T(8,128)S(1)} %get-tuple-element.41), channel_id=1, replica_groups=mesh['line'=4,'z'=8,'y'=8,'core'=2] {'y'}, dimensions={0} | all-to-all | bytes 131072 | tf_op jit(solution)/shard_map/all_to_all | solution.py:357
  63.4 14.9 %all_to_all.23.refs_0_ = f32[16,16,128]{2,1,0:T(8,128)S(1)} all-to-all(f32[16,16,128]{2,1,0:T(8,128)S(1)} %shard_map.53), channel_id=1, replica_groups=mesh['line'=4,'z'=8,'y'=8,'core'=2] {'z','core'}, dimensions={0} | all-to-all | bytes 262144 | tf_op jit(solution)/shard_map/all_to_all | solution.py:357
  78.4 2.7 %shard_map.54 = f32[10,64,128]{2,1,0:T(8,128)} custom-call(f32[16,16,128]{2,1,0:T(8,128)S(1)} %all_to_all.23.refs_0_, f32[10,64,128]{2,1,0:T(8,128)S(1)} %get-tuple-element.42.refs_1_, f32[16,128]{1,0:T(8,128)S(1)} %get-tuple-element.43.refs_2_, f32[16,128]{1,0:T(8,128)S(1)} %get-tuple-element.44.refs_3_), custom_call_target="tpu_custom_call" | custom-call | flops 6553600 | bytes 802816 | tf_op jit(solution)/shard_map/pallas_call | solution.py:42
  (1 shorter events, 0.0 us)
Async XLA Ops:
  1.2 18.3 %collective-permute-start = (f32[10,64,128]{2,1,0:T(8,128)S(1)}, f32[10,64,128]{2,1,0:T(8,128)S(1)}, u32[]{:S(2)}, u32[]{:S(2)}) collective-permute-start(f32[10,64,128]{2,1,0:T(8,128)S(1)} %get-tuple-element.27.s_ref), channel_id=1, source_target_pairs={{0,127},{1,2},{2,1},{3,4},{4,3},{5,6},{6,5},{7,8},{8,7},{9,10},{10... | collective-permute-start | bytes 983048 | tf_op jit(solution)/shard_map/ppermute | solution.py:374
  29.2 10.5 %collective-permute-start.1 = (f32[10,64,128]{2,1,0:T(8,128)S(1)}, f32[10,64,128]{2,1,0:T(8,128)S(1)}, u32[]{:S(2)}, u32[]{:S(2)}) collective-permute-start(f32[10,64,128]{2,1,0:T(8,128)S(1)} %get-tuple-element.36.up_ref), channel_id=1, source_target_pairs={{0,127},{1,2},{2,1},{3,4},{4,3},{5,6},{6,5},{7,8},{8,7},{9,10},{10... | collective-permute-start | bytes 983048 | tf_op jit(solution)/shard_map/ppermute | solution.py:389

commit v4 on v3

--- a/solution.py
+++ b/solution.py
@@ -80,7 +80,7 @@
     return (col == (row - shift) * LANES + at).astype(jnp.bfloat16)
 
 
-def start_body(f_hbm, b_hbm, w_hbm, s_ref, b_ref, w_ref, f_ref, sems):
+def start_body(f_hbm, b_hbm, w_hbm, s_ref, pack_ref, f_ref, b_ref, w_ref, sems):
     copies = [
         pltpu.make_async_copy(src, dst, sems.at[i])
         for i, (src, dst) in enumerate(((f_hbm, f_ref), (b_hbm, b_ref), (w_hbm, w_ref)))
@@ -93,28 +93,33 @@
     for g in range(0, cols, 16):
         vals = [f_ref[m, g : g + 16, :] for m in range(n)]
         for k in range(n):
-            s_ref[k, g : g + 16, :] = apply_rows(lambda m: b_ref[k, m], n, lambda m: vals[m])
-
-
-def side_body(
-    c_ref, b_ref, w_ref, s_ref,
-    cb_ref, base_ref, edge_ref, up_ref, down_ref, pre_ref, suf_ref, row_ref, ext_ref, a_ref,
-):
-    n = w_ref.shape[1]
+            v = apply_rows(lambda m: b_ref[k, m], n, lambda m: vals[m])
+            s_ref[k * cols + g : k * cols + g + 16, :] = v
+            pack_ref[k * cols + g : k * cols + g + 16, :] = v
+    at = n * cols
+    for k in range(n):
+        for m in range(n):
+            pack_ref[at + k * n + m : at + k * n + m + 1, :] = b_ref[k, m]
+    at += n * n
+    for i in range(2):
+        for k in range(n):
+            pack_ref[at + i * n + k : at + i * n + k + 1, :] = w_ref[i, k]
+
+
+def rate_tables(up, down):
+    n = up.shape[0]
     lane = lane_ids(n)
-    up, down = (jnp.concatenate([w_ref[i, k] for k in range(n)], axis=0) for i in range(2))
     pre, suf = up, down
     p = jnp.where(lane >= 1, up, 0.0)
     q = jnp.where(lane < LANES - 1, down, 0.0)
-    for i, d in enumerate(STEPS):
-        up_ref[i, 0:n, :] = p
-        down_ref[i, 0:n, :] = q
+    ps, qs = [], []
+    for d in STEPS:
+        ps.append(p)
+        qs.append(q)
         p = p * pltpu.roll(p, d, 1)
         q = q * pltpu.roll(q, LANES - d, 1)
         pre = jnp.where(lane >= d, pre * pltpu.roll(pre, d, 1), pre)
         suf = jnp.where(lane < LANES - d, suf * pltpu.roll(suf, LANES - d, 1), suf)
-    pre_ref[0:n, :] = pre
-    suf_ref[0:n, :] = suf
     norm = jnp.sum(suf * suf, axis=1, keepdims=True)
     table = jnp.zeros((8, LANES), F32)
     at, row = lane_ids(8), row_ids(8)
@@ -124,7 +129,35 @@
         mine = jnp.where(row == 2, suf[k : k + 1, 0:1], mine)
         mine = jnp.where(row == 3, norm[k : k + 1, 0:1], mine)
         table = jnp.where(lax.rem(at, 16) == k, mine, table)
+    return ps, qs, pre, suf, table
+
+
+def sweep_tables(n, cols, pack_ref, base_ref, edge_ref, up_ref, pre_ref, row_ref, a_ref):
+    at = n * cols + n * n
+    up, down = pack_ref[at : at + n, :], pack_ref[at + n : at + 2 * n, :]
+    ps, qs, pre, suf, table = rate_tables(up, down)
+    for i, p in enumerate(ps):
+        up_ref[i, 0:n, :] = p
+    pre_ref[0:n, :] = pre
     row_ref[...] = table
+    inner = lane_ids(cols) < LANES - 1
+    for k in range(n):
+        start = pack_ref[k * cols : (k + 1) * cols, :]
+        a_ref[:, k * LANES : (k + 1) * LANES] = start
+        above = jnp.where(inner, pltpu.roll(start, LANES - 1, 1), 0.0)
+        base_ref[k] = start + down[k : k + 1, :] * above
+    edge_ref[...] = pick(a_ref[...], lane_mask(32, n, 16, 0))
+    return qs, suf
+
+
+def side_body(
+    pack_ref, base_ref, edge_ref, up_ref, pre_ref, row_ref, down_ref, suf_ref, ext_ref, a_ref
+):
+    n, cols, _ = base_ref.shape
+    qs, suf = sweep_tables(n, cols, pack_ref, base_ref, edge_ref, up_ref, pre_ref, row_ref, a_ref)
+    for i, q in enumerate(qs):
+        down_ref[i, 0:n, :] = q
+    suf_ref[0:n, :] = suf
     place = row_ids(64)
     first = (lane_ids(64) == 0).astype(F32)
     for k in range(n):
@@ -133,97 +166,115 @@
         ext_ref[:, k * LANES : (k + 1) * LANES] = block
 
 
-    inner = lane_ids(64) < LANES - 1
-    for k in range(n):
-        for m in range(n):
-            cb_ref[k * n + m : k * n + m + 1, :] = c_ref[m] * b_ref[k, m]
-        start = s_ref[k]
-        a_ref[:, k * LANES : (k + 1) * LANES] = start
-        above = jnp.where(inner, pltpu.roll(start, LANES - 1, 1), 0.0)
-        base_ref[k] = start + w_ref[1, k] * above
-    edge_ref[...] = pick(a_ref[...], lane_mask(32, n, 16, 0))
-
-
-def neighbours_into(h_ref, n_ref, g_ref):
-    other = 1 - lax.axis_index("core")
-    for m in range(n_ref.shape[0]):
-        h_ref[m] = n_ref[m] + g_ref[other, m]
-
-
-def coupled(cb_ref, h_ref, k, n, rows):
+def far_side_body(pack_ref, base_ref, edge_ref, up_ref, pre_ref, row_ref, a_ref):
+    n, cols, _ = base_ref.shape
+    sweep_tables(n, cols, pack_ref, base_ref, edge_ref, up_ref, pre_ref, row_ref, a_ref)
+
+
+def coupled(pack_ref, h_ref, k, n, rows):
+    at = n * h_ref.shape[1] + k * n
     return apply_rows(
-        lambda m: cb_ref[k * n + m : k * n + m + 1, :], n, lambda m: h_ref[m, rows, :]
-    )
-
-
-def up_body(cb_ref, base_ref, n_ref, g_ref, up_ref, edge_ref, row_ref, loc_ref, pay_ref, h_ref, a_ref):
+        lambda m: pack_ref[at + m : at + m + 1, :], n, lambda m: h_ref[m, rows, :]
+    )
+
+
+def rise(c_ref, pack_ref, base_ref, one, two, up_ref, edge_ref, row_ref, loc_ref, h_ref, a_ref):
     n, cols, _ = base_ref.shape
-    neighbours_into(h_ref, n_ref, g_ref)
+    for m in range(n):
+        rows = slice(m * cols, (m + 1) * cols)
+        h_ref[m] = c_ref[m] * (one(rows) + two(rows))
     for k in range(n):
         for g in range(cols // 16):
             rows = slice(16 * g, 16 * g + 16)
-            v = base_ref[k, rows, :] + coupled(cb_ref, h_ref, k, n, rows)
+            v = base_ref[k, rows, :] + coupled(pack_ref, h_ref, k, n, rows)
             for i, d in enumerate(STEPS):
                 v = v + up_ref[i, k : k + 1, :] * pltpu.roll(v, d, 1)
-            loc_ref[k, rows, :] = v
+            loc_ref[k * cols + 16 * g : k * cols + 16 * g + 16, :] = v
             a_ref[rows, k * LANES : (k + 1) * LANES] = v
     ends = pick(a_ref[...], lane_mask(32, n, 0, LANES - 1)) + edge_ref[...]
     ends = jnp.concatenate([ends, jnp.zeros((cols, LANES - 32), F32)], axis=1)
     pay = ends[0:16, :]
     for g in range(1, cols // 16):
         pay = pay + pltpu.roll(ends[16 * g : 16 * g + 16, :], 32 * g, 1)
+    return jnp.concatenate([pay, row_ref[...]], axis=0)
+
+
+def own_body(
+    c_ref, pack_ref, base_ref, far_ref, near_ref, up_ref, edge_ref, row_ref, pre_ref,
+    buf_ref, h_ref, a_ref,
+):
+    size = base_ref.shape[0] * base_ref.shape[1]
+    other = 1 - lax.axis_index("core")
+    pay = rise(
+        c_ref, pack_ref, base_ref, lambda rows: far_ref[rows, :], lambda rows: near_ref[other, rows, :],
+        up_ref, edge_ref, row_ref, buf_ref, h_ref, a_ref,
+    )
+    buf_ref[size : size + 24, :] = pay
+    buf_ref[size + 24 : size + 40, :] = pre_ref[...]
+
+
+def far_body(
+    c_ref, pack_ref, base_ref, start_ref, next_ref, up_ref, edge_ref, row_ref, buf_ref, both_ref,
+    loc_ref, pay_ref, h_ref, a_ref,
+):
+    size = base_ref.shape[0] * base_ref.shape[1]
+    other = 1 - lax.axis_index("core")
+    pay = rise(
+        c_ref, pack_ref, base_ref, lambda rows: start_ref[rows, :], lambda rows: next_ref[rows, :],
+        up_ref, edge_ref, row_ref, loc_ref, h_ref, a_ref,
+    )
     for peer in range(pay_ref.shape[0]):
-        pay_ref[peer, 0:16, :] = pay
-        pay_ref[peer, 16:24, :] = row_ref[...]
-
-
-def enter_body(r_ref, loc_ref, pre_ref, out_ref, edge_ref):
-    n, cols, _ = loc_ref.shape
-    peers = r_ref.shape[0]
+        pay_ref[peer, 0:24, :] = buf_ref[size : size + 24, :]
+        pay_ref[peer, 24:48, :] = both_ref[other, size : size + 24, :]
+        pay_ref[peer, 48:72, :] = pay
+
+
+def entering(r_ref, station):
     mine = lax.axis_index("line")
+    at0 = 24 * station
     state = jnp.zeros((16, LANES), F32)
     entry = state
     top = state
-    for at in range(peers - 1):
-        lead = pltpu.roll(r_ref[at + 1, 0:16, :], LANES - 16, 1)
-        tail = r_ref[at, 17:18, :] * lead
+    for at in range(r_ref.shape[0] - 1):
+        lead = pltpu.roll(r_ref[at + 1, at0 : at0 + 16, :], LANES - 16, 1)
+        tail = r_ref[at, at0 + 17 : at0 + 18, :] * lead
         top = jnp.where(mine == at, tail, top)
-        state = r_ref[at, 16:17, :] * state + (r_ref[at, 0:16, :] + tail)
+        state = r_ref[at, at0 + 16 : at0 + 17, :] * state + (r_ref[at, at0 : at0 + 16, :] + tail)
         entry = jnp.where(mine == at + 1, state, entry)
+    return entry, top
+
+
+def down_body(
+    c_ref, pack_ref, r_ref, buf_ref, both_ref, floc_ref, fpre_ref, down_ref, ext_ref, row_ref,
+    loc_ref, pay_ref, h_ref, a_ref,
+):
+    n, cols, _ = loc_ref.shape
+    size = n * cols
+    other = 1 - lax.axis_index("core")
+    mine, _ = entering(r_ref, 0)
+    near, near_top = entering(r_ref, 1)
+    far, far_top = entering(r_ref, 2)
+    top = near_top + far_top
     lane = lane_ids(16)
-    for k in range(n):
-        pre = pre_ref[k : k + 1, :]
+    last, first = lane == LANES - 1, lane == 0
+    for m in range(n):
+        npre = both_ref[other, size + 24 + m : size + 25 + m, :]
+        fpre = fpre_ref[m : m + 1, :]
+        for g in range(cols // 16):
+            rows, at = slice(m * cols + 16 * g, m * cols + 16 * g + 16), 32 * g + m
+            v = both_ref[other, rows, :] + floc_ref[rows, :]
+            v = v + npre * near[:, at : at + 1] + fpre * far[:, at : at + 1]
+            h_ref[m, 16 * g : 16 * g + 16, :] = c_ref[m] * jnp.where(last, v + top[:, at : at + 1], v)
+    one = lane_ids(1) == 0
+    for k in range(n):
+        up = pack_ref[size + n * n + k : size + n * n + k + 1, :]
+        pre = buf_ref[size + 24 + k : size + 25 + k, :]
+        pre = jnp.where(one, 1.0, pltpu.roll(pre, 1, 1))
         for g in range(cols // 16):
             rows = slice(16 * g, 16 * g + 16)
-            at = 32 * g + k
-            v = loc_ref[k, rows, :] + pre * entry[:, at : at + 1]
-            out_ref[k, rows, :] = jnp.where(lane == LANES - 1, v + top[:, at : at + 1], v)
-    edge_ref[...] = entry
-
-
-def below_body(s_ref, up_ref, edge_ref, w_ref, out_ref):
-    n, cols, _ = s_ref.shape
-    lane = lane_ids(16)
-    entry = edge_ref[...]
-    for k in range(n):
-        rise = w_ref[0, k]
-        for g in range(cols // 16):
-            rows = slice(16 * g, 16 * g + 16)
-            at = 32 * g + k
-            below = pltpu.roll(up_ref[k, rows, :], 1, 1)
-            below = jnp.where(lane == 0, entry[:, at : at + 1], below)
-            out_ref[k, rows, :] = s_ref[k, rows, :] + rise * below
-
-
-def down_body(
-    cb_ref, base_ref, n_ref, g_ref, down_ref, ext_ref, row_ref, loc_ref, pay_ref, h_ref, a_ref
-):
-    n, cols, _ = base_ref.shape
-    neighbours_into(h_ref, n_ref, g_ref)
-    for k in range(n):
-        for g in range(cols // 16):
-            rows = slice(16 * g, 16 * g + 16)
-            v = base_ref[k, rows, :] + coupled(cb_ref, h_ref, k, n, rows)
+            wide, at = slice(k * cols + 16 * g, k * cols + 16 * g + 16), 32 * g + k
+            below = jnp.where(first, 0.0, pltpu.roll(buf_ref[wide, :], 1, 1)) + pre * mine[:, at : at + 1]
+            v = pack_ref[wide, :] + up * below + coupled(pack_ref, h_ref, k, n, rows)
             for i, d in enumerate(STEPS):
                 v = v + down_ref[i, k : k + 1, :] * pltpu.roll(v, LANES - d, 1)
             loc_ref[k, rows, :] = v
@@ -364,34 +415,43 @@
     rows = n * stations * pts * peers
     field = (n, cols, pts)
     f, b, w, c = map(in_hbm, (forcing.reshape(field), block_inverse, wall_rates, span_couple))
-    across = [(i, (i + 1) % stations if i % 2 else (i - 1) % stations) for i in range(stations)]
+    pairs = [(i, 1 if i % 2 else -1) for i in range(stations)]
+    across = [(i, (i + d) % stations) for i, d in pairs]
+    beyond = [(i, (i - 2 * d) % stations) for i, d in pairs]
     work = 2 * n * n * cols * pts
+    size = n * cols
     scratch = pltpu.VMEM(field, F32)
-
-    start, b, w = call(
-        start_body, [field, b.shape, w.shape], work, [scratch, pltpu.SemaphoreType.DMA((3,))], HBM
+    wide = pltpu.VMEM((cols, n * pts), F32)
+    tall = pltpu.VMEM((2 * cols, n * pts), F32)
+
+    inputs = [pltpu.VMEM(a.shape, F32) for a in (f, b, w)]
+    start, pack = call(
+        start_body,
+        [(size, pts), (size + n * n + 2 * n, pts)],
+        work,
+        inputs + [pltpu.SemaphoreType.DMA((3,))],
+        HBM,
     )(f, b, w)
-    far = lax.ppermute(start, TILE, across)
+    fpack = lax.ppermute(pack, TILE, across)
     near = lax.all_gather(start, "core")
-    steps = (len(STEPS), 16, pts)
-    wide = pltpu.VMEM((cols, n * pts), F32)
-    cb, base, edge, up, down, pre, suf, row, ext = call(
-        side_body,
-        [(n * n, pts), field, (cols, 32), steps, steps, (16, pts), (16, pts), (8, pts), (64, n * pts)],
-        work // 4,
-        [wide],
-    )(c, b, w, start)
-    loc, pay = call(up_body, [field, (peers, 24, pts)], 2 * work, [scratch, wide])(
-        cb, base, far, near, up, edge, row
+    steps, rows16 = (len(STEPS), 16, pts), (16, pts)
+    tables = [field, (cols, 32), steps, rows16, (8, pts)]
+    base, edge, up, pre, row, down, suf, ext = call(
+        side_body, tables + [steps, rows16, (64, n * pts)], work // 4, [wide]
+    )(pack)
+    held, _, _ = lax.optimization_barrier((start, near, base))
+    beyond = lax.ppermute(held, TILE, beyond)
+    buf = call(own_body, [(size + 40, pts)], 2 * work, [scratch, wide])(
+        c, pack, base, fpack, near, up, edge, row, pre
+    )[0]
+    both = lax.all_gather(buf, "core")
+    fbase, fedge, fup, fpre, frow = call(far_side_body, tables, work // 4, [wide])(fpack)
+    floc, pay = call(far_body, [(size, pts), (peers, 72, pts)], 2 * work, [scratch, wide])(
+        c, fpack, fbase, start, beyond, fup, fedge, frow, buf, both
     )
     got = exchange(pay, "line")
-    rising, edge = call(enter_body, [field, (16, pts)], work // 4)(got, loc, pre)
-    far = lax.ppermute(rising, TILE, across)
-    near = lax.all_gather(rising, "core")
-    base = call(below_body, field, work // 4)(start, rising, edge, w)
-    tall = pltpu.VMEM((2 * cols, n * pts), F32)
     loc, pay = call(down_body, [field, (peers * NCORE, 40, pts)], 4 * work, [scratch, tall])(
-        cb, base, far, near, down, ext, row
+        c, pack, got, buf, both, floc, fpre, down, ext, row
     )
     side = pltpu.VMEM((cols, NCORE * pts), F32)
     part = (cols // 4, pts)

time: 81.5 us -> 81.1 us (level)
  blocking collectives: 65 us -> 60.4 us
  Pallas kernels: 9.58 us -> 12.7 us
  starting transfers between devices: 6.5 us -> 7.54 us
    all_gather x1, blocking collectives: 8.18 us -> 2.3 us  [local(): both = lax.all_gather(buf, 'core')]
    pallas_call x9, Pallas kernels: 9.58 us -> 12.7 us  [run(): pl.pallas_call(body, out_shape=shapes if many else shapes[0], in_specs=[S...]
    all_to_all x4, blocking collectives: 44.7 us -> 46 us  [exchange(): return lax.all_to_all(value, axis, 0, 0, tiled=True)]
    ppermute x2, starting transfers between devices: 6.5 us -> 7.54 us  [the longest x1 4.58 us: local(): fpack = lax.ppermute(pack, TILE, across)]
  transfers between devices with their start and end apart: 2 -> 2, of which waited for: 0 -> 0; matrix products, arithmetic and copies ran while one was open for 0% -> 0% of each run, Pallas kernels for 2% -> 4%
where the time goes in v4:
time: 81.1 us; the launch traced here: 80.7 us
  blocking collectives  60.4 us (74%)
  Pallas kernels  12.7 us (16%)
  starting transfers between devices  7.54 us (9%)
    all_to_all x4, blocking collectives, exchange(): return lax.all_to_all(value, axis, 0, 0, tiled=True)  46 us
    pallas_call x9, Pallas kernels, run(): pl.pallas_call(body, out_shape=shapes if many else shapes[0], in_specs=[S...  12.7 us
    all_gather x1, blocking collectives, local(): near = lax.all_gather(start, 'core')  12.1 us
    ppermute x1, starting transfers between devices, local(): fpack = lax.ppermute(pack, TILE, across)  4.58 us
    ppermute x1, starting transfers between devices, local(): beyond = lax.ppermute(held, TILE, beyond)  2.96 us
    all_gather x1, blocking collectives, local(): both = lax.all_gather(buf, 'core')  2.3 us
  transfers between devices with their start and end apart: 2, of which 0 were waited for; matrix products, arithmetic and copies ran while one was open for 0% of the time, Pallas kernels for 4%

profile of v4, /device:TPU:1, one launch (start us, length us, event | category | flops | bytes accessed | tf_op | source)
XLA Modules:
  0.0 80.7 jit_solution(8928125061975622281)
XLA Ops:
  0.0 1.2 %shard_map.46 = (f32[640,128]{1,0:T(8,128)S(1)}, f32[760,128]{1,0:T(8,128)S(1)}) custom-call(f32[10,64,128]{2,1,0:T(8,128)} %bitcast.9, f32[10,10,1,128]{3,2,1,0:T(1,128)} %b_hbm.1, f32[2,10,1,128]{3,2,1,0:T(1,128)} %w_hbm.1), custom_call_target="tpu_custom_call" | custom-call | flops 1638400 | bytes 1105920 | tf_op jit(solution)/shard_map/pallas_call | solution.py:42
  1.2 4.6 %collective-permute-start = (f32[760,128]{1,0:T(8,128)S(1)}, f32[760,128]{1,0:T(8,128)S(1)}, u32[]{:S(2)}, u32[]{:S(2)}) collective-permute-start(f32[760,128]{1,0:T(8,128)S(1)} %get-tuple-element.27.pack_ref), channel_id=1, source_target_pairs={{0,127},{1,2},{2,1},{3,4},{4,3},{5,6},{6,5},{7,8},{8,7},{9,10},{10... | collective-permute-start | bytes 1167368 | tf_op jit(solution)/shard_map/ppermute | solution.py:435
  5.8 0.8 %shard_map.48 = (f32[10,64,128]{2,1,0:T(8,128)S(1)}, f32[64,32]{1,0:T(8,128)S(1)}, f32[7,16,128]{2,1,0:T(8,128)S(1)}, f32[16,128]{1,0:T(8,128)S(1)}, f32[8,128]{...) custom-call(f32[760,128]{1,0:T(8,128)S(1)} %get-tuple-element.27.pack_ref), custom_call_target="tpu_custom_call" | custom-call | flops 409600 | bytes 1187840 | tf_op jit(solution)/shard_map/pallas_call | solution.py:42
  6.7 12.1 %all-gather = f32[1280,128]{1,0:T(8,128)S(1)} all-gather(f32[640,128]{1,0:T(8,128)S(1)} %get-tuple-element.31.start_ref), channel_id=2, replica_groups=mesh['line'=4,'z'=8,'y'=8,'core'=2] {'core'}, dimensions={0}, use_global_device_ids=true | all-gather | bytes 983040 | tf_op jit(solution)/shard_map/all_gather | solution.py:436
  18.8 3.0 %collective-permute-start.1 = (f32[640,128]{1,0:T(8,128)S(1)}, f32[640,128]{1,0:T(8,128)S(1)}, u32[]{:S(2)}, u32[]{:S(2)}) collective-permute-start(f32[640,128]{1,0:T(8,128)S(1)} %get-tuple-element.31.start_ref), channel_id=1, source_target_pairs={{0,2},{1,127},{2,4},{3,1},{4,6},{5,3},{6,8},{7,5},{8,10},{9,7},{10... | collective-permute-start | bytes 983048 | tf_op jit(solution)/shard_map/ppermute | solution.py:443
  21.7 0.0 collective-permute-done.pack_ref.far_ref
  21.7 0.9 %shard_map.47 = (f32[10,64,128]{2,1,0:T(8,128)S(1)}, f32[64,32]{1,0:T(8,128)S(1)}, f32[7,16,128]{2,1,0:T(8,128)S(1)}, f32[16,128]{1,0:T(8,128)S(1)}, f32[8,128]{1,0:T(8,128)S(1)}) custom-call(f32[760,128]{1,0:T(8,128)S(1)} %collective-permute-done.pack_ref.far_ref), custom_call_target="tpu_custom_call" | custom-call | flops 409600 | bytes 794624 | tf_op jit(solution)/shard_map/pallas_call | solution.py:42
  22.6 1.8 %shard_map.49.buf_ref = f32[680,128]{1,0:T(8,128)S(1)} custom-call(f32[10]{0:T(128)} %c_ref.5, f32[760,128]{1,0:T(8,128)S(1)} %get-tuple-element.27.pack_ref, f32[10,64,128]{2,1,0:T(8,128)S(1)} %get-tuple-element.30.base_ref, f32[760,128]{1,0:T(8,128)S(1)} %collective-permute-done.pack_ref.far_ref, f32[2,640,128]{2,1,0:T(8,128)S(1)} %bitcast.8, ...), custom_call_target="tpu_custom_call" | custom-call | flops 3276800 | bytes 2187304 | tf_op jit(solution)/shard_map/pallas_call | solution.py:42
  24.4 2.3 %all-gather.1 = f32[1360,128]{1,0:T(8,128)S(1)} all-gather(f32[680,128]{1,0:T(8,128)S(1)} %shard_map.49.buf_ref), channel_id=3, replica_groups=mesh['line'=4,'z'=8,'y'=8,'core'=2] {'core'}, dimensions={0}, use_global_device_ids=true | all-gather | bytes 1044480 | tf_op jit(solution)/shard_map/all_gather | solution.py:447
  26.7 0.0 collective-permute-done.1.next_ref
  26.7 1.8 %shard_map.50 = (f32[640,128]{1,0:T(8,128)S(1)}, f32[4,72,128]{2,1,0:T(8,128)S(1)}) custom-call(f32[10]{0:T(128)} %c_ref.5, f32[760,128]{1,0:T(8,128)S(1)} %collective-permute-done.pack_ref.far_ref, f32[10,64,128]{2,1,0:T(8,128)S(1)} %get-tuple-element.28.base_ref, f32[640,128]{1,0:T(8,128)S(1)} %get-tuple-element.31.start_ref, ...), custom_call_target="tpu_custom_call" | custom-call | flops 3276800 | bytes 2961448 | tf_op jit(solution)/shard_map/pallas_call | solution.py:42
  28.5 8.7 %all_to_all.20.r_ref = f32[4,72,128]{2,1,0:T(8,128)S(1)} all-to-all(f32[4,72,128]{2,1,0:T(8,128)S(1)} %get-tuple-element.39), channel_id=1, replica_groups=mesh['line'=4,'z'=8,'y'=8,'core'=2] {'line'}, dimensions={0} | all-to-all | bytes 294912 | tf_op jit(solution)/shard_map/all_to_all | solution.py:408
  37.3 2.9 %shard_map.51 = (f32[10,64,128]{2,1,0:T(8,128)S(1)}, f32[8,40,128]{2,1,0:T(8,128)S(1)}) custom-call(f32[10]{0:T(128)} %c_ref.5, f32[760,128]{1,0:T(8,128)S(1)} %get-tuple-element.27.pack_ref, f32[4,72,128]{2,1,0:T(8,128)S(1)} %all_to_all.20.r_ref, f32[680,128]{1,0:T(8,128)S(1)} %shard_map.49.buf_ref, f32[2,680,128]{2,1,0:T(8,128)S(1)} %bitcast.7, ...), custom_call_target="tpu_custom_call" | custom-call | flops 6553600 | bytes 2797608 | tf_op jit(solution)/shard_map/pallas_call | solution.py:42
  40.2 14.0 %all_to_all.21.r_ref = f32[8,40,128]{2,1,0:T(8,128)S(1)} all-to-all(f32[8,40,128]{2,1,0:T(8,128)S(1)} %get-tuple-element.44), channel_id=1, replica_groups=mesh['line'=4,'z'=8,'y'=8,'core'=2] {'line','core'}, dimensions={0} | all-to-all | bytes 327680 | tf_op jit(solution)/shard_map/all_to_all | solution.py:408
  54.2 0.5 shard_map.52
  54.7 9.7 %all_to_all.22.r_ref = f32[8,16,128]{2,1,0:T(8,128)S(1)} all-to-all(f32[8,16,128]{2,1,0:T(8,128)S(1)} %get-tuple-element.45), channel_id=1, replica_groups=mesh['line'=4,'z'=8,'y'=8,'core'=2] {'y'}, dimensions={0} | all-to-all | bytes 131072 | tf_op jit(solution)/shard_map/all_to_all | solution.py:408
  64.4 13.5 %all_to_all.23.refs_0_ = f32[16,16,128]{2,1,0:T(8,128)S(1)} all-to-all(f32[16,16,128]{2,1,0:T(8,128)S(1)} %shard_map.53), channel_id=1, replica_groups=mesh['line'=4,'z'=8,'y'=8,'core'=2] {'z','core'}, dimensions={0} | all-to-all | bytes 262144 | tf_op jit(solution)/shard_map/all_to_all | solution.py:408
  78.0 2.7 %shard_map.54 = f32[10,64,128]{2,1,0:T(8,128)} custom-call(f32[16,16,128]{2,1,0:T(8,128)S(1)} %all_to_all.23.refs_0_, f32[10,64,128]{2,1,0:T(8,128)S(1)} %get-tuple-element.46.refs_1_, f32[16,128]{1,0:T(8,128)S(1)} %get-tuple-element.47.refs_2_, f32[16,128]{1,0:T(8,128)S(1)} %get-tuple-element.48.refs_3_), custom_call_target="tpu_custom_call" | custom-call | flops 6553600 | bytes 802816 | tf_op jit(solution)/shard_map/pallas_call | solution.py:42
  (1 shorter events, 0.0 us)
Async XLA Ops:
  1.2 20.5 %collective-permute-start = (f32[760,128]{1,0:T(8,128)S(1)}, f32[760,128]{1,0:T(8,128)S(1)}, u32[]{:S(2)}, u32[]{:S(2)}) collective-permute-start(f32[760,128]{1,0:T(8,128)S(1)} %get-tuple-element.27.pack_ref), channel_id=1, source_target_pairs={{0,127},{1,2},{2,1},{3,4},{4,3},{5,6},{6,5},{7,8},{8,7},{9,10},{10... | collective-permute-start | bytes 1167368 | tf_op jit(solution)/shard_map/ppermute | solution.py:435
  18.8 8.0 %collective-permute-start.1 = (f32[640,128]{1,0:T(8,128)S(1)}, f32[640,128]{1,0:T(8,128)S(1)}, u32[]{:S(2)}, u32[]{:S(2)}) collective-permute-start(f32[640,128]{1,0:T(8,128)S(1)} %get-tuple-element.31.start_ref), channel_id=1, source_target_pairs={{0,2},{1,127},{2,4},{3,1},{4,6},{5,3},{6,8},{7,5},{8,10},{9,7},{10... | collective-permute-start | bytes 983048 | tf_op jit(solution)/shard_map/ppermute | solution.py:443

commit v5 on v4

--- a/solution.py
+++ b/solution.py
@@ -15,7 +15,6 @@
 LIMIT = 16 << 20
 STEPS = (1, 2, 4, 8, 16, 32, 64)
 VMEM = pl.BlockSpec(memory_space=pltpu.VMEM)
-SMEM = pl.BlockSpec(memory_space=pltpu.SMEM)
 HBM = pl.BlockSpec(memory_space=pltpu.HBM)
 
 
@@ -42,7 +41,7 @@
         return pl.pallas_call(
             body,
             out_shape=shapes if many else shapes[0],
-            in_specs=[SMEM if a.ndim == 1 else space for a in args],
+            in_specs=[space] * len(args),
             out_specs=[VMEM] * len(shapes) if many else VMEM,
             scratch_shapes=list(scratch),
             compiler_params=pltpu.CompilerParams(vmem_limit_bytes=LIMIT),
@@ -80,10 +79,12 @@
     return (col == (row - shift) * LANES + at).astype(jnp.bfloat16)
 
 
-def start_body(f_hbm, b_hbm, w_hbm, s_ref, pack_ref, f_ref, b_ref, w_ref, sems):
+def start_body(f_hbm, b_hbm, w_hbm, c_hbm, s_ref, pack_ref, f_ref, b_ref, w_ref, c_ref, sems):
     copies = [
         pltpu.make_async_copy(src, dst, sems.at[i])
-        for i, (src, dst) in enumerate(((f_hbm, f_ref), (b_hbm, b_ref), (w_hbm, w_ref)))
+        for i, (src, dst) in enumerate(
+            ((f_hbm, f_ref), (b_hbm, b_ref), (w_hbm, w_ref), (c_hbm, c_ref))
+        )
     ]
     for copy in copies:
         copy.start()
@@ -99,7 +100,7 @@
     at = n * cols
     for k in range(n):
         for m in range(n):
-            pack_ref[at + k * n + m : at + k * n + m + 1, :] = b_ref[k, m]
+            pack_ref[at + k * n + m : at + k * n + m + 1, :] = c_ref[m] * b_ref[k, m]
     at += n * n
     for i in range(2):
         for k in range(n):
@@ -178,11 +179,11 @@
     )
 
 
-def rise(c_ref, pack_ref, base_ref, one, two, up_ref, edge_ref, row_ref, loc_ref, h_ref, a_ref):
+def rise(pack_ref, base_ref, one, two, up_ref, edge_ref, row_ref, loc_ref, h_ref, a_ref):
     n, cols, _ = base_ref.shape
     for m in range(n):
         rows = slice(m * cols, (m + 1) * cols)
-        h_ref[m] = c_ref[m] * (one(rows) + two(rows))
+        h_ref[m] = one(rows) + two(rows)
     for k in range(n):
         for g in range(cols // 16):
             rows = slice(16 * g, 16 * g + 16)
@@ -200,13 +201,13 @@
 
 
 def own_body(
-    c_ref, pack_ref, base_ref, far_ref, near_ref, up_ref, edge_ref, row_ref, pre_ref,
+    pack_ref, base_ref, far_ref, near_ref, up_ref, edge_ref, row_ref, pre_ref,
     buf_ref, h_ref, a_ref,
 ):
     size = base_ref.shape[0] * base_ref.shape[1]
     other = 1 - lax.axis_index("core")
     pay = rise(
-        c_ref, pack_ref, base_ref, lambda rows: far_ref[rows, :], lambda rows: near_ref[other, rows, :],
+        pack_ref, base_ref, lambda rows: far_ref[rows, :], lambda rows: near_ref[other, rows, :],
         up_ref, edge_ref, row_ref, buf_ref, h_ref, a_ref,
     )
     buf_ref[size : size + 24, :] = pay
@@ -214,13 +215,13 @@
 
 
 def far_body(
-    c_ref, pack_ref, base_ref, start_ref, next_ref, up_ref, edge_ref, row_ref, buf_ref, both_ref,
+    pack_ref, base_ref, start_ref, next_ref, up_ref, edge_ref, row_ref, buf_ref, both_ref,
     loc_ref, pay_ref, h_ref, a_ref,
 ):
     size = base_ref.shape[0] * base_ref.shape[1]
     other = 1 - lax.axis_index("core")
     pay = rise(
-        c_ref, pack_ref, base_ref, lambda rows: start_ref[rows, :], lambda rows: next_ref[rows, :],
+        pack_ref, base_ref, lambda rows: start_ref[rows, :], lambda rows: next_ref[rows, :],
         up_ref, edge_ref, row_ref, loc_ref, h_ref, a_ref,
     )
     for peer in range(pay_ref.shape[0]):
@@ -245,7 +246,7 @@
 
 
 def down_body(
-    c_ref, pack_ref, r_ref, buf_ref, both_ref, floc_ref, fpre_ref, down_ref, ext_ref, row_ref,
+    pack_ref, r_ref, buf_ref, both_ref, floc_ref, fpre_ref, down_ref, ext_ref, row_ref,
     loc_ref, pay_ref, h_ref, a_ref,
 ):
     n, cols, _ = loc_ref.shape
@@ -264,7 +265,7 @@
             rows, at = slice(m * cols + 16 * g, m * cols + 16 * g + 16), 32 * g + m
             v = both_ref[other, rows, :] + floc_ref[rows, :]
             v = v + npre * near[:, at : at + 1] + fpre * far[:, at : at + 1]
-            h_ref[m, 16 * g : 16 * g + 16, :] = c_ref[m] * jnp.where(last, v + top[:, at : at + 1], v)
+            h_ref[m, 16 * g : 16 * g + 16, :] = jnp.where(last, v + top[:, at : at + 1], v)
     one = lane_ids(1) == 0
     for k in range(n):
         up = pack_ref[size + n * n + k : size + n * n + k + 1, :]
@@ -429,29 +430,29 @@
         start_body,
         [(size, pts), (size + n * n + 2 * n, pts)],
         work,
-        inputs + [pltpu.SemaphoreType.DMA((3,))],
+        inputs + [pltpu.SMEM(c.shape, F32), pltpu.SemaphoreType.DMA((4,))],
         HBM,
-    )(f, b, w)
+    )(f, b, w, c)
     fpack = lax.ppermute(pack, TILE, across)
     near = lax.all_gather(start, "core")
     steps, rows16 = (len(STEPS), 16, pts), (16, pts)
     tables = [field, (cols, 32), steps, rows16, (8, pts)]
+    held, tables_of, _ = lax.optimization_barrier((start, pack, near))
+    beyond = lax.ppermute(held, TILE, beyond)
     base, edge, up, pre, row, down, suf, ext = call(
         side_body, tables + [steps, rows16, (64, n * pts)], work // 4, [wide]
-    )(pack)
-    held, _, _ = lax.optimization_barrier((start, near, base))
-    beyond = lax.ppermute(held, TILE, beyond)
+    )(tables_of)
     buf = call(own_body, [(size + 40, pts)], 2 * work, [scratch, wide])(
-        c, pack, base, fpack, near, up, edge, row, pre
+        pack, base, fpack, near, up, edge, row, pre
     )[0]
     both = lax.all_gather(buf, "core")
     fbase, fedge, fup, fpre, frow = call(far_side_body, tables, work // 4, [wide])(fpack)
     floc, pay = call(far_body, [(size, pts), (peers, 72, pts)], 2 * work, [scratch, wide])(
-        c, fpack, fbase, start, beyond, fup, fedge, frow, buf, both
+        fpack, fbase, start, beyond, fup, fedge, frow, buf, both
     )
     got = exchange(pay, "line")
     loc, pay = call(down_body, [field, (peers * NCORE, 40, pts)], 4 * work, [scratch, tall])(
-        c, pack, got, buf, both, floc, fpre, down, ext, row
+        pack, got, buf, both, floc, fpre, down, ext, row
     )
     side = pltpu.VMEM((cols, NCORE * pts), F32)
     part = (cols // 4, pts)

time: 81.1 us -> 78.9 us (0.973)
  Pallas kernels: 12.7 us -> 10.7 us
    pallas_call x9, Pallas kernels: 12.7 us -> 10.7 us  [run(): pl.pallas_call(body, out_shape=shapes if many else shapes[0], in_specs=[s...]
where the time goes in v5:
time: 78.9 us; the launch traced here: 78.6 us
  blocking collectives  60.2 us (76%)
  Pallas kernels  10.7 us (14%)
  starting transfers between devices  7.55 us (10%)
    all_to_all x4, blocking collectives, exchange(): return lax.all_to_all(value, axis, 0, 0, tiled=True)  45.8 us
    all_gather x1, blocking collectives, local(): near = lax.all_gather(start, 'core')  12.1 us
    pallas_call x9, Pallas kernels, run(): pl.pallas_call(body, out_shape=shapes if many else shapes[0], in_specs=[s...  10.7 us
    ppermute x1, starting transfers between devices, local(): fpack = lax.ppermute(pack, TILE, across)  4.58 us
    ppermute x1, starting transfers between devices, local(): beyond = lax.ppermute(held, TILE, beyond)  2.96 us
    all_gather x1, blocking collectives, local(): both = lax.all_gather(buf, 'core')  2.3 us
  transfers between devices with their start and end apart: 2, of which 0 were waited for; matrix products, arithmetic and copies ran while one was open for 0% of the time, Pallas kernels for 4%

profile of v5, /device:TPU:1, one launch (start us, length us, event | category | flops | bytes accessed | tf_op | source)
XLA Modules:
  0.0 78.6 jit_solution(15014783380320025042)
XLA Ops:
  0.0 1.3 %shard_map.46 = (f32[640,128]{1,0:T(8,128)S(1)}, f32[760,128]{1,0:T(8,128)S(1)}) custom-call(f32[10,64,128]{2,1,0:T(8,128)} %bitcast.9, f32[10,10,1,128]{3,2,1,0:T(1,128)} %b_hbm.1, f32[2,10,1,128]{3,2,1,0:T(1,128)} %w_hbm.1, f32[10]{0:T(128)} %c_hbm.1), custom_call_target="tpu_custom_call" | custom-call | flops 1638400 | bytes 1105960 | tf_op jit(solution)/shard_map/pallas_call | solution.py:41
  1.3 4.6 %collective-permute-start = (f32[760,128]{1,0:T(8,128)S(1)}, f32[760,128]{1,0:T(8,128)S(1)}, u32[]{:S(2)}, u32[]{:S(2)}) collective-permute-start(f32[760,128]{1,0:T(8,128)S(1)} %get-tuple-element.35.pack_ref), channel_id=1, source_target_pairs={{0,127},{1,2},{2,1},{3,4},{4,3},{5,6},{6,5},{7,8},{8,7},{9,10},{10... | collective-permute-start | bytes 1167368 | tf_op jit(solution)/shard_map/ppermute | solution.py:436
  5.9 12.1 %all-gather = f32[1280,128]{1,0:T(8,128)S(1)} all-gather(f32[640,128]{1,0:T(8,128)S(1)} %get-tuple-element.31.start_ref), channel_id=2, replica_groups=mesh['line'=4,'z'=8,'y'=8,'core'=2] {'core'}, dimensions={0}, use_global_device_ids=true | all-gather | bytes 983040 | tf_op jit(solution)/shard_map/all_gather | solution.py:437
  18.0 3.0 %collective-permute-start.1 = (f32[640,128]{1,0:T(8,128)S(1)}, f32[640,128]{1,0:T(8,128)S(1)}, u32[]{:S(2)}, u32[]{:S(2)}) collective-permute-start(f32[640,128]{1,0:T(8,128)S(1)} %get-tuple-element.31.start_ref), channel_id=1, source_target_pairs={{0,2},{1,127},{2,4},{3,1},{4,6},{5,3},{6,8},{7,5},{8,10},{9,7},{10... | collective-permute-start | bytes 983048 | tf_op jit(solution)/shard_map/ppermute | solution.py:441
  20.9 0.8 %shard_map.48 = (f32[10,64,128]{2,1,0:T(8,128)S(1)}, f32[64,32]{1,0:T(8,128)S(1)}, f32[7,16,128]{2,1,0:T(8,128)S(1)}, f32[16,128]{1,0:T(8,128)S(1)}, f32[8,128]{...) custom-call(f32[760,128]{1,0:T(8,128)S(1)} %get-tuple-element.35.pack_ref), custom_call_target="tpu_custom_call" | custom-call | flops 409600 | bytes 1187840 | tf_op jit(solution)/shard_map/pallas_call | solution.py:41
  21.8 0.0 collective-permute-done.pack_ref.far_ref
  21.8 0.9 %shard_map.47 = (f32[10,64,128]{2,1,0:T(8,128)S(1)}, f32[64,32]{1,0:T(8,128)S(1)}, f32[7,16,128]{2,1,0:T(8,128)S(1)}, f32[16,128]{1,0:T(8,128)S(1)}, f32[8,128]{1,0:T(8,128)S(1)}) custom-call(f32[760,128]{1,0:T(8,128)S(1)} %collective-permute-done.pack_ref.far_ref), custom_call_target="tpu_custom_call" | custom-call | flops 409600 | bytes 794624 | tf_op jit(solution)/shard_map/pallas_call | solution.py:41
  22.7 1.1 %shard_map.49.buf_ref = f32[680,128]{1,0:T(8,128)S(1)} custom-call(f32[760,128]{1,0:T(8,128)S(1)} %get-tuple-element.35.pack_ref, f32[10,64,128]{2,1,0:T(8,128)S(1)} %get-tuple-element.36.base_ref, f32[760,128]{1,0:T(8,128)S(1)} %collective-permute-done.pack_ref.far_ref, f32[2,640,128]{2,1,0:T(8,128)S(1)} %bitcast.8, ...), custom_call_target="tpu_custom_call" | custom-call | flops 3276800 | bytes 2187264 | tf_op jit(solution)/shard_map/pallas_call | solution.py:41
  23.8 2.3 %all-gather.1 = f32[1360,128]{1,0:T(8,128)S(1)} all-gather(f32[680,128]{1,0:T(8,128)S(1)} %shard_map.49.buf_ref), channel_id=3, replica_groups=mesh['line'=4,'z'=8,'y'=8,'core'=2] {'core'}, dimensions={0}, use_global_device_ids=true | all-gather | bytes 1044480 | tf_op jit(solution)/shard_map/all_gather | solution.py:448
  26.1 0.0 collective-permute-done.1.next_ref
  26.1 1.1 %shard_map.50 = (f32[640,128]{1,0:T(8,128)S(1)}, f32[4,72,128]{2,1,0:T(8,128)S(1)}) custom-call(f32[760,128]{1,0:T(8,128)S(1)} %collective-permute-done.pack_ref.far_ref, f32[10,64,128]{2,1,0:T(8,128)S(1)} %get-tuple-element.29.base_ref, f32[640,128]{1,0:T(8,128)S(1)} %get-tuple-element.31.start_ref, f32[640,128]{1,0:T(8,128)S(1)} %collective-permute-done.1.next_ref, ...), custom_call_target="tpu_custom_call" | custom-call | flops 3276800 | bytes 2961408 | tf_op jit(solution)/shard_map/pallas_call | solution.py:41
  27.2 8.7 %all_to_all.20.r_ref = f32[4,72,128]{2,1,0:T(8,128)S(1)} all-to-all(f32[4,72,128]{2,1,0:T(8,128)S(1)} %get-tuple-element.41), channel_id=1, replica_groups=mesh['line'=4,'z'=8,'y'=8,'core'=2] {'line'}, dimensions={0} | all-to-all | bytes 294912 | tf_op jit(solution)/shard_map/all_to_all | solution.py:409
  36.0 2.2 %shard_map.51 = (f32[10,64,128]{2,1,0:T(8,128)S(1)}, f32[8,40,128]{2,1,0:T(8,128)S(1)}) custom-call(f32[760,128]{1,0:T(8,128)S(1)} %get-tuple-element.35.pack_ref, f32[4,72,128]{2,1,0:T(8,128)S(1)} %all_to_all.20.r_ref, f32[680,128]{1,0:T(8,128)S(1)} %shard_map.49.buf_ref, f32[2,680,128]{2,1,0:T(8,128)S(1)} %bitcast.7, ...), custom_call_target="tpu_custom_call" | custom-call | flops 6553600 | bytes 2797568 | tf_op jit(solution)/shard_map/pallas_call | solution.py:41
  38.2 13.9 %all_to_all.21.r_ref = f32[8,40,128]{2,1,0:T(8,128)S(1)} all-to-all(f32[8,40,128]{2,1,0:T(8,128)S(1)} %get-tuple-element.46), channel_id=1, replica_groups=mesh['line'=4,'z'=8,'y'=8,'core'=2] {'line','core'}, dimensions={0} | all-to-all | bytes 327680 | tf_op jit(solution)/shard_map/all_to_all | solution.py:409
  52.1 0.5 shard_map.52
  52.6 9.7 %all_to_all.22.r_ref = f32[8,16,128]{2,1,0:T(8,128)S(1)} all-to-all(f32[8,16,128]{2,1,0:T(8,128)S(1)} %get-tuple-element.47), channel_id=1, replica_groups=mesh['line'=4,'z'=8,'y'=8,'core'=2] {'y'}, dimensions={0} | all-to-all | bytes 131072 | tf_op jit(solution)/shard_map/all_to_all | solution.py:409
  62.3 13.5 %all_to_all.23.refs_0_ = f32[16,16,128]{2,1,0:T(8,128)S(1)} all-to-all(f32[16,16,128]{2,1,0:T(8,128)S(1)} %shard_map.53), channel_id=1, replica_groups=mesh['line'=4,'z'=8,'y'=8,'core'=2] {'z','core'}, dimensions={0} | all-to-all | bytes 262144 | tf_op jit(solution)/shard_map/all_to_all | solution.py:409
  75.8 2.7 %shard_map.54 = f32[10,64,128]{2,1,0:T(8,128)} custom-call(f32[16,16,128]{2,1,0:T(8,128)S(1)} %all_to_all.23.refs_0_, f32[10,64,128]{2,1,0:T(8,128)S(1)} %get-tuple-element.48.refs_1_, f32[16,128]{1,0:T(8,128)S(1)} %get-tuple-element.49.refs_2_, f32[16,128]{1,0:T(8,128)S(1)} %get-tuple-element.50.refs_3_), custom_call_target="tpu_custom_call" | custom-call | flops 6553600 | bytes 802816 | tf_op jit(solution)/shard_map/pallas_call | solution.py:41
  (1 shorter events, 0.0 us)
Async XLA Ops:
  1.3 20.5 %collective-permute-start = (f32[760,128]{1,0:T(8,128)S(1)}, f32[760,128]{1,0:T(8,128)S(1)}, u32[]{:S(2)}, u32[]{:S(2)}) collective-permute-start(f32[760,128]{1,0:T(8,128)S(1)} %get-tuple-element.35.pack_ref), channel_id=1, source_target_pairs={{0,127},{1,2},{2,1},{3,4},{4,3},{5,6},{6,5},{7,8},{8,7},{9,10},{10... | collective-permute-start | bytes 1167368 | tf_op jit(solution)/shard_map/ppermute | solution.py:436
  18.0 8.1 %collective-permute-start.1 = (f32[640,128]{1,0:T(8,128)S(1)}, f32[640,128]{1,0:T(8,128)S(1)}, u32[]{:S(2)}, u32[]{:S(2)}) collective-permute-start(f32[640,128]{1,0:T(8,128)S(1)} %get-tuple-element.31.start_ref), channel_id=1, source_target_pairs={{0,2},{1,127},{2,4},{3,1},{4,6},{5,3},{6,8},{7,5},{8,10},{9,7},{10... | collective-permute-start | bytes 983048 | tf_op jit(solution)/shard_map/ppermute | solution.py:441

commit v6 on v5

--- a/solution.py
+++ b/solution.py
@@ -72,11 +72,13 @@
     return total
 
 
-def lane_mask(rows, n, shift, at):
-    wide = (rows, n * LANES)
+def end_mask(n):
+    wide = (32, n * LANES)
     col = lax.broadcasted_iota(jnp.int32, wide, 1)
     row = lax.broadcasted_iota(jnp.int32, wide, 0)
-    return (col == (row - shift) * LANES + at).astype(jnp.bfloat16)
+    return (col == jnp.where(row < 16, row * LANES + LANES - 1, (row - 16) * LANES)).astype(
+        jnp.bfloat16
+    )
 
 
 def start_body(f_hbm, b_hbm, w_hbm, c_hbm, s_ref, pack_ref, f_ref, b_ref, w_ref, c_ref, sems):
@@ -133,7 +135,7 @@
     return ps, qs, pre, suf, table
 
 
-def sweep_tables(n, cols, pack_ref, base_ref, edge_ref, up_ref, pre_ref, row_ref, a_ref):
+def sweep_tables(n, cols, pack_ref, base_ref, up_ref, pre_ref, row_ref):
     at = n * cols + n * n
     up, down = pack_ref[at : at + n, :], pack_ref[at + n : at + 2 * n, :]
     ps, qs, pre, suf, table = rate_tables(up, down)
@@ -144,32 +146,27 @@
     inner = lane_ids(cols) < LANES - 1
     for k in range(n):
         start = pack_ref[k * cols : (k + 1) * cols, :]
-        a_ref[:, k * LANES : (k + 1) * LANES] = start
         above = jnp.where(inner, pltpu.roll(start, LANES - 1, 1), 0.0)
         base_ref[k] = start + down[k : k + 1, :] * above
-    edge_ref[...] = pick(a_ref[...], lane_mask(32, n, 16, 0))
     return qs, suf
 
 
-def side_body(
-    pack_ref, base_ref, edge_ref, up_ref, pre_ref, row_ref, down_ref, suf_ref, ext_ref, a_ref
-):
+def side_body(pack_ref, base_ref, up_ref, pre_ref, row_ref, down_ref, suf_ref, ext_ref):
     n, cols, _ = base_ref.shape
-    qs, suf = sweep_tables(n, cols, pack_ref, base_ref, edge_ref, up_ref, pre_ref, row_ref, a_ref)
+    qs, suf = sweep_tables(n, cols, pack_ref, base_ref, up_ref, pre_ref, row_ref)
     for i, q in enumerate(qs):
         down_ref[i, 0:n, :] = q
     suf_ref[0:n, :] = suf
-    place = row_ids(64)
-    first = (lane_ids(64) == 0).astype(F32)
-    for k in range(n):
-        block = jnp.where(place == k, jnp.broadcast_to(suf[k : k + 1, :], (64, LANES)), 0.0)
+    place = row_ids(32)
+    first = (lane_ids(32) == 0).astype(F32)
+    for k in range(n):
+        block = jnp.where(place == k, jnp.broadcast_to(suf[k : k + 1, :], (32, LANES)), 0.0)
         block = jnp.where(place == 16 + k, first, block)
         ext_ref[:, k * LANES : (k + 1) * LANES] = block
 
 
-def far_side_body(pack_ref, base_ref, edge_ref, up_ref, pre_ref, row_ref, a_ref):
-    n, cols, _ = base_ref.shape
-    sweep_tables(n, cols, pack_ref, base_ref, edge_ref, up_ref, pre_ref, row_ref, a_ref)
+def other_body(near_ref, out_ref):
+    out_ref[...] = near_ref[1 - lax.axis_index("core")]
 
 
 def coupled(pack_ref, h_ref, k, n, rows):
@@ -179,70 +176,110 @@
     )
 
 
-def rise(pack_ref, base_ref, one, two, up_ref, edge_ref, row_ref, loc_ref, h_ref, a_ref):
+def rise(pack_ref, base_ref, one, two, up_ref, loc_ref, h_ref, a_ref):
     n, cols, _ = base_ref.shape
     for m in range(n):
         rows = slice(m * cols, (m + 1) * cols)
         h_ref[m] = one(rows) + two(rows)
+    first = lane_ids(16) == 0
     for k in range(n):
         for g in range(cols // 16):
             rows = slice(16 * g, 16 * g + 16)
             v = base_ref[k, rows, :] + coupled(pack_ref, h_ref, k, n, rows)
             for i, d in enumerate(STEPS):
                 v = v + up_ref[i, k : k + 1, :] * pltpu.roll(v, d, 1)
-            loc_ref[k * cols + 16 * g : k * cols + 16 * g + 16, :] = v
-            a_ref[rows, k * LANES : (k + 1) * LANES] = v
-    ends = pick(a_ref[...], lane_mask(32, n, 0, LANES - 1)) + edge_ref[...]
+            wide = slice(k * cols + 16 * g, k * cols + 16 * g + 16)
+            loc_ref[wide, :] = v
+            a_ref[rows, k * LANES : (k + 1) * LANES] = jnp.where(first, pack_ref[wide, :], v)
+    ends = pick(a_ref[...], end_mask(n))
     ends = jnp.concatenate([ends, jnp.zeros((cols, LANES - 32), F32)], axis=1)
     pay = ends[0:16, :]
     for g in range(1, cols // 16):
         pay = pay + pltpu.roll(ends[16 * g : 16 * g + 16, :], 32 * g, 1)
-    return jnp.concatenate([pay, row_ref[...]], axis=0)
+    return pay
 
 
 def own_body(
-    pack_ref, base_ref, far_ref, near_ref, up_ref, edge_ref, row_ref, pre_ref,
-    buf_ref, h_ref, a_ref,
+    pack_ref, base_ref, far_ref, near_ref, up_ref, row_ref, pre_ref,
+    buf_ref, fbase_ref, fup_ref, fpre_ref, frow_ref, h_ref, a_ref,
 ):
-    size = base_ref.shape[0] * base_ref.shape[1]
+    n, cols, _ = base_ref.shape
+    size = n * cols
     other = 1 - lax.axis_index("core")
-    pay = rise(
+    sweep_tables(n, cols, far_ref, fbase_ref, fup_ref, fpre_ref, frow_ref)
+    buf_ref[size : size + 16, :] = rise(
         pack_ref, base_ref, lambda rows: far_ref[rows, :], lambda rows: near_ref[other, rows, :],
-        up_ref, edge_ref, row_ref, buf_ref, h_ref, a_ref,
-    )
-    buf_ref[size : size + 24, :] = pay
+        up_ref, buf_ref, h_ref, a_ref,
+    )
+    buf_ref[size + 16 : size + 24, :] = row_ref[...]
     buf_ref[size + 24 : size + 40, :] = pre_ref[...]
 
 
 def far_body(
-    pack_ref, base_ref, start_ref, next_ref, up_ref, edge_ref, row_ref, buf_ref, both_ref,
+    pack_ref, base_ref, start_ref, next_ref, up_ref, row_ref, buf_ref, both_ref,
     loc_ref, pay_ref, h_ref, a_ref,
 ):
     size = base_ref.shape[0] * base_ref.shape[1]
     other = 1 - lax.axis_index("core")
     pay = rise(
         pack_ref, base_ref, lambda rows: start_ref[rows, :], lambda rows: next_ref[rows, :],
-        up_ref, edge_ref, row_ref, loc_ref, h_ref, a_ref,
-    )
+        up_ref, loc_ref, h_ref, a_ref,
+    )
+    own, near = buf_ref[size : size + 24, :], both_ref[other, size : size + 24, :]
+    row = row_ids(8)
+    table = jnp.where(row < 2, own[16:24, :], pltpu.roll(near[16:24, :], 2, 0))
+    table = jnp.where(row < 4, table, pltpu.roll(row_ref[...], 4, 0))
     for peer in range(pay_ref.shape[0]):
-        pay_ref[peer, 0:24, :] = buf_ref[size : size + 24, :]
-        pay_ref[peer, 24:48, :] = both_ref[other, size : size + 24, :]
-        pay_ref[peer, 48:72, :] = pay
+        pay_ref[peer, 0:16, :] = own[0:16, :]
+        pay_ref[peer, 16:32, :] = near[0:16, :]
+        pay_ref[peer, 32:48, :] = pay
+        pay_ref[peer, 48:56, :] = table
 
 
 def entering(r_ref, station):
     mine = lax.axis_index("line")
-    at0 = 24 * station
+    at0, row = 16 * station, 48 + 2 * station
     state = jnp.zeros((16, LANES), F32)
     entry = state
     top = state
     for at in range(r_ref.shape[0] - 1):
         lead = pltpu.roll(r_ref[at + 1, at0 : at0 + 16, :], LANES - 16, 1)
-        tail = r_ref[at, at0 + 17 : at0 + 18, :] * lead
+        tail = r_ref[at, row + 1 : row + 2, :] * lead
         top = jnp.where(mine == at, tail, top)
-        state = r_ref[at, at0 + 16 : at0 + 17, :] * state + (r_ref[at, at0 : at0 + 16, :] + tail)
+        state = r_ref[at, row : row + 1, :] * state + (r_ref[at, at0 : at0 + 16, :] + tail)
         entry = jnp.where(mine == at + 1, state, entry)
     return entry, top
+
+
+def packed_blocks(gram):
+    lane, row = lane_ids(32), row_ids(32)
+    corner = pltpu.roll(gram[32:64, :], LANES - 32, 1)
+    joined = jnp.where(lane >= row, gram[0:32, :], corner)
+    extra = jnp.sum(jnp.where(lane == row, corner, 0.0), axis=0, keepdims=True)
+    quarter = lane_ids(8) // 32
+    blocks = []
+    for part in (pltpu.roll(gram[0:32, :], LANES - 32, 1), joined):
+        block = jnp.zeros((8, LANES), F32)
+        for a in range(4):
+            block = jnp.where(quarter == a, pltpu.roll(part[8 * a : 8 * a + 8, :], 32 * a, 1), block)
+        blocks.append(block)
+    return (blocks[0], jnp.zeros((1, LANES), F32)), (blocks[1], extra)
+
+
+def unpacked(upper, joined, extra):
+    def spread(block):
+        return jnp.concatenate([pltpu.roll(block, (LANES - 32 * a) % LANES, 1) for a in range(4)], axis=0)
+
+    lane, row = lane_ids(32), row_ids(32)
+    upper, joined = spread(upper), spread(joined)
+    turned = jnp.where(lane < 32, joined, pltpu.roll(upper, 32, 1)).T
+    turned = jnp.concatenate([turned, jnp.zeros((LANES, LANES - 32), F32)], axis=1)
+    first, second = turned[0:32, :], turned[32:64, :]
+    low = jnp.where(lane >= row, joined, first)
+    high = jnp.where(lane < row, joined, jnp.where(lane == row, extra, first))
+    top = jnp.where(lane < 32, low, pltpu.roll(upper, 32, 1))
+    bottom = jnp.where(lane < 32, second, pltpu.roll(high, 32, 1))
+    return jnp.concatenate([top, bottom], axis=0)
 
 
 def down_body(
@@ -280,20 +317,20 @@
                 v = v + down_ref[i, k : k + 1, :] * pltpu.roll(v, LANES - d, 1)
             loc_ref[k, rows, :] = v
             a_ref[rows, k * LANES : (k + 1) * LANES] = v
-    a_ref[cols : 2 * cols, :] = ext_ref[...]
+    a_ref[cols : cols + 32, :] = ext_ref[...]
     total = dot_nt(a_ref[0:cols, :], a_ref[...])
+    total = jnp.concatenate([total, jnp.zeros((cols, 32), F32)], axis=1)
     lane = lane_ids(16)
     edges = jnp.zeros((16, LANES), F32)
     for g in range(cols // 16):
         moved = pltpu.roll(total[16 * g : 16 * g + 16, :], (32 * g + 64) % LANES, 1)
         edges = jnp.where(lane // 32 == g, moved, edges)
-    half = cols // 2
+    blocks = packed_blocks(total)
     for peer in range(pay_ref.shape[0]):
-        at = half * (peer % NCORE)
-        low = pltpu.roll(total[at + 16 : at + 32, :], 64, 1)
-        pay_ref[peer, 0:16, :] = jnp.where(lane < 64, total[at : at + 16, :], low)
-        pay_ref[peer, 16:32, :] = edges
-        pay_ref[peer, 32:40, :] = row_ref[...]
+        block, extra = blocks[peer % NCORE]
+        pay_ref[peer, 0:8, :] = block
+        pay_ref[peer, 8:24, :] = edges
+        pay_ref[peer, 24:32, :] = jnp.where(row_ids(8) == 4, extra, row_ref[...])
 
 
 def line_body(r_ref, gram_ref, entry_ref, left_ref, right_ref):
@@ -310,10 +347,10 @@
         right = [zero] * (cols // 16)
         for at in range(peers - 2, -1, -1):
             above, here = NCORE * (at + 1) + station, NCORE * at + station
-            state = r_ref[above, 34:35, :] * state + r_ref[above, 16:32, :]
+            state = r_ref[above, 26:27, :] * state + r_ref[above, 8:24, :]
             entry = jnp.where((mine == at) & (core == station), state, entry)
             back = pltpu.roll(state, LANES - 16, 1)
-            cross = r_ref[here, 16:32, :] + (0.5 * r_ref[here, 35:36, :]) * back
+            cross = r_ref[here, 8:24, :] + (0.5 * r_ref[here, 27:28, :]) * back
             a = jnp.where(first, cross, state)
             b = jnp.where(first, back, pltpu.roll(cross, 16, 1))
             for g in range(cols // 16):
@@ -324,23 +361,36 @@
             rows = slice(16 * g, 16 * g + 16)
             left_ref[rows, station * LANES : (station + 1) * LANES] = left[g]
             right_ref[rows, station * LANES : (station + 1) * LANES] = right[g]
-    half = cols // 2
-    mine = left_ref[pl.ds(pl.multiple_of(half * core, half), half), :]
-    fix = dot_nt(mine, right_ref[...])
-    total = jnp.concatenate([fix[0:16, :], fix[16:32, :]], axis=1)
+    fix = dot_nt(left_ref[...], right_ref[...])
+    fix = jnp.concatenate([fix, jnp.zeros((cols, LANES - cols), F32)], axis=1)
+    (one, none), (two, extra) = packed_blocks(fix)
+    total = jnp.where(core == 0, one, two)
+    extra = jnp.where(core == 0, none, extra)
     for i in range(r_ref.shape[0]):
-        total = total + r_ref[i, 0:16, :]
-    for peer in range(gram_ref.shape[0]):
-        gram_ref[peer] = total
+        total = total + r_ref[i, 0:8, :]
+        extra = extra + r_ref[i, 28:29, :]
+    spread_rows(gram_ref, [total[i : i + 1, :] for i in range(8)] + [extra])
     entry_ref[...] = entry
 
 
+def spread_rows(out_ref, rows):
+    for peer in range(out_ref.shape[0]):
+        for i, row in enumerate(rows):
+            out_ref[peer, i] = row
+
+
+def summed_rows(r_ref, first, step):
+    rows = []
+    for i in range(r_ref.shape[1]):
+        total = r_ref[first, i]
+        for peer in range(first + step, r_ref.shape[0], step):
+            total = total + r_ref[peer, i]
+        rows.append(total)
+    return rows
+
+
 def sum_body(r_ref, o_ref):
-    total = r_ref[0]
-    for i in range(1, r_ref.shape[0]):
-        total = total + r_ref[i]
-    for peer in range(o_ref.shape[0]):
-        o_ref[peer] = total
+    spread_rows(o_ref, summed_rows(r_ref, 0, 1))
 
 
 def inverse_factor(scale, gram, v_ref):
@@ -388,14 +438,9 @@
             rows, at = slice(16 * g, 16 * g + 16), 32 * g + 16 + k
             v = loc_ref[k, rows, :] + suf * entry_ref[:, at : at + 1]
             f_ref[rows, k * LANES : (k + 1) * LANES] = v
-    parts = []
-    for core in range(NCORE):
-        packed = r_ref[core]
-        for i in range(NCORE + core, r_ref.shape[0], NCORE):
-            packed = packed + r_ref[i]
-        parts += [packed, pltpu.roll(packed, 64, 1)]
-    unpacked = jnp.concatenate(parts, axis=0)
-    inv = inverse_factor(scale, unpacked, v_ref)
+    upper, joined = (summed_rows(r_ref, core, NCORE) for core in range(NCORE))
+    gram = unpacked(jnp.concatenate(upper[:8], axis=0), jnp.concatenate(joined[:8], axis=0), joined[8])
+    inv = inverse_factor(scale, gram, v_ref)
     out = jnp.dot(inv, f_ref[...], precision=HIGH, preferred_element_type=F32)
     for k in range(n):
         out_ref[k] = out[:, k * LANES : (k + 1) * LANES]
@@ -418,12 +463,11 @@
     f, b, w, c = map(in_hbm, (forcing.reshape(field), block_inverse, wall_rates, span_couple))
     pairs = [(i, 1 if i % 2 else -1) for i in range(stations)]
     across = [(i, (i + d) % stations) for i, d in pairs]
-    beyond = [(i, (i - 2 * d) % stations) for i, d in pairs]
     work = 2 * n * n * cols * pts
     size = n * cols
     scratch = pltpu.VMEM(field, F32)
     wide = pltpu.VMEM((cols, n * pts), F32)
-    tall = pltpu.VMEM((2 * cols, n * pts), F32)
+    tall = pltpu.VMEM((cols + 32, n * pts), F32)
 
     inputs = [pltpu.VMEM(a.shape, F32) for a in (f, b, w)]
     start, pack = call(
@@ -436,26 +480,25 @@
     fpack = lax.ppermute(pack, TILE, across)
     near = lax.all_gather(start, "core")
     steps, rows16 = (len(STEPS), 16, pts), (16, pts)
-    tables = [field, (cols, 32), steps, rows16, (8, pts)]
-    held, tables_of, _ = lax.optimization_barrier((start, pack, near))
-    beyond = lax.ppermute(held, TILE, beyond)
-    base, edge, up, pre, row, down, suf, ext = call(
-        side_body, tables + [steps, rows16, (64, n * pts)], work // 4, [wide]
+    tables = [field, steps, rows16, (8, pts)]
+    beyond = lax.ppermute(call(other_body, (size, pts))(near), TILE, across)
+    tables_of, near = lax.optimization_barrier((pack, near))
+    base, up, pre, row, down, suf, ext = call(
+        side_body, tables + [steps, rows16, (32, n * pts)], work // 4
     )(tables_of)
-    buf = call(own_body, [(size + 40, pts)], 2 * work, [scratch, wide])(
-        pack, base, fpack, near, up, edge, row, pre
-    )[0]
+    buf, fbase, fup, fpre, frow = call(
+        own_body, [(size + 40, pts)] + tables, 2 * work, [scratch, wide]
+    )(pack, base, fpack, near, up, row, pre)
     both = lax.all_gather(buf, "core")
-    fbase, fedge, fup, fpre, frow = call(far_side_body, tables, work // 4, [wide])(fpack)
-    floc, pay = call(far_body, [(size, pts), (peers, 72, pts)], 2 * work, [scratch, wide])(
-        fpack, fbase, start, beyond, fup, fedge, frow, buf, both
+    floc, pay = call(far_body, [(size, pts), (peers, 56, pts)], 2 * work, [scratch, wide])(
+        fpack, fbase, start, beyond, fup, frow, buf, both
     )
     got = exchange(pay, "line")
-    loc, pay = call(down_body, [field, (peers * NCORE, 40, pts)], 4 * work, [scratch, tall])(
+    loc, pay = call(down_body, [field, (peers * NCORE, 32, pts)], 4 * work, [scratch, tall])(
         pack, got, buf, both, floc, fpre, down, ext, row
     )
     side = pltpu.VMEM((cols, NCORE * pts), F32)
-    part = (cols // 4, pts)
+    part = (9, 1, pts)
     gram, entry = call(line_body, [(NY,) + part, (16, pts)], work // 4, [side, side])(
         exchange(pay, ("line", "core"))
     )

time: 78.9 us -> 76.6 us (0.971)
  blocking collectives: 60.2 us -> 58.2 us
  starting transfers between devices: 7.55 us -> 6.5 us
  waiting for transfers between devices: 0.01 us -> 0.93 us
    all_to_all x4, blocking collectives: 45.8 us -> 42.7 us  [exchange(): return lax.all_to_all(value, axis, 0, 0, tiled=True)]
    all_gather x1, blocking collectives: 2.3 us -> 3.38 us  [local(): both = lax.all_gather(buf, 'core')]
    ppermute x1, starting transfers between devices: 2.96 us -> 1.92 us  [local(): beyond = lax.ppermute(call(other_body, (size, pts))(near), TILE, across)]
    ppermute x1, waiting for transfers between devices: 0.01 us -> 0.93 us  [local(): beyond = lax.ppermute(call(other_body, (size, pts))(near), TILE, across)]
  transfers between devices with their start and end apart: 2 -> 2, of which waited for: 0 -> 1; matrix products, arithmetic and copies ran while one was open for 0% -> 0% of each run, Pallas kernels for 4% -> 3%
where the time goes in v6:
time: 76.6 us; the launch traced here: 76.3 us
  blocking collectives  58.2 us (76%)
  Pallas kernels  10.6 us (14%)
  starting transfers between devices  6.5 us (8%)
  waiting for transfers between devices  0.93 us (1%)
    all_to_all x4, blocking collectives, exchange(): return lax.all_to_all(value, axis, 0, 0, tiled=True)  42.7 us
    all_gather x1, blocking collectives, local(): near = lax.all_gather(start, 'core')  12.1 us
    pallas_call x9, Pallas kernels, run(): pl.pallas_call(body, out_shape=shapes if many else shapes[0], in_specs=[s...  10.6 us
    ppermute x1, starting transfers between devices, local(): fpack = lax.ppermute(pack, TILE, across)  4.58 us
    all_gather x1, blocking collectives, local(): both = lax.all_gather(buf, 'core')  3.38 us
    ppermute x1, starting transfers between devices, local(): beyond = lax.ppermute(call(other_body, (size, pts))(near), TILE, across)  1.92 us
  transfers between devices with their start and end apart: 2, of which 1 were waited for; matrix products, arithmetic and copies ran while one was open for 0% of the time, Pallas kernels for 3%

profile of v6, /device:TPU:1, one launch (start us, length us, event | category | flops | bytes accessed | tf_op | source)
XLA Modules:
  0.0 76.3 jit_solution(7462144895739871215)
XLA Ops:
  0.0 1.3 %shard_map.46 = (f32[640,128]{1,0:T(8,128)S(1)}, f32[760,128]{1,0:T(8,128)S(1)}) custom-call(f32[10,64,128]{2,1,0:T(8,128)} %bitcast.10, f32[10,10,1,128]{3,2,1,0:T(1,128)} %b_hbm.1, f32[2,10,1,128]{3,2,1,0:T(1,128)} %w_hbm.1, f32[10]{0:T(128)} %c_hbm.1), custom_call_target="tpu_custom_call" | custom-call | flops 1638400 | bytes 1105960 | tf_op jit(solution)/shard_map/pallas_call | solution.py:41
  1.3 4.6 %collective-permute-start = (f32[760,128]{1,0:T(8,128)S(1)}, f32[760,128]{1,0:T(8,128)S(1)}, u32[]{:S(2)}, u32[]{:S(2)}) collective-permute-start(f32[760,128]{1,0:T(8,128)S(1)} %get-tuple-element.29.pack_ref), channel_id=1, source_target_pairs={{0,127},{1,2},{2,1},{3,4},{4,3},{5,6},{6,5},{7,8},{8,7},{9,10},{10... | collective-permute-start | bytes 1167368 | tf_op jit(solution)/shard_map/ppermute | solution.py:480
  5.9 12.1 %all-gather = f32[1280,128]{1,0:T(8,128)S(1)} all-gather(f32[640,128]{1,0:T(8,128)S(1)} %get-tuple-element.28.start_ref), channel_id=2, replica_groups=mesh['line'=4,'z'=8,'y'=8,'core'=2] {'core'}, dimensions={0}, use_global_device_ids=true | all-gather | bytes 983040 | tf_op jit(solution)/shard_map/all_gather | solution.py:481
  18.0 1.9 %collective-permute-start.1 = (f32[640,128]{1,0:T(8,128)S(1)}, f32[640,128]{1,0:T(8,128)S(1)}, u32[]{:S(2)}, u32[]{:S(2)}) collective-permute-start(f32[640,128]{1,0:T(8,128)S(1)} %shard_map.49), channel_id=1, source_target_pairs={{0,127},{1,2},{2,1},{3,4},{4,3},{5,6},{6,5},{7,8},{8,7},{9,10},{10... | collective-permute-start | bytes 983048 | tf_op jit(solution)/shard_map/ppermute | solution.py:484
  19.9 0.8 %shard_map.47 = (f32[10,64,128]{2,1,0:T(8,128)S(1)}, f32[7,16,128]{2,1,0:T(8,128)S(1)}, f32[16,128]{1,0:T(8,128)S(1)}, f32[8,128]{1,0:T(8,128)S(1)}, f32[7,16,12...) custom-call(f32[760,128]{1,0:T(8,128)S(1)} %get-tuple-element.29.pack_ref), custom_call_target="tpu_custom_call" | custom-call | flops 409600 | bytes 1015808 | tf_op jit(solution)/shard_map/pallas_call | solution.py:41
  20.7 0.0 collective-permute-done.far_ref.pack_ref
  20.7 1.6 %shard_map.48 = (f32[680,128]{1,0:T(8,128)S(1)}, f32[10,64,128]{2,1,0:T(8,128)S(1)}, f32[7,16,128]{2,1,0:T(8,128)S(1)}, f32[16,128]{1,0:T(8,128)S(1)}, f32[8,128]{1,0:T(8,128)S(1)}) custom-call(f32[760,128]{1,0:T(8,128)S(1)} %get-tuple-element.29.pack_ref, f32[10,64,128]{2,1,0:T(8,128)S(1)} %get-tuple-element.30.base_ref, ...), custom_call_target="tpu_custom_call" | custom-call | flops 3276800 | bytes 2576384 | tf_op jit(solution)/shard_map/pallas_call | solution.py:41
  22.4 3.4 %all-gather.1 = f32[1360,128]{1,0:T(8,128)S(1)} all-gather(f32[680,128]{1,0:T(8,128)S(1)} %get-tuple-element.38.buf_ref), channel_id=3, replica_groups=mesh['line'=4,'z'=8,'y'=8,'core'=2] {'core'}, dimensions={0}, use_global_device_ids=true | all-gather | bytes 1044480 | tf_op jit(solution)/shard_map/all_gather | solution.py:492
  25.8 0.9 %collective-permute-done.1.next_ref = f32[640,128]{1,0:T(8,128)S(1)} collective-permute-done((f32[640,128]{1,0:T(8,128)S(1)}, f32[640,128]{1,0:T(8,128)S(1)}, u32[]{:S(2)}, u32[]{:S(2)}) %collective-permute-start.1) | collective-permute-done | bytes 327712 | tf_op jit(solution)/shard_map/ppermute | solution.py:484
  26.7 1.1 %shard_map.50 = (f32[640,128]{1,0:T(8,128)S(1)}, f32[4,56,128]{2,1,0:T(8,128)S(1)}) custom-call(f32[760,128]{1,0:T(8,128)S(1)} %collective-permute-done.far_ref.pack_ref, f32[10,64,128]{2,1,0:T(8,128)S(1)} %get-tuple-element.35.base_ref, f32[640,128]{1,0:T(8,128)S(1)} %get-tuple-element.28.start_ref, f32[640,128]{1,0:T(8,128)S(1)} %collective-permute-done.1.next_ref, ...), custom_call_target="tpu_custom_call" | custom-call | flops 3276800 | bytes 2920448 | tf_op jit(solution)/shard_map/pallas_call | solution.py:41
  27.8 8.6 %all_to_all.20.r_ref = f32[4,56,128]{2,1,0:T(8,128)S(1)} all-to-all(f32[4,56,128]{2,1,0:T(8,128)S(1)} %get-tuple-element.39), channel_id=1, replica_groups=mesh['line'=4,'z'=8,'y'=8,'core'=2] {'line'}, dimensions={0} | all-to-all | bytes 229376 | tf_op jit(solution)/shard_map/all_to_all | solution.py:454
  36.4 2.2 %shard_map.51 = (f32[10,64,128]{2,1,0:T(8,128)S(1)}, f32[8,32,128]{2,1,0:T(8,128)S(1)}) custom-call(f32[760,128]{1,0:T(8,128)S(1)} %get-tuple-element.29.pack_ref, f32[4,56,128]{2,1,0:T(8,128)S(1)} %all_to_all.20.r_ref, f32[680,128]{1,0:T(8,128)S(1)} %get-tuple-element.38.buf_ref, f32[2,680,128]{2,1,0:T(8,128)S(1)} %bitcast.7, ...), custom_call_target="tpu_custom_call" | custom-call | flops 6553600 | bytes 2568192 | tf_op jit(solution)/shard_map/pallas_call | solution.py:41
  38.5 12.4 %all_to_all.21.r_ref = f32[8,32,128]{2,1,0:T(8,128)S(1)} all-to-all(f32[8,32,128]{2,1,0:T(8,128)S(1)} %get-tuple-element.44), channel_id=1, replica_groups=mesh['line'=4,'z'=8,'y'=8,'core'=2] {'line','core'}, dimensions={0} | all-to-all | bytes 262144 | tf_op jit(solution)/shard_map/all_to_all | solution.py:454
  51.0 0.6 shard_map.52
  51.6 9.3 %all_to_all.22.r_ref = f32[8,9,1,128]{3,2,1,0:T(1,128)S(1)} all-to-all(f32[8,9,1,128]{3,2,1,0:T(1,128)S(1)} %get-tuple-element.45), channel_id=1, replica_groups=mesh['line'=4,'z'=8,'y'=8,'core'=2] {'y'}, dimensions={0} | all-to-all | bytes 73728 | tf_op jit(solution)/shard_map/all_to_all | solution.py:454
  60.9 12.4 %all_to_all.23.refs_0_ = f32[16,9,1,128]{3,2,1,0:T(1,128)S(1)} all-to-all(f32[16,9,1,128]{3,2,1,0:T(1,128)S(1)} %shard_map.53), channel_id=1, replica_groups=mesh['line'=4,'z'=8,'y'=8,'core'=2] {'z','core'}, dimensions={0} | all-to-all | bytes 147456 | tf_op jit(solution)/shard_map/all_to_all | solution.py:454
  73.3 3.0 %shard_map.54 = f32[10,64,128]{2,1,0:T(8,128)} custom-call(f32[16,9,1,128]{3,2,1,0:T(1,128)S(1)} %all_to_all.23.refs_0_, f32[10,64,128]{2,1,0:T(8,128)S(1)} %get-tuple-element.46.refs_1_, f32[16,128]{1,0:T(8,128)S(1)} %get-tuple-element.47.refs_2_, f32[16,128]{1,0:T(8,128)S(1)} %get-tuple-element.48.refs_3_), custom_call_target="tpu_custom_call" | custom-call | flops 6553600 | bytes 745472 | tf_op jit(solution)/shard_map/pallas_call | solution.py:41
  (2 shorter events, 0.1 us)
Async XLA Ops:
  1.3 19.5 %collective-permute-start = (f32[760,128]{1,0:T(8,128)S(1)}, f32[760,128]{1,0:T(8,128)S(1)}, u32[]{:S(2)}, u32[]{:S(2)}) collective-permute-start(f32[760,128]{1,0:T(8,128)S(1)} %get-tuple-element.29.pack_ref), channel_id=1, source_target_pairs={{0,127},{1,2},{2,1},{3,4},{4,3},{5,6},{6,5},{7,8},{8,7},{9,10},{10... | collective-permute-start | bytes 1167368 | tf_op jit(solution)/shard_map/ppermute | solution.py:480
  18.0 8.7 %collective-permute-start.1 = (f32[640,128]{1,0:T(8,128)S(1)}, f32[640,128]{1,0:T(8,128)S(1)}, u32[]{:S(2)}, u32[]{:S(2)}) collective-permute-start(f32[640,128]{1,0:T(8,128)S(1)} %shard_map.49), channel_id=1, source_target_pairs={{0,127},{1,2},{2,1},{3,4},{4,3},{5,6},{6,5},{7,8},{8,7},{9,10},{10... | collective-permute-start | bytes 983048 | tf_op jit(solution)/shard_map/ppermute | solution.py:484

commit v7 on v6

--- a/solution.py
+++ b/solution.py
@@ -79,34 +79,6 @@
     return (col == jnp.where(row < 16, row * LANES + LANES - 1, (row - 16) * LANES)).astype(
         jnp.bfloat16
     )
-
-
-def start_body(f_hbm, b_hbm, w_hbm, c_hbm, s_ref, pack_ref, f_ref, b_ref, w_ref, c_ref, sems):
-    copies = [
-        pltpu.make_async_copy(src, dst, sems.at[i])
-        for i, (src, dst) in enumerate(
-            ((f_hbm, f_ref), (b_hbm, b_ref), (w_hbm, w_ref), (c_hbm, c_ref))
-        )
-    ]
-    for copy in copies:
-        copy.start()
-    for copy in copies:
-        copy.wait()
-    n, cols, _ = f_ref.shape
-    for g in range(0, cols, 16):
-        vals = [f_ref[m, g : g + 16, :] for m in range(n)]
-        for k in range(n):
-            v = apply_rows(lambda m: b_ref[k, m], n, lambda m: vals[m])
-            s_ref[k * cols + g : k * cols + g + 16, :] = v
-            pack_ref[k * cols + g : k * cols + g + 16, :] = v
-    at = n * cols
-    for k in range(n):
-        for m in range(n):
-            pack_ref[at + k * n + m : at + k * n + m + 1, :] = c_ref[m] * b_ref[k, m]
-    at += n * n
-    for i in range(2):
-        for k in range(n):
-            pack_ref[at + i * n + k : at + i * n + k + 1, :] = w_ref[i, k]
 
 
 def rate_tables(up, down):
@@ -135,34 +107,49 @@
     return ps, qs, pre, suf, table
 
 
-def sweep_tables(n, cols, pack_ref, base_ref, up_ref, pre_ref, row_ref):
-    at = n * cols + n * n
-    up, down = pack_ref[at : at + n, :], pack_ref[at + n : at + 2 * n, :]
-    ps, qs, pre, suf, table = rate_tables(up, down)
-    for i, p in enumerate(ps):
+def start_body(
+    f_hbm, b_hbm, w_hbm, c_hbm, s_ref, pack_ref, f_ref, b_ref, w_ref, c_ref, sems
+):
+    n, cols, _ = f_ref.shape
+    few = [(w_hbm, w_ref), (c_hbm, c_ref), (b_hbm, b_ref)]
+    few += [(f_hbm.at[:, g : g + 16, :], f_ref.at[:, g : g + 16, :]) for g in range(0, cols, 16)]
+    copies = [pltpu.make_async_copy(src, dst, sems.at[i]) for i, (src, dst) in enumerate(few)]
+    for copy in copies:
+        copy.start()
+    size = n * cols
+    at = size + n * n
+    for copy in copies[:3]:
+        copy.wait()
+    for k in range(n):
+        for m in range(n):
+            pack_ref[size + k * n + m : size + k * n + m + 1, :] = c_ref[m] * b_ref[k, m]
+    for i in range(2):
+        for k in range(n):
+            pack_ref[at + i * n + k : at + i * n + k + 1, :] = w_ref[i, k]
+    for i, g in enumerate(range(0, cols, 16)):
+        copies[3 + i].wait()
+        vals = [f_ref[m, g : g + 16, :] for m in range(n)]
+        for k in range(n):
+            v = apply_rows(lambda m: b_ref[k, m], n, lambda m: vals[m])
+            s_ref[k * cols + g : k * cols + g + 16, :] = v
+            pack_ref[k * cols + g : k * cols + g + 16, :] = v
+
+
+def side_body(pack_ref, up_ref, down_ref, suf_ref, tab_ref, ext_ref):
+    n = ext_ref.shape[1] // LANES
+    at = pack_ref.shape[0] - 2 * n
+    ps, qs, pre, suf, table = rate_tables(pack_ref[at : at + n, :], pack_ref[at + n : at + 2 * n, :])
+    tab_ref[0:8, :] = table
+    tab_ref[8 : 8 + n, :] = pre
+    for i, (p, q) in enumerate(zip(ps, qs)):
         up_ref[i, 0:n, :] = p
-    pre_ref[0:n, :] = pre
-    row_ref[...] = table
-    inner = lane_ids(cols) < LANES - 1
-    for k in range(n):
-        start = pack_ref[k * cols : (k + 1) * cols, :]
-        above = jnp.where(inner, pltpu.roll(start, LANES - 1, 1), 0.0)
-        base_ref[k] = start + down[k : k + 1, :] * above
-    return qs, suf
-
-
-def side_body(pack_ref, base_ref, up_ref, pre_ref, row_ref, down_ref, suf_ref, ext_ref):
-    n, cols, _ = base_ref.shape
-    qs, suf = sweep_tables(n, cols, pack_ref, base_ref, up_ref, pre_ref, row_ref)
-    for i, q in enumerate(qs):
         down_ref[i, 0:n, :] = q
     suf_ref[0:n, :] = suf
     place = row_ids(32)
     first = (lane_ids(32) == 0).astype(F32)
     for k in range(n):
         block = jnp.where(place == k, jnp.broadcast_to(suf[k : k + 1, :], (32, LANES)), 0.0)
-        block = jnp.where(place == 16 + k, first, block)
-        ext_ref[:, k * LANES : (k + 1) * LANES] = block
+        ext_ref[:, k * LANES : (k + 1) * LANES] = jnp.where(place == 16 + k, first, block)
 
 
 def other_body(near_ref, out_ref):
@@ -176,21 +163,27 @@
     )
 
 
-def rise(pack_ref, base_ref, one, two, up_ref, loc_ref, h_ref, a_ref):
-    n, cols, _ = base_ref.shape
+def rise(pack_ref, one, two, up_ref, loc_ref, h_ref, a_ref, between=lambda k: None):
+    n, cols, _ = h_ref.shape
     for m in range(n):
         rows = slice(m * cols, (m + 1) * cols)
         h_ref[m] = one(rows) + two(rows)
-    first = lane_ids(16) == 0
-    for k in range(n):
+    lane = lane_ids(16)
+    first, inner = lane == 0, lane < LANES - 1
+    for k in range(n):
+        at = n * cols + n * n + n + k
+        fall = pack_ref[at : at + 1, :]
+        between(k)
         for g in range(cols // 16):
             rows = slice(16 * g, 16 * g + 16)
-            v = base_ref[k, rows, :] + coupled(pack_ref, h_ref, k, n, rows)
+            wide = slice(k * cols + 16 * g, k * cols + 16 * g + 16)
+            start = pack_ref[wide, :]
+            above = jnp.where(inner, pltpu.roll(start, LANES - 1, 1), 0.0)
+            v = start + fall * above + coupled(pack_ref, h_ref, k, n, rows)
             for i, d in enumerate(STEPS):
                 v = v + up_ref[i, k : k + 1, :] * pltpu.roll(v, d, 1)
-            wide = slice(k * cols + 16 * g, k * cols + 16 * g + 16)
             loc_ref[wide, :] = v
-            a_ref[rows, k * LANES : (k + 1) * LANES] = jnp.where(first, pack_ref[wide, :], v)
+            a_ref[rows, k * LANES : (k + 1) * LANES] = jnp.where(first, start, v)
     ends = pick(a_ref[...], end_mask(n))
     ends = jnp.concatenate([ends, jnp.zeros((cols, LANES - 32), F32)], axis=1)
     pay = ends[0:16, :]
@@ -199,36 +192,52 @@
     return pay
 
 
-def own_body(
-    pack_ref, base_ref, far_ref, near_ref, up_ref, row_ref, pre_ref,
-    buf_ref, fbase_ref, fup_ref, fpre_ref, frow_ref, h_ref, a_ref,
+def own_body(pack_ref, far_ref, near_ref, up_ref, tab_ref, buf_ref, fup_ref, ftab_ref, h_ref, a_ref):
+    n, cols, _ = h_ref.shape
+    size = n * cols
+    at = size + n * n
+    other = 1 - lax.axis_index("core")
+    up, down = far_ref[at : at + n, :], far_ref[at + n : at + 2 * n, :]
+    lane = lane_ids(n)
+    state = [jnp.where(lane >= 1, up, 0.0), up]
+
+    def far_table(k):
+        if k < len(STEPS):
+            d = STEPS[k]
+            p, pre = state
+            fup_ref[k, 0:n, :] = p
+            state[0] = p * pltpu.roll(p, d, 1)
+            state[1] = jnp.where(lane >= d, pre * pltpu.roll(pre, d, 1), pre)
+
+    buf_ref[size : size + 16, :] = rise(
+        pack_ref, lambda rows: far_ref[rows, :], lambda rows: near_ref[other, rows, :],
+        up_ref, buf_ref, h_ref, a_ref, far_table,
+    )
+    buf_ref[size + 16 : size + 40, :] = tab_ref[...]
+    pre = state[1]
+    ftab_ref[8 : 8 + n, :] = pre
+    table = jnp.zeros((8, LANES), F32)
+    at, row = lane_ids(8), row_ids(8)
+    for k in range(n):
+        mine = jnp.where(row == 0, pre[k : k + 1, LANES - 1 : LANES], down[k : k + 1, LANES - 1 : LANES])
+        table = jnp.where(lax.rem(at, 16) == k, mine, table)
+    ftab_ref[0:8, :] = table
+
+
+def far_body(
+    pack_ref, start_ref, next_ref, up_ref, tab_ref, buf_ref, both_ref, loc_ref, pay_ref, h_ref, a_ref
 ):
-    n, cols, _ = base_ref.shape
+    n, cols, _ = h_ref.shape
     size = n * cols
     other = 1 - lax.axis_index("core")
-    sweep_tables(n, cols, far_ref, fbase_ref, fup_ref, fpre_ref, frow_ref)
-    buf_ref[size : size + 16, :] = rise(
-        pack_ref, base_ref, lambda rows: far_ref[rows, :], lambda rows: near_ref[other, rows, :],
-        up_ref, buf_ref, h_ref, a_ref,
-    )
-    buf_ref[size + 16 : size + 24, :] = row_ref[...]
-    buf_ref[size + 24 : size + 40, :] = pre_ref[...]
-
-
-def far_body(
-    pack_ref, base_ref, start_ref, next_ref, up_ref, row_ref, buf_ref, both_ref,
-    loc_ref, pay_ref, h_ref, a_ref,
-):
-    size = base_ref.shape[0] * base_ref.shape[1]
-    other = 1 - lax.axis_index("core")
     pay = rise(
-        pack_ref, base_ref, lambda rows: start_ref[rows, :], lambda rows: next_ref[rows, :],
+        pack_ref, lambda rows: start_ref[rows, :], lambda rows: next_ref[rows, :],
         up_ref, loc_ref, h_ref, a_ref,
     )
     own, near = buf_ref[size : size + 24, :], both_ref[other, size : size + 24, :]
     row = row_ids(8)
     table = jnp.where(row < 2, own[16:24, :], pltpu.roll(near[16:24, :], 2, 0))
-    table = jnp.where(row < 4, table, pltpu.roll(row_ref[...], 4, 0))
+    table = jnp.where(row < 4, table, pltpu.roll(tab_ref[0:8, :], 4, 0))
     for peer in range(pay_ref.shape[0]):
         pay_ref[peer, 0:16, :] = own[0:16, :]
         pay_ref[peer, 16:32, :] = near[0:16, :]
@@ -283,7 +292,7 @@
 
 
 def down_body(
-    pack_ref, r_ref, buf_ref, both_ref, floc_ref, fpre_ref, down_ref, ext_ref, row_ref,
+    pack_ref, r_ref, buf_ref, both_ref, floc_ref, ftab_ref, down_ref, ext_ref,
     loc_ref, pay_ref, h_ref, a_ref,
 ):
     n, cols, _ = loc_ref.shape
@@ -297,7 +306,7 @@
     last, first = lane == LANES - 1, lane == 0
     for m in range(n):
         npre = both_ref[other, size + 24 + m : size + 25 + m, :]
-        fpre = fpre_ref[m : m + 1, :]
+        fpre = ftab_ref[8 + m : 9 + m, :]
         for g in range(cols // 16):
             rows, at = slice(m * cols + 16 * g, m * cols + 16 * g + 16), 32 * g + m
             v = both_ref[other, rows, :] + floc_ref[rows, :]
@@ -330,7 +339,7 @@
         block, extra = blocks[peer % NCORE]
         pay_ref[peer, 0:8, :] = block
         pay_ref[peer, 8:24, :] = edges
-        pay_ref[peer, 24:32, :] = jnp.where(row_ids(8) == 4, extra, row_ref[...])
+        pay_ref[peer, 24:32, :] = jnp.where(row_ids(8) == 4, extra, buf_ref[size + 16 : size + 24, :])
 
 
 def line_body(r_ref, gram_ref, entry_ref, left_ref, right_ref):
@@ -469,33 +478,32 @@
     wide = pltpu.VMEM((cols, n * pts), F32)
     tall = pltpu.VMEM((cols + 32, n * pts), F32)
 
-    inputs = [pltpu.VMEM(a.shape, F32) for a in (f, b, w)]
+    inputs = [pltpu.VMEM(a.shape, F32) for a in (f, b, w)] + [pltpu.SMEM(c.shape, F32)]
+    steps = (len(STEPS), 16, pts)
     start, pack = call(
         start_body,
         [(size, pts), (size + n * n + 2 * n, pts)],
         work,
-        inputs + [pltpu.SMEM(c.shape, F32), pltpu.SemaphoreType.DMA((4,))],
+        inputs + [pltpu.SemaphoreType.DMA((3 + cols // 16,))],
         HBM,
     )(f, b, w, c)
     fpack = lax.ppermute(pack, TILE, across)
     near = lax.all_gather(start, "core")
-    steps, rows16 = (len(STEPS), 16, pts), (16, pts)
-    tables = [field, steps, rows16, (8, pts)]
+    tables_of, near = lax.optimization_barrier((pack, near))
     beyond = lax.ppermute(call(other_body, (size, pts))(near), TILE, across)
-    tables_of, near = lax.optimization_barrier((pack, near))
-    base, up, pre, row, down, suf, ext = call(
-        side_body, tables + [steps, rows16, (32, n * pts)], work // 4
+    up, down, suf, tab, ext = call(
+        side_body, [steps, steps, (16, pts), (24, pts), (32, n * pts)], work // 4
     )(tables_of)
-    buf, fbase, fup, fpre, frow = call(
-        own_body, [(size + 40, pts)] + tables, 2 * work, [scratch, wide]
-    )(pack, base, fpack, near, up, row, pre)
+    buf, fup, ftab = call(own_body, [(size + 40, pts), steps, (24, pts)], 2 * work, [scratch, wide])(
+        pack, fpack, near, up, tab
+    )
     both = lax.all_gather(buf, "core")
     floc, pay = call(far_body, [(size, pts), (peers, 56, pts)], 2 * work, [scratch, wide])(
-        fpack, fbase, start, beyond, fup, frow, buf, both
+        fpack, start, beyond, fup, ftab, buf, both
     )
     got = exchange(pay, "line")
     loc, pay = call(down_body, [field, (peers * NCORE, 32, pts)], 4 * work, [scratch, tall])(
-        pack, got, buf, both, floc, fpre, down, ext, row
+        pack, got, buf, both, floc, ftab, down, ext
     )
     side = pltpu.VMEM((cols, NCORE * pts), F32)
     part = (9, 1, pts)

time: 76.6 us -> 76.6 us (level)
  no operation moved by 1% of the time
where the time goes in v7:
time: 76.6 us; the launch traced here: 76.3 us
  blocking collectives  58.2 us (76%)
  Pallas kernels  10.1 us (13%)
  starting transfers between devices  6.5 us (8%)
  waiting for transfers between devices  1.47 us (2%)
    all_to_all x4, blocking collectives, exchange(): return lax.all_to_all(value, axis, 0, 0, tiled=True)  42.7 us
    all_gather x1, blocking collectives, local(): near = lax.all_gather(start, 'core')  12.1 us
    pallas_call x9, Pallas kernels, run(): pl.pallas_call(body, out_shape=shapes if many else shapes[0], in_specs=[s...  10.1 us
    ppermute x1, starting transfers between devices, local(): fpack = lax.ppermute(pack, TILE, across)  4.58 us
    all_gather x1, blocking collectives, local(): both = lax.all_gather(buf, 'core')  3.38 us
    ppermute x1, starting transfers between devices, local(): beyond = lax.ppermute(call(other_body, (size, pts))(near), TILE, across)  1.92 us
  transfers between devices with their start and end apart: 2, of which 1 were waited for; matrix products, arithmetic and copies ran while one was open for 0% of the time, Pallas kernels for 3%

profile of v7, /device:TPU:1, one launch (start us, length us, event | category | flops | bytes accessed | tf_op | source)
XLA Modules:
  0.0 76.3 jit_solution(9588775239593461660)
XLA Ops:
  0.0 1.2 %shard_map.46 = (f32[640,128]{1,0:T(8,128)S(1)}, f32[760,128]{1,0:T(8,128)S(1)}) custom-call(f32[10,64,128]{2,1,0:T(8,128)} %bitcast.10, f32[10,10,1,128]{3,2,1,0:T(1,128)} %b_hbm.1, f32[2,10,1,128]{3,2,1,0:T(1,128)} %w_hbm.1, f32[10]{0:T(128)} %c_hbm.1), custom_call_target="tpu_custom_call" | custom-call | flops 1638400 | bytes 1105960 | tf_op jit(solution)/shard_map/pallas_call | solution.py:41
  1.2 4.6 %collective-permute-start = (f32[760,128]{1,0:T(8,128)S(1)}, f32[760,128]{1,0:T(8,128)S(1)}, u32[]{:S(2)}, u32[]{:S(2)}) collective-permute-start(f32[760,128]{1,0:T(8,128)S(1)} %get-tuple-element.26.pack_ref), channel_id=1, source_target_pairs={{0,127},{1,2},{2,1},{3,4},{4,3},{5,6},{6,5},{7,8},{8,7},{9,10},{10... | collective-permute-start | bytes 1167368 | tf_op jit(solution)/shard_map/ppermute | solution.py:490
  5.8 12.1 %all-gather = f32[1280,128]{1,0:T(8,128)S(1)} all-gather(f32[640,128]{1,0:T(8,128)S(1)} %get-tuple-element.24.start_ref), channel_id=2, replica_groups=mesh['line'=4,'z'=8,'y'=8,'core'=2] {'core'}, dimensions={0}, use_global_device_ids=true | all-gather | bytes 983040 | tf_op jit(solution)/shard_map/all_gather | solution.py:491
  18.0 1.9 %collective-permute-start.1 = (f32[640,128]{1,0:T(8,128)S(1)}, f32[640,128]{1,0:T(8,128)S(1)}, u32[]{:S(2)}, u32[]{:S(2)}) collective-permute-start(f32[640,128]{1,0:T(8,128)S(1)} %shard_map.47), channel_id=1, source_target_pairs={{0,127},{1,2},{2,1},{3,4},{4,3},{5,6},{6,5},{7,8},{8,7},{9,10},{10... | collective-permute-start | bytes 983048 | tf_op jit(solution)/shard_map/ppermute | solution.py:493
  19.9 0.6 shard_map.48
  20.5 0.0 collective-permute-done.far_ref.pack_ref
  20.5 1.3 %shard_map.49 = (f32[680,128]{1,0:T(8,128)S(1)}, f32[7,16,128]{2,1,0:T(8,128)S(1)}, f32[24,128]{1,0:T(8,128)S(1)}) custom-call(f32[760,128]{1,0:T(8,128)S(1)} %get-tuple-element.26.pack_ref, f32[760,128]{1,0:T(8,128)S(1)} %collective-permute-done.far_ref.pack_ref, f32[2,640,128]{2,1,0:T(8,128)S(1)} %bitcast.9, f32[7,16,128]{2,1,0:T(8,128)S(1)} %get-tuple-element.27.up_ref, ...), custom_call_target="tpu_custom_call" | custom-call | flops 3276800 | bytes 1921024 | tf_op jit(solution)/shard_map/pallas_call | solution.py:41
  21.8 3.4 %all-gather.1 = f32[1360,128]{1,0:T(8,128)S(1)} all-gather(f32[680,128]{1,0:T(8,128)S(1)} %get-tuple-element.31.buf_ref), channel_id=3, replica_groups=mesh['line'=4,'z'=8,'y'=8,'core'=2] {'core'}, dimensions={0}, use_global_device_ids=true | all-gather | bytes 1044480 | tf_op jit(solution)/shard_map/all_gather | solution.py:500
  25.2 1.5 %collective-permute-done.1.next_ref = f32[640,128]{1,0:T(8,128)S(1)} collective-permute-done((f32[640,128]{1,0:T(8,128)S(1)}, f32[640,128]{1,0:T(8,128)S(1)}, u32[]{:S(2)}, u32[]{:S(2)}) %collective-permute-start.1) | collective-permute-done | bytes 327712 | tf_op jit(solution)/shard_map/ppermute | solution.py:493
  26.7 1.2 %shard_map.50 = (f32[640,128]{1,0:T(8,128)S(1)}, f32[4,56,128]{2,1,0:T(8,128)S(1)}) custom-call(f32[760,128]{1,0:T(8,128)S(1)} %collective-permute-done.far_ref.pack_ref, f32[640,128]{1,0:T(8,128)S(1)} %get-tuple-element.24.start_ref, f32[640,128]{1,0:T(8,128)S(1)} %collective-permute-done.1.next_ref, f32[7,16,128]{2,1,0:T(8,128)S(1)} %get-tuple-element.29.up_ref, ...), custom_call_target="tpu_custom_call" | custom-call | flops 3276800 | bytes 2600960 | tf_op jit(solution)/shard_map/pallas_call | solution.py:41
  27.8 8.5 %all_to_all.20.r_ref = f32[4,56,128]{2,1,0:T(8,128)S(1)} all-to-all(f32[4,56,128]{2,1,0:T(8,128)S(1)} %get-tuple-element.32), channel_id=1, replica_groups=mesh['line'=4,'z'=8,'y'=8,'core'=2] {'line'}, dimensions={0} | all-to-all | bytes 229376 | tf_op jit(solution)/shard_map/all_to_all | solution.py:463
  36.4 2.1 %shard_map.51 = (f32[10,64,128]{2,1,0:T(8,128)S(1)}, f32[8,32,128]{2,1,0:T(8,128)S(1)}) custom-call(f32[760,128]{1,0:T(8,128)S(1)} %get-tuple-element.26.pack_ref, f32[4,56,128]{2,1,0:T(8,128)S(1)} %all_to_all.20.r_ref, f32[680,128]{1,0:T(8,128)S(1)} %get-tuple-element.31.buf_ref, f32[2,680,128]{2,1,0:T(8,128)S(1)} %bitcast.7, ...), custom_call_target="tpu_custom_call" | custom-call | flops 6553600 | bytes 2568192 | tf_op jit(solution)/shard_map/pallas_call | solution.py:41
  38.5 12.4 %all_to_all.21.r_ref = f32[8,32,128]{2,1,0:T(8,128)S(1)} all-to-all(f32[8,32,128]{2,1,0:T(8,128)S(1)} %get-tuple-element.36), channel_id=1, replica_groups=mesh['line'=4,'z'=8,'y'=8,'core'=2] {'line','core'}, dimensions={0} | all-to-all | bytes 262144 | tf_op jit(solution)/shard_map/all_to_all | solution.py:463
  51.0 0.6 shard_map.52
  51.5 9.3 %all_to_all.22.r_ref = f32[8,9,1,128]{3,2,1,0:T(1,128)S(1)} all-to-all(f32[8,9,1,128]{3,2,1,0:T(1,128)S(1)} %get-tuple-element.37), channel_id=1, replica_groups=mesh['line'=4,'z'=8,'y'=8,'core'=2] {'y'}, dimensions={0} | all-to-all | bytes 73728 | tf_op jit(solution)/shard_map/all_to_all | solution.py:463
  60.9 12.4 %all_to_all.23.refs_0_ = f32[16,9,1,128]{3,2,1,0:T(1,128)S(1)} all-to-all(f32[16,9,1,128]{3,2,1,0:T(1,128)S(1)} %shard_map.53), channel_id=1, replica_groups=mesh['line'=4,'z'=8,'y'=8,'core'=2] {'z','core'}, dimensions={0} | all-to-all | bytes 147456 | tf_op jit(solution)/shard_map/all_to_all | solution.py:463
  73.3 3.0 %shard_map.54 = f32[10,64,128]{2,1,0:T(8,128)} custom-call(f32[16,9,1,128]{3,2,1,0:T(1,128)S(1)} %all_to_all.23.refs_0_, f32[10,64,128]{2,1,0:T(8,128)S(1)} %get-tuple-element.38.refs_1_, f32[16,128]{1,0:T(8,128)S(1)} %get-tuple-element.39.refs_2_, f32[16,128]{1,0:T(8,128)S(1)} %get-tuple-element.40.refs_3_), custom_call_target="tpu_custom_call" | custom-call | flops 6553600 | bytes 745472 | tf_op jit(solution)/shard_map/pallas_call | solution.py:41
  (2 shorter events, 0.1 us)
Async XLA Ops:
  1.2 19.3 %collective-permute-start = (f32[760,128]{1,0:T(8,128)S(1)}, f32[760,128]{1,0:T(8,128)S(1)}, u32[]{:S(2)}, u32[]{:S(2)}) collective-permute-start(f32[760,128]{1,0:T(8,128)S(1)} %get-tuple-element.26.pack_ref), channel_id=1, source_target_pairs={{0,127},{1,2},{2,1},{3,4},{4,3},{5,6},{6,5},{7,8},{8,7},{9,10},{10... | collective-permute-start | bytes 1167368 | tf_op jit(solution)/shard_map/ppermute | solution.py:490
  18.0 8.7 %collective-permute-start.1 = (f32[640,128]{1,0:T(8,128)S(1)}, f32[640,128]{1,0:T(8,128)S(1)}, u32[]{:S(2)}, u32[]{:S(2)}) collective-permute-start(f32[640,128]{1,0:T(8,128)S(1)} %shard_map.47), channel_id=1, source_target_pairs={{0,127},{1,2},{2,1},{3,4},{4,3},{5,6},{6,5},{7,8},{8,7},{9,10},{10... | collective-permute-start | bytes 983048 | tf_op jit(solution)/shard_map/ppermute | solution.py:493

commit v8 on v7

--- a/solution.py
+++ b/solution.py
@@ -334,51 +334,52 @@
     for g in range(cols // 16):
         moved = pltpu.roll(total[16 * g : 16 * g + 16, :], (32 * g + 64) % LANES, 1)
         edges = jnp.where(lane // 32 == g, moved, edges)
-    blocks = packed_blocks(total)
+    (one, _), (two, extra) = packed_blocks(total)
     for peer in range(pay_ref.shape[0]):
-        block, extra = blocks[peer % NCORE]
-        pay_ref[peer, 0:8, :] = block
-        pay_ref[peer, 8:24, :] = edges
-        pay_ref[peer, 24:32, :] = jnp.where(row_ids(8) == 4, extra, buf_ref[size + 16 : size + 24, :])
+        pay_ref[peer, 0:8, :] = one
+        pay_ref[peer, 8:16, :] = two
+        pay_ref[peer, 16:32, :] = edges
+        pay_ref[peer, 32:40, :] = jnp.where(row_ids(8) == 4, extra, buf_ref[size + 16 : size + 24, :])
 
 
 def line_body(r_ref, gram_ref, entry_ref, left_ref, right_ref):
-    peers = r_ref.shape[0] // NCORE
+    peers = r_ref.shape[0]
     cols = left_ref.shape[0]
-    mine, core = lax.axis_index("line"), lax.axis_index("core")
+    mine = lax.axis_index("line")
     lane = lane_ids(16)
     first = lane % 32 < 16
     zero = jnp.zeros((16, LANES), F32)
     entry = zero
-    for station in range(NCORE):
-        state = zero
-        left = [zero] * (cols // 16)
-        right = [zero] * (cols // 16)
-        for at in range(peers - 2, -1, -1):
-            above, here = NCORE * (at + 1) + station, NCORE * at + station
-            state = r_ref[above, 26:27, :] * state + r_ref[above, 8:24, :]
-            entry = jnp.where((mine == at) & (core == station), state, entry)
-            back = pltpu.roll(state, LANES - 16, 1)
-            cross = r_ref[here, 8:24, :] + (0.5 * r_ref[here, 27:28, :]) * back
-            a = jnp.where(first, cross, state)
-            b = jnp.where(first, back, pltpu.roll(cross, 16, 1))
-            for g in range(cols // 16):
-                shift = (32 * (at - g)) % LANES
-                left[g] = jnp.where(lane // 32 == at, pltpu.roll(a, shift, 1), left[g])
-                right[g] = jnp.where(lane // 32 == at, pltpu.roll(b, shift, 1), right[g])
+    state = zero
+    left = [zero] * (cols // 16)
+    right = [zero] * (cols // 16)
+    for at in range(peers - 2, -1, -1):
+        state = r_ref[at + 1, 34:35, :] * state + r_ref[at + 1, 16:32, :]
+        entry = jnp.where(mine == at, state, entry)
+        back = pltpu.roll(state, LANES - 16, 1)
+        cross = r_ref[at, 16:32, :] + (0.5 * r_ref[at, 35:36, :]) * back
+        a = jnp.where(first, cross, state)
+        b = jnp.where(first, back, pltpu.roll(cross, 16, 1))
         for g in range(cols // 16):
-            rows = slice(16 * g, 16 * g + 16)
-            left_ref[rows, station * LANES : (station + 1) * LANES] = left[g]
-            right_ref[rows, station * LANES : (station + 1) * LANES] = right[g]
+            shift = (32 * (at - g)) % LANES
+            left[g] = jnp.where(lane // 32 == at, pltpu.roll(a, shift, 1), left[g])
+            right[g] = jnp.where(lane // 32 == at, pltpu.roll(b, shift, 1), right[g])
+    for g in range(cols // 16):
+        rows = slice(16 * g, 16 * g + 16)
+        left_ref[rows, :] = left[g]
+        right_ref[rows, :] = right[g]
     fix = dot_nt(left_ref[...], right_ref[...])
     fix = jnp.concatenate([fix, jnp.zeros((cols, LANES - cols), F32)], axis=1)
     (one, none), (two, extra) = packed_blocks(fix)
-    total = jnp.where(core == 0, one, two)
-    extra = jnp.where(core == 0, none, extra)
-    for i in range(r_ref.shape[0]):
-        total = total + r_ref[i, 0:8, :]
-        extra = extra + r_ref[i, 28:29, :]
-    spread_rows(gram_ref, [total[i : i + 1, :] for i in range(8)] + [extra])
+    for at in range(peers):
+        one = one + r_ref[at, 0:8, :]
+        two = two + r_ref[at, 8:16, :]
+        extra = extra + r_ref[at, 36:37, :]
+    for block, row, core in ((one, none, 0), (two, extra, 1)):
+        for peer in range(core, gram_ref.shape[0], NCORE):
+            for i in range(8):
+                gram_ref[peer, i] = block[i : i + 1, :]
+            gram_ref[peer, 8] = row
     entry_ref[...] = entry
 
 
@@ -502,15 +503,15 @@
         fpack, start, beyond, fup, ftab, buf, both
     )
     got = exchange(pay, "line")
-    loc, pay = call(down_body, [field, (peers * NCORE, 32, pts)], 4 * work, [scratch, tall])(
+    loc, pay = call(down_body, [field, (peers, 40, pts)], 4 * work, [scratch, tall])(
         pack, got, buf, both, floc, ftab, down, ext
     )
-    side = pltpu.VMEM((cols, NCORE * pts), F32)
+    side = pltpu.VMEM((cols, pts), F32)
     part = (9, 1, pts)
-    gram, entry = call(line_body, [(NY,) + part, (16, pts)], work // 4, [side, side])(
-        exchange(pay, ("line", "core"))
-    )
-    gram = call(sum_body, (NZ * NCORE,) + part)(exchange(gram, "y"))
+    gram, entry = call(line_body, [(NY * NCORE,) + part, (16, pts)], work // 4, [side, side])(
+        exchange(pay, "line")
+    )
+    gram = call(sum_body, (NZ * NCORE,) + part)(exchange(gram, ("y", "core")))
     gram = exchange(gram, ("z", "core"))
 
     def basis(*refs):

time: 76.6 us -> 76.2 us (level)
  no operation moved by 1% of the time
where the time goes in v8:
time: 76.2 us; the launch traced here: 75.9 us
  blocking collectives  57.8 us (76%)
  Pallas kernels  10.1 us (13%)
  starting transfers between devices  6.5 us (9%)
  waiting for transfers between devices  1.47 us (2%)
    all_to_all x4, blocking collectives, exchange(): return lax.all_to_all(value, axis, 0, 0, tiled=True)  42.3 us
    all_gather x1, blocking collectives, local(): near = lax.all_gather(start, 'core')  12.1 us
    pallas_call x9, Pallas kernels, run(): pl.pallas_call(body, out_shape=shapes if many else shapes[0], in_specs=[s...  10.1 us
    ppermute x1, starting transfers between devices, local(): fpack = lax.ppermute(pack, TILE, across)  4.58 us
    all_gather x1, blocking collectives, local(): both = lax.all_gather(buf, 'core')  3.38 us
    ppermute x1, starting transfers between devices, local(): beyond = lax.ppermute(call(other_body, (size, pts))(near), TILE, across)  1.92 us
  transfers between devices with their start and end apart: 2, of which 1 were waited for; matrix products, arithmetic and copies ran while one was open for 0% of the time, Pallas kernels for 3%

profile of v8, /device:TPU:1, one launch (start us, length us, event | category | flops | bytes accessed | tf_op | source)
XLA Modules:
  0.0 75.9 jit_solution(11960550090379956526)
XLA Ops:
  0.0 1.2 %shard_map.46 = (f32[640,128]{1,0:T(8,128)S(1)}, f32[760,128]{1,0:T(8,128)S(1)}) custom-call(f32[10,64,128]{2,1,0:T(8,128)} %bitcast.10, f32[10,10,1,128]{3,2,1,0:T(1,128)} %b_hbm.1, f32[2,10,1,128]{3,2,1,0:T(1,128)} %w_hbm.1, f32[10]{0:T(128)} %c_hbm.1), custom_call_target="tpu_custom_call" | custom-call | flops 1638400 | bytes 1105960 | tf_op jit(solution)/shard_map/pallas_call | solution.py:41
  1.2 4.6 %collective-permute-start = (f32[760,128]{1,0:T(8,128)S(1)}, f32[760,128]{1,0:T(8,128)S(1)}, u32[]{:S(2)}, u32[]{:S(2)}) collective-permute-start(f32[760,128]{1,0:T(8,128)S(1)} %get-tuple-element.26.pack_ref), channel_id=1, source_target_pairs={{0,127},{1,2},{2,1},{3,4},{4,3},{5,6},{6,5},{7,8},{8,7},{9,10},{10... | collective-permute-start | bytes 1167368 | tf_op jit(solution)/shard_map/ppermute | solution.py:491
  5.8 12.1 %all-gather = f32[1280,128]{1,0:T(8,128)S(1)} all-gather(f32[640,128]{1,0:T(8,128)S(1)} %get-tuple-element.24.start_ref), channel_id=2, replica_groups=mesh['line'=4,'z'=8,'y'=8,'core'=2] {'core'}, dimensions={0}, use_global_device_ids=true | all-gather | bytes 983040 | tf_op jit(solution)/shard_map/all_gather | solution.py:492
  18.0 1.9 %collective-permute-start.1 = (f32[640,128]{1,0:T(8,128)S(1)}, f32[640,128]{1,0:T(8,128)S(1)}, u32[]{:S(2)}, u32[]{:S(2)}) collective-permute-start(f32[640,128]{1,0:T(8,128)S(1)} %shard_map.47), channel_id=1, source_target_pairs={{0,127},{1,2},{2,1},{3,4},{4,3},{5,6},{6,5},{7,8},{8,7},{9,10},{10... | collective-permute-start | bytes 983048 | tf_op jit(solution)/shard_map/ppermute | solution.py:494
  19.9 0.6 shard_map.48
  20.5 0.0 collective-permute-done.far_ref.pack_ref
  20.5 1.3 %shard_map.49 = (f32[680,128]{1,0:T(8,128)S(1)}, f32[7,16,128]{2,1,0:T(8,128)S(1)}, f32[24,128]{1,0:T(8,128)S(1)}) custom-call(f32[760,128]{1,0:T(8,128)S(1)} %get-tuple-element.26.pack_ref, f32[760,128]{1,0:T(8,128)S(1)} %collective-permute-done.far_ref.pack_ref, f32[2,640,128]{2,1,0:T(8,128)S(1)} %bitcast.9, f32[7,16,128]{2,1,0:T(8,128)S(1)} %get-tuple-element.27.up_ref, ...), custom_call_target="tpu_custom_call" | custom-call | flops 3276800 | bytes 1921024 | tf_op jit(solution)/shard_map/pallas_call | solution.py:41
  21.8 3.4 %all-gather.1 = f32[1360,128]{1,0:T(8,128)S(1)} all-gather(f32[680,128]{1,0:T(8,128)S(1)} %get-tuple-element.31.buf_ref), channel_id=3, replica_groups=mesh['line'=4,'z'=8,'y'=8,'core'=2] {'core'}, dimensions={0}, use_global_device_ids=true | all-gather | bytes 1044480 | tf_op jit(solution)/shard_map/all_gather | solution.py:501
  25.2 1.5 %collective-permute-done.1.next_ref = f32[640,128]{1,0:T(8,128)S(1)} collective-permute-done((f32[640,128]{1,0:T(8,128)S(1)}, f32[640,128]{1,0:T(8,128)S(1)}, u32[]{:S(2)}, u32[]{:S(2)}) %collective-permute-start.1) | collective-permute-done | bytes 327712 | tf_op jit(solution)/shard_map/ppermute | solution.py:494
  26.7 1.2 %shard_map.50 = (f32[640,128]{1,0:T(8,128)S(1)}, f32[4,56,128]{2,1,0:T(8,128)S(1)}) custom-call(f32[760,128]{1,0:T(8,128)S(1)} %collective-permute-done.far_ref.pack_ref, f32[640,128]{1,0:T(8,128)S(1)} %get-tuple-element.24.start_ref, f32[640,128]{1,0:T(8,128)S(1)} %collective-permute-done.1.next_ref, f32[7,16,128]{2,1,0:T(8,128)S(1)} %get-tuple-element.29.up_ref, ...), custom_call_target="tpu_custom_call" | custom-call | flops 3276800 | bytes 2600960 | tf_op jit(solution)/shard_map/pallas_call | solution.py:41
  27.8 8.5 %all_to_all.20.r_ref = f32[4,56,128]{2,1,0:T(8,128)S(1)} all-to-all(f32[4,56,128]{2,1,0:T(8,128)S(1)} %get-tuple-element.32), channel_id=1, replica_groups=mesh['line'=4,'z'=8,'y'=8,'core'=2] {'line'}, dimensions={0} | all-to-all | bytes 229376 | tf_op jit(solution)/shard_map/all_to_all | solution.py:464
  36.4 2.1 %shard_map.51 = (f32[10,64,128]{2,1,0:T(8,128)S(1)}, f32[4,40,128]{2,1,0:T(8,128)S(1)}) custom-call(f32[760,128]{1,0:T(8,128)S(1)} %get-tuple-element.26.pack_ref, f32[4,56,128]{2,1,0:T(8,128)S(1)} %all_to_all.20.r_ref, f32[680,128]{1,0:T(8,128)S(1)} %get-tuple-element.31.buf_ref, f32[2,680,128]{2,1,0:T(8,128)S(1)} %bitcast.7, ...), custom_call_target="tpu_custom_call" | custom-call | flops 6553600 | bytes 2519040 | tf_op jit(solution)/shard_map/pallas_call | solution.py:41
  38.5 6.9 %all_to_all.21.r_ref = f32[4,40,128]{2,1,0:T(8,128)S(1)} all-to-all(f32[4,40,128]{2,1,0:T(8,128)S(1)} %get-tuple-element.36), channel_id=1, replica_groups=mesh['line'=4,'z'=8,'y'=8,'core'=2] {'line'}, dimensions={0} | all-to-all | bytes 163840 | tf_op jit(solution)/shard_map/all_to_all | solution.py:464
  45.5 0.5 shard_map.52
  46.0 16.4 %all_to_all.22.r_ref = f32[16,9,1,128]{3,2,1,0:T(1,128)S(1)} all-to-all(f32[16,9,1,128]{3,2,1,0:T(1,128)S(1)} %get-tuple-element.37), channel_id=1, replica_groups=mesh['line'=4,'z'=8,'y'=8,'core'=2] {'y','core'}, dimensions={0} | all-to-all | bytes 147456 | tf_op jit(solution)/shard_map/all_to_all | solution.py:464
  62.4 0.1 shard_map.53
  62.4 10.5 %all_to_all.23.refs_0_ = f32[16,9,1,128]{3,2,1,0:T(1,128)S(1)} all-to-all(f32[16,9,1,128]{3,2,1,0:T(1,128)S(1)} %shard_map.53), channel_id=1, replica_groups=mesh['line'=4,'z'=8,'y'=8,'core'=2] {'z','core'}, dimensions={0} | all-to-all | bytes 147456 | tf_op jit(solution)/shard_map/all_to_all | solution.py:464
  72.9 3.0 %shard_map.54 = f32[10,64,128]{2,1,0:T(8,128)} custom-call(f32[16,9,1,128]{3,2,1,0:T(1,128)S(1)} %all_to_all.23.refs_0_, f32[10,64,128]{2,1,0:T(8,128)S(1)} %get-tuple-element.38.refs_1_, f32[16,128]{1,0:T(8,128)S(1)} %get-tuple-element.39.refs_2_, f32[16,128]{1,0:T(8,128)S(1)} %get-tuple-element.40.refs_3_), custom_call_target="tpu_custom_call" | custom-call | flops 6553600 | bytes 745472 | tf_op jit(solution)/shard_map/pallas_call | solution.py:41
  (1 shorter events, 0.0 us)
Async XLA Ops:
  1.2 19.3 %collective-permute-start = (f32[760,128]{1,0:T(8,128)S(1)}, f32[760,128]{1,0:T(8,128)S(1)}, u32[]{:S(2)}, u32[]{:S(2)}) collective-permute-start(f32[760,128]{1,0:T(8,128)S(1)} %get-tuple-element.26.pack_ref), channel_id=1, source_target_pairs={{0,127},{1,2},{2,1},{3,4},{4,3},{5,6},{6,5},{7,8},{8,7},{9,10},{10... | collective-permute-start | bytes 1167368 | tf_op jit(solution)/shard_map/ppermute | solution.py:491
  18.0 8.7 %collective-permute-start.1 = (f32[640,128]{1,0:T(8,128)S(1)}, f32[640,128]{1,0:T(8,128)S(1)}, u32[]{:S(2)}, u32[]{:S(2)}) collective-permute-start(f32[640,128]{1,0:T(8,128)S(1)} %shard_map.47), channel_id=1, source_target_pairs={{0,127},{1,2},{2,1},{3,4},{4,3},{5,6},{6,5},{7,8},{8,7},{9,10},{10... | collective-permute-start | bytes 983048 | tf_op jit(solution)/shard_map/ppermute | solution.py:494

commit v9 on v8

--- a/solution.py
+++ b/solution.py
@@ -168,15 +168,15 @@
     for m in range(n):
         rows = slice(m * cols, (m + 1) * cols)
         h_ref[m] = one(rows) + two(rows)
-    lane = lane_ids(16)
+    lane = lane_ids(32)
     first, inner = lane == 0, lane < LANES - 1
     for k in range(n):
         at = n * cols + n * n + n + k
         fall = pack_ref[at : at + 1, :]
         between(k)
-        for g in range(cols // 16):
-            rows = slice(16 * g, 16 * g + 16)
-            wide = slice(k * cols + 16 * g, k * cols + 16 * g + 16)
+        for g in range(cols // 32):
+            rows = slice(32 * g, 32 * g + 32)
+            wide = slice(k * cols + 32 * g, k * cols + 32 * g + 32)
             start = pack_ref[wide, :]
             above = jnp.where(inner, pltpu.roll(start, LANES - 1, 1), 0.0)
             v = start + fall * above + coupled(pack_ref, h_ref, k, n, rows)
@@ -317,10 +317,11 @@
         up = pack_ref[size + n * n + k : size + n * n + k + 1, :]
         pre = buf_ref[size + 24 + k : size + 25 + k, :]
         pre = jnp.where(one, 1.0, pltpu.roll(pre, 1, 1))
-        for g in range(cols // 16):
-            rows = slice(16 * g, 16 * g + 16)
-            wide, at = slice(k * cols + 16 * g, k * cols + 16 * g + 16), 32 * g + k
-            below = jnp.where(first, 0.0, pltpu.roll(buf_ref[wide, :], 1, 1)) + pre * mine[:, at : at + 1]
+        for g in range(cols // 32):
+            rows = slice(32 * g, 32 * g + 32)
+            wide, at = slice(k * cols + 32 * g, k * cols + 32 * g + 32), 64 * g + k
+            entry = jnp.concatenate([mine[:, at : at + 1], mine[:, at + 32 : at + 33]], axis=0)
+            below = jnp.where(lane_ids(32) == 0, 0.0, pltpu.roll(buf_ref[wide, :], 1, 1)) + pre * entry
             v = pack_ref[wide, :] + up * below + coupled(pack_ref, h_ref, k, n, rows)
             for i, d in enumerate(STEPS):
                 v = v + down_ref[i, k : k + 1, :] * pltpu.roll(v, LANES - d, 1)

time: 76.2 us -> 76.3 us (level)
  no operation moved by 1% of the time
where the time goes in v9:
time: 76.3 us; the launch traced here: 76 us
  blocking collectives  57.8 us (76%)
  Pallas kernels  10.1 us (13%)
  starting transfers between devices  6.5 us (9%)
  waiting for transfers between devices  1.49 us (2%)
    all_to_all x4, blocking collectives, exchange(): return lax.all_to_all(value, axis, 0, 0, tiled=True)  42.3 us
    all_gather x1, blocking collectives, local(): near = lax.all_gather(start, 'core')  12.1 us
    pallas_call x9, Pallas kernels, run(): pl.pallas_call(body, out_shape=shapes if many else shapes[0], in_specs=[s...  10.1 us
    ppermute x1, starting transfers between devices, local(): fpack = lax.ppermute(pack, TILE, across)  4.58 us
    all_gather x1, blocking collectives, local(): both = lax.all_gather(buf, 'core')  3.38 us
    ppermute x1, starting transfers between devices, local(): beyond = lax.ppermute(call(other_body, (size, pts))(near), TILE, across)  1.92 us
  transfers between devices with their start and end apart: 2, of which 1 were waited for; matrix products, arithmetic and copies ran while one was open for 0% of the time, Pallas kernels for 3%

profile of v9, /device:TPU:1, one launch (start us, length us, event | category | flops | bytes accessed | tf_op | source)
XLA Modules:
  0.0 76.0 jit_solution(7647487527189660029)
XLA Ops:
  0.0 1.2 %shard_map.46 = (f32[640,128]{1,0:T(8,128)S(1)}, f32[760,128]{1,0:T(8,128)S(1)}) custom-call(f32[10,64,128]{2,1,0:T(8,128)} %bitcast.10, f32[10,10,1,128]{3,2,1,0:T(1,128)} %b_hbm.1, f32[2,10,1,128]{3,2,1,0:T(1,128)} %w_hbm.1, f32[10]{0:T(128)} %c_hbm.1), custom_call_target="tpu_custom_call" | custom-call | flops 1638400 | bytes 1105960 | tf_op jit(solution)/shard_map/pallas_call | solution.py:41
  1.2 4.6 %collective-permute-start = (f32[760,128]{1,0:T(8,128)S(1)}, f32[760,128]{1,0:T(8,128)S(1)}, u32[]{:S(2)}, u32[]{:S(2)}) collective-permute-start(f32[760,128]{1,0:T(8,128)S(1)} %get-tuple-element.26.pack_ref), channel_id=1, source_target_pairs={{0,127},{1,2},{2,1},{3,4},{4,3},{5,6},{6,5},{7,8},{8,7},{9,10},{10... | collective-permute-start | bytes 1167368 | tf_op jit(solution)/shard_map/ppermute | solution.py:492
  5.8 12.1 %all-gather = f32[1280,128]{1,0:T(8,128)S(1)} all-gather(f32[640,128]{1,0:T(8,128)S(1)} %get-tuple-element.24.start_ref), channel_id=2, replica_groups=mesh['line'=4,'z'=8,'y'=8,'core'=2] {'core'}, dimensions={0}, use_global_device_ids=true | all-gather | bytes 983040 | tf_op jit(solution)/shard_map/all_gather | solution.py:493
  18.0 1.9 %collective-permute-start.1 = (f32[640,128]{1,0:T(8,128)S(1)}, f32[640,128]{1,0:T(8,128)S(1)}, u32[]{:S(2)}, u32[]{:S(2)}) collective-permute-start(f32[640,128]{1,0:T(8,128)S(1)} %shard_map.47), channel_id=1, source_target_pairs={{0,127},{1,2},{2,1},{3,4},{4,3},{5,6},{6,5},{7,8},{8,7},{9,10},{10... | collective-permute-start | bytes 983048 | tf_op jit(solution)/shard_map/ppermute | solution.py:495
  19.9 0.6 shard_map.48
  20.5 0.0 collective-permute-done.far_ref.pack_ref
  20.5 1.2 %shard_map.49 = (f32[680,128]{1,0:T(8,128)S(1)}, f32[7,16,128]{2,1,0:T(8,128)S(1)}, f32[24,128]{1,0:T(8,128)S(1)}) custom-call(f32[760,128]{1,0:T(8,128)S(1)} %get-tuple-element.26.pack_ref, f32[760,128]{1,0:T(8,128)S(1)} %collective-permute-done.far_ref.pack_ref, f32[2,640,128]{2,1,0:T(8,128)S(1)} %bitcast.9, f32[7,16,128]{2,1,0:T(8,128)S(1)} %get-tuple-element.27.up_ref, ...), custom_call_target="tpu_custom_call" | custom-call | flops 3276800 | bytes 1921024 | tf_op jit(solution)/shard_map/pallas_call | solution.py:41
  21.8 3.4 %all-gather.1 = f32[1360,128]{1,0:T(8,128)S(1)} all-gather(f32[680,128]{1,0:T(8,128)S(1)} %get-tuple-element.31.buf_ref), channel_id=3, replica_groups=mesh['line'=4,'z'=8,'y'=8,'core'=2] {'core'}, dimensions={0}, use_global_device_ids=true | all-gather | bytes 1044480 | tf_op jit(solution)/shard_map/all_gather | solution.py:502
  25.2 1.5 %collective-permute-done.1.next_ref = f32[640,128]{1,0:T(8,128)S(1)} collective-permute-done((f32[640,128]{1,0:T(8,128)S(1)}, f32[640,128]{1,0:T(8,128)S(1)}, u32[]{:S(2)}, u32[]{:S(2)}) %collective-permute-start.1) | collective-permute-done | bytes 327712 | tf_op jit(solution)/shard_map/ppermute | solution.py:495
  26.7 1.2 %shard_map.50 = (f32[640,128]{1,0:T(8,128)S(1)}, f32[4,56,128]{2,1,0:T(8,128)S(1)}) custom-call(f32[760,128]{1,0:T(8,128)S(1)} %collective-permute-done.far_ref.pack_ref, f32[640,128]{1,0:T(8,128)S(1)} %get-tuple-element.24.start_ref, f32[640,128]{1,0:T(8,128)S(1)} %collective-permute-done.1.next_ref, f32[7,16,128]{2,1,0:T(8,128)S(1)} %get-tuple-element.29.up_ref, ...), custom_call_target="tpu_custom_call" | custom-call | flops 3276800 | bytes 2600960 | tf_op jit(solution)/shard_map/pallas_call | solution.py:41
  27.8 8.6 %all_to_all.20.r_ref = f32[4,56,128]{2,1,0:T(8,128)S(1)} all-to-all(f32[4,56,128]{2,1,0:T(8,128)S(1)} %get-tuple-element.32), channel_id=1, replica_groups=mesh['line'=4,'z'=8,'y'=8,'core'=2] {'line'}, dimensions={0} | all-to-all | bytes 229376 | tf_op jit(solution)/shard_map/all_to_all | solution.py:465
  36.4 2.2 %shard_map.51 = (f32[10,64,128]{2,1,0:T(8,128)S(1)}, f32[4,40,128]{2,1,0:T(8,128)S(1)}) custom-call(f32[760,128]{1,0:T(8,128)S(1)} %get-tuple-element.26.pack_ref, f32[4,56,128]{2,1,0:T(8,128)S(1)} %all_to_all.20.r_ref, f32[680,128]{1,0:T(8,128)S(1)} %get-tuple-element.31.buf_ref, f32[2,680,128]{2,1,0:T(8,128)S(1)} %bitcast.7, ...), custom_call_target="tpu_custom_call" | custom-call | flops 6553600 | bytes 2519040 | tf_op jit(solution)/shard_map/pallas_call | solution.py:41
  38.6 6.9 %all_to_all.21.r_ref = f32[4,40,128]{2,1,0:T(8,128)S(1)} all-to-all(f32[4,40,128]{2,1,0:T(8,128)S(1)} %get-tuple-element.36), channel_id=1, replica_groups=mesh['line'=4,'z'=8,'y'=8,'core'=2] {'line'}, dimensions={0} | all-to-all | bytes 163840 | tf_op jit(solution)/shard_map/all_to_all | solution.py:465
  45.5 0.5 shard_map.52
  46.1 16.4 %all_to_all.22.r_ref = f32[16,9,1,128]{3,2,1,0:T(1,128)S(1)} all-to-all(f32[16,9,1,128]{3,2,1,0:T(1,128)S(1)} %get-tuple-element.37), channel_id=1, replica_groups=mesh['line'=4,'z'=8,'y'=8,'core'=2] {'y','core'}, dimensions={0} | all-to-all | bytes 147456 | tf_op jit(solution)/shard_map/all_to_all | solution.py:465
  62.4 0.1 shard_map.53
  62.5 10.5 %all_to_all.23.refs_0_ = f32[16,9,1,128]{3,2,1,0:T(1,128)S(1)} all-to-all(f32[16,9,1,128]{3,2,1,0:T(1,128)S(1)} %shard_map.53), channel_id=1, replica_groups=mesh['line'=4,'z'=8,'y'=8,'core'=2] {'z','core'}, dimensions={0} | all-to-all | bytes 147456 | tf_op jit(solution)/shard_map/all_to_all | solution.py:465
  73.0 3.0 %shard_map.54 = f32[10,64,128]{2,1,0:T(8,128)} custom-call(f32[16,9,1,128]{3,2,1,0:T(1,128)S(1)} %all_to_all.23.refs_0_, f32[10,64,128]{2,1,0:T(8,128)S(1)} %get-tuple-element.38.refs_1_, f32[16,128]{1,0:T(8,128)S(1)} %get-tuple-element.39.refs_2_, f32[16,128]{1,0:T(8,128)S(1)} %get-tuple-element.40.refs_3_), custom_call_target="tpu_custom_call" | custom-call | flops 6553600 | bytes 745472 | tf_op jit(solution)/shard_map/pallas_call | solution.py:41
  (1 shorter events, 0.0 us)
Async XLA Ops:
  1.2 19.3 %collective-permute-start = (f32[760,128]{1,0:T(8,128)S(1)}, f32[760,128]{1,0:T(8,128)S(1)}, u32[]{:S(2)}, u32[]{:S(2)}) collective-permute-start(f32[760,128]{1,0:T(8,128)S(1)} %get-tuple-element.26.pack_ref), channel_id=1, source_target_pairs={{0,127},{1,2},{2,1},{3,4},{4,3},{5,6},{6,5},{7,8},{8,7},{9,10},{10... | collective-permute-start | bytes 1167368 | tf_op jit(solution)/shard_map/ppermute | solution.py:492
  18.0 8.7 %collective-permute-start.1 = (f32[640,128]{1,0:T(8,128)S(1)}, f32[640,128]{1,0:T(8,128)S(1)}, u32[]{:S(2)}, u32[]{:S(2)}) collective-permute-start(f32[640,128]{1,0:T(8,128)S(1)} %shard_map.47), channel_id=1, source_target_pairs={{0,127},{1,2},{2,1},{3,4},{4,3},{5,6},{6,5},{7,8},{8,7},{9,10},{10... | collective-permute-start | bytes 983048 | tf_op jit(solution)/shard_map/ppermute | solution.py:495

commit v10 on v8

--- a/solution.py
+++ b/solution.py
@@ -403,7 +403,7 @@
     spread_rows(o_ref, summed_rows(r_ref, 0, 1))
 
 
-def inverse_factor(scale, gram, v_ref):
+def inverse_factor(scale, gram, v_ref, after):
     cols = gram.shape[0]
     count = cols // 8
     lane, row = lane_ids(8), row_ids(8)
@@ -437,7 +437,7 @@
         for x, t in enumerate(later):
             for i in range(8):
                 tiles[t] = tiles[t] - c[i][x] * scaled[i]
-    return pltpu.roll(v_ref[...], 64, 1)[:, 0:64]
+        after(p)
 
 
 def basis_body(scale, r_ref, loc_ref, suf_ref, entry_ref, out_ref, f_ref, v_ref):
@@ -450,10 +450,16 @@
             f_ref[rows, k * LANES : (k + 1) * LANES] = v
     upper, joined = (summed_rows(r_ref, core, NCORE) for core in range(NCORE))
     gram = unpacked(jnp.concatenate(upper[:8], axis=0), jnp.concatenate(joined[:8], axis=0), joined[8])
-    inv = inverse_factor(scale, gram, v_ref)
-    out = jnp.dot(inv, f_ref[...], precision=HIGH, preferred_element_type=F32)
-    for k in range(n):
-        out_ref[k] = out[:, k * LANES : (k + 1) * LANES]
+    half = cols // 2
+
+    def product(low, depth):
+        inv = pltpu.roll(v_ref[low : low + half, :], 64, 1)[:, 0:depth]
+        out = jnp.dot(inv, f_ref[0:depth, :], precision=HIGH, preferred_element_type=F32)
+        for k in range(n):
+            out_ref[k, low : low + half, :] = out[:, k * LANES : (k + 1) * LANES]
+
+    inverse_factor(scale, gram, v_ref, lambda p: product(0, half) if p == half // 8 - 1 else None)
+    product(half, cols)
 
 
 def in_hbm(value):

time: 76.2 us -> 76.1 us (level)
  no operation moved by 1% of the time
where the time goes in v10:
time: 76.1 us; the launch traced here: 75.8 us
  blocking collectives  57.8 us (76%)
  Pallas kernels  9.94 us (13%)
  starting transfers between devices  6.5 us (9%)
  waiting for transfers between devices  1.47 us (2%)
    all_to_all x4, blocking collectives, exchange(): return lax.all_to_all(value, axis, 0, 0, tiled=True)  42.3 us
    all_gather x1, blocking collectives, local(): near = lax.all_gather(start, 'core')  12.1 us
    pallas_call x9, Pallas kernels, run(): pl.pallas_call(body, out_shape=shapes if many else shapes[0], in_specs=[s...  9.94 us
    ppermute x1, starting transfers between devices, local(): fpack = lax.ppermute(pack, TILE, across)  4.58 us
    all_gather x1, blocking collectives, local(): both = lax.all_gather(buf, 'core')  3.38 us
    ppermute x1, starting transfers between devices, local(): beyond = lax.ppermute(call(other_body, (size, pts))(near), TILE, across)  1.92 us
  transfers between devices with their start and end apart: 2, of which 1 were waited for; matrix products, arithmetic and copies ran while one was open for 0% of the time, Pallas kernels for 3%

profile of v10, /device:TPU:1, one launch (start us, length us, event | category | flops | bytes accessed | tf_op | source)
XLA Modules:
  0.0 75.8 jit_solution(14837773858849001411)
XLA Ops:
  0.0 1.2 %shard_map.46 = (f32[640,128]{1,0:T(8,128)S(1)}, f32[760,128]{1,0:T(8,128)S(1)}) custom-call(f32[10,64,128]{2,1,0:T(8,128)} %bitcast.10, f32[10,10,1,128]{3,2,1,0:T(1,128)} %b_hbm.1, f32[2,10,1,128]{3,2,1,0:T(1,128)} %w_hbm.1, f32[10]{0:T(128)} %c_hbm.1), custom_call_target="tpu_custom_call" | custom-call | flops 1638400 | bytes 1105960 | tf_op jit(solution)/shard_map/pallas_call | solution.py:41
  1.2 4.6 %collective-permute-start = (f32[760,128]{1,0:T(8,128)S(1)}, f32[760,128]{1,0:T(8,128)S(1)}, u32[]{:S(2)}, u32[]{:S(2)}) collective-permute-start(f32[760,128]{1,0:T(8,128)S(1)} %get-tuple-element.26.pack_ref), channel_id=1, source_target_pairs={{0,127},{1,2},{2,1},{3,4},{4,3},{5,6},{6,5},{7,8},{8,7},{9,10},{10... | collective-permute-start | bytes 1167368 | tf_op jit(solution)/shard_map/ppermute | solution.py:497
  5.8 12.1 %all-gather = f32[1280,128]{1,0:T(8,128)S(1)} all-gather(f32[640,128]{1,0:T(8,128)S(1)} %get-tuple-element.24.start_ref), channel_id=2, replica_groups=mesh['line'=4,'z'=8,'y'=8,'core'=2] {'core'}, dimensions={0}, use_global_device_ids=true | all-gather | bytes 983040 | tf_op jit(solution)/shard_map/all_gather | solution.py:498
  18.0 1.9 %collective-permute-start.1 = (f32[640,128]{1,0:T(8,128)S(1)}, f32[640,128]{1,0:T(8,128)S(1)}, u32[]{:S(2)}, u32[]{:S(2)}) collective-permute-start(f32[640,128]{1,0:T(8,128)S(1)} %shard_map.47), channel_id=1, source_target_pairs={{0,127},{1,2},{2,1},{3,4},{4,3},{5,6},{6,5},{7,8},{8,7},{9,10},{10... | collective-permute-start | bytes 983048 | tf_op jit(solution)/shard_map/ppermute | solution.py:500
  19.9 0.6 shard_map.48
  20.5 0.0 collective-permute-done.far_ref.pack_ref
  20.5 1.3 %shard_map.49 = (f32[680,128]{1,0:T(8,128)S(1)}, f32[7,16,128]{2,1,0:T(8,128)S(1)}, f32[24,128]{1,0:T(8,128)S(1)}) custom-call(f32[760,128]{1,0:T(8,128)S(1)} %get-tuple-element.26.pack_ref, f32[760,128]{1,0:T(8,128)S(1)} %collective-permute-done.far_ref.pack_ref, f32[2,640,128]{2,1,0:T(8,128)S(1)} %bitcast.9, f32[7,16,128]{2,1,0:T(8,128)S(1)} %get-tuple-element.27.up_ref, ...), custom_call_target="tpu_custom_call" | custom-call | flops 3276800 | bytes 1921024 | tf_op jit(solution)/shard_map/pallas_call | solution.py:41
  21.8 3.4 %all-gather.1 = f32[1360,128]{1,0:T(8,128)S(1)} all-gather(f32[680,128]{1,0:T(8,128)S(1)} %get-tuple-element.31.buf_ref), channel_id=3, replica_groups=mesh['line'=4,'z'=8,'y'=8,'core'=2] {'core'}, dimensions={0}, use_global_device_ids=true | all-gather | bytes 1044480 | tf_op jit(solution)/shard_map/all_gather | solution.py:507
  25.2 1.5 %collective-permute-done.1.next_ref = f32[640,128]{1,0:T(8,128)S(1)} collective-permute-done((f32[640,128]{1,0:T(8,128)S(1)}, f32[640,128]{1,0:T(8,128)S(1)}, u32[]{:S(2)}, u32[]{:S(2)}) %collective-permute-start.1) | collective-permute-done | bytes 327712 | tf_op jit(solution)/shard_map/ppermute | solution.py:500
  26.7 1.2 %shard_map.50 = (f32[640,128]{1,0:T(8,128)S(1)}, f32[4,56,128]{2,1,0:T(8,128)S(1)}) custom-call(f32[760,128]{1,0:T(8,128)S(1)} %collective-permute-done.far_ref.pack_ref, f32[640,128]{1,0:T(8,128)S(1)} %get-tuple-element.24.start_ref, f32[640,128]{1,0:T(8,128)S(1)} %collective-permute-done.1.next_ref, f32[7,16,128]{2,1,0:T(8,128)S(1)} %get-tuple-element.29.up_ref, ...), custom_call_target="tpu_custom_call" | custom-call | flops 3276800 | bytes 2600960 | tf_op jit(solution)/shard_map/pallas_call | solution.py:41
  27.8 8.5 %all_to_all.20.r_ref = f32[4,56,128]{2,1,0:T(8,128)S(1)} all-to-all(f32[4,56,128]{2,1,0:T(8,128)S(1)} %get-tuple-element.32), channel_id=1, replica_groups=mesh['line'=4,'z'=8,'y'=8,'core'=2] {'line'}, dimensions={0} | all-to-all | bytes 229376 | tf_op jit(solution)/shard_map/all_to_all | solution.py:470
  36.4 2.1 %shard_map.51 = (f32[10,64,128]{2,1,0:T(8,128)S(1)}, f32[4,40,128]{2,1,0:T(8,128)S(1)}) custom-call(f32[760,128]{1,0:T(8,128)S(1)} %get-tuple-element.26.pack_ref, f32[4,56,128]{2,1,0:T(8,128)S(1)} %all_to_all.20.r_ref, f32[680,128]{1,0:T(8,128)S(1)} %get-tuple-element.31.buf_ref, f32[2,680,128]{2,1,0:T(8,128)S(1)} %bitcast.7, ...), custom_call_target="tpu_custom_call" | custom-call | flops 6553600 | bytes 2519040 | tf_op jit(solution)/shard_map/pallas_call | solution.py:41
  38.5 6.9 %all_to_all.21.r_ref = f32[4,40,128]{2,1,0:T(8,128)S(1)} all-to-all(f32[4,40,128]{2,1,0:T(8,128)S(1)} %get-tuple-element.36), channel_id=1, replica_groups=mesh['line'=4,'z'=8,'y'=8,'core'=2] {'line'}, dimensions={0} | all-to-all | bytes 163840 | tf_op jit(solution)/shard_map/all_to_all | solution.py:470
  45.5 0.5 shard_map.52
  46.0 16.4 %all_to_all.22.r_ref = f32[16,9,1,128]{3,2,1,0:T(1,128)S(1)} all-to-all(f32[16,9,1,128]{3,2,1,0:T(1,128)S(1)} %get-tuple-element.37), channel_id=1, replica_groups=mesh['line'=4,'z'=8,'y'=8,'core'=2] {'y','core'}, dimensions={0} | all-to-all | bytes 147456 | tf_op jit(solution)/shard_map/all_to_all | solution.py:470
  62.4 0.1 shard_map.53
  62.4 10.5 %all_to_all.23.refs_0_ = f32[16,9,1,128]{3,2,1,0:T(1,128)S(1)} all-to-all(f32[16,9,1,128]{3,2,1,0:T(1,128)S(1)} %shard_map.53), channel_id=1, replica_groups=mesh['line'=4,'z'=8,'y'=8,'core'=2] {'z','core'}, dimensions={0} | all-to-all | bytes 147456 | tf_op jit(solution)/shard_map/all_to_all | solution.py:470
  72.9 2.9 %shard_map.54 = f32[10,64,128]{2,1,0:T(8,128)} custom-call(f32[16,9,1,128]{3,2,1,0:T(1,128)S(1)} %all_to_all.23.refs_0_, f32[10,64,128]{2,1,0:T(8,128)S(1)} %get-tuple-element.38.refs_1_, f32[16,128]{1,0:T(8,128)S(1)} %get-tuple-element.39.refs_2_, f32[16,128]{1,0:T(8,128)S(1)} %get-tuple-element.40.refs_3_), custom_call_target="tpu_custom_call" | custom-call | flops 6553600 | bytes 745472 | tf_op jit(solution)/shard_map/pallas_call | solution.py:41
  (1 shorter events, 0.0 us)
Async XLA Ops:
  1.2 19.3 %collective-permute-start = (f32[760,128]{1,0:T(8,128)S(1)}, f32[760,128]{1,0:T(8,128)S(1)}, u32[]{:S(2)}, u32[]{:S(2)}) collective-permute-start(f32[760,128]{1,0:T(8,128)S(1)} %get-tuple-element.26.pack_ref), channel_id=1, source_target_pairs={{0,127},{1,2},{2,1},{3,4},{4,3},{5,6},{6,5},{7,8},{8,7},{9,10},{10... | collective-permute-start | bytes 1167368 | tf_op jit(solution)/shard_map/ppermute | solution.py:497
  18.0 8.7 %collective-permute-start.1 = (f32[640,128]{1,0:T(8,128)S(1)}, f32[640,128]{1,0:T(8,128)S(1)}, u32[]{:S(2)}, u32[]{:S(2)}) collective-permute-start(f32[640,128]{1,0:T(8,128)S(1)} %shard_map.47), channel_id=1, source_target_pairs={{0,127},{1,2},{2,1},{3,4},{4,3},{5,6},{6,5},{7,8},{8,7},{9,10},{10... | collective-permute-start | bytes 983048 | tf_op jit(solution)/shard_map/ppermute | solution.py:500
